TPU v7x, 32 devices: a whole 2x2x4 slice. The times are simulated.
32 devices in a mesh: dp: 2 (over x), ctx: 4 (over z), tp: 4 (over y, core).
Axes of the slice: x: 2, y: 2, z: 4, core: 2. Of those that a mesh axis runs over, the one named last changes fastest.
Arguments:
- hidden_in: bfloat16 [2, 2, 2048, 768], P(None, 'dp', 'ctx'), may hold values from -6 to 6
- prefix: int32 [2, 2], P(None, 'dp'), may hold values from 204 to 1024
- block_order: int32 [8], replicated, may hold values from 0 to 7, each once
- qkv_weight: bfloat16 [3, 768, 768], P(None, 'dp', 'tp'), may hold values from -0.3125 to 0.3125
- out_weight: bfloat16 [768, 768], P('tp', 'dp'), may hold values from -2.5 to 2.5
- up_weight: bfloat16 [768, 3072], P('dp', 'tp'), may hold values from -0.21875 to 0.21875
- down_weight: bfloat16 [3072, 768], P('tp', 'dp'), may hold values from -0.4375 to 0.4375
- ln_gains: bfloat16 [2, 768], P(None, 'dp'), may hold values from 0.5 to 1.5
- ln_shifts: bfloat16 [2, 768], P(None, 'dp'), may hold values from -2 to 2
- cotangent: bfloat16 [2, 2, 2048, 768], P(None, 'dp', 'ctx'), may hold values from -6 to 6
Outputs:
- block_out: bfloat16 [2, 2, 2048, 768], P(None, 'dp', 'ctx')
- grad_in: float32 [2, 2, 2048, 768], P(None, 'dp', 'ctx')
- grad_qkv: float32 [3, 768, 768], P(None, 'dp', 'tp')
- grad_out: float32 [768, 768], P('tp', 'dp')
- grad_up: float32 [768, 3072], P('dp', 'tp')
- grad_down: float32 [3072, 768], P('tp', 'dp')
- grad_gains: float32 [2, 768], P(None, 'dp')
- grad_shifts: float32 [2, 768], P(None, 'dp')
Inputs may be any that keep to these rules, and one draw needn't show every extreme that they name: `prefix`: leading positions of each sequence that all of its queries see. `block_order`: each of the 2 * 4 block numbers appears once.
All inputs are finite; a program needn't handle non-finite values.
Results may differ from a plain program's by a relative error of at most 0.012.
The roundings to bfloat16 on the way count: a program that leaves them out, or rounds other values in their place, can miss the bound.
Values may be sent and summed in bfloat16 or wider, within the bound.
A program may use at most 128 MiB of HBM per device.

v0:
```python
import jax
import jax.numpy as jnp
from jax import lax
from jax.sharding import PartitionSpec as P

HEAD_DIM = 64
DEPTH = 12


EPS = 1e-05
GELU_C = 0.7978845608028654
GELU_A = 0.044715
NEG = -1e30
ROW_BLOCK = 512


def apply_layer_norm(values, norm_gain, norm_shift):
    row_mean = jnp.mean(values, axis=1, keepdims=True)
    centered_input = values - row_mean
    inverse_deviation = lax.rsqrt(
        jnp.mean(centered_input * centered_input, axis=1, keepdims=True) + EPS
    )
    normalized_input = centered_input * inverse_deviation
    return (normalized_input * norm_gain + norm_shift, normalized_input, inverse_deviation)


def norm_backward(normed_gradient, normalized_input, inverse_deviation, norm_gain):
    scaled_gradient = normed_gradient * norm_gain
    return inverse_deviation * (
        scaled_gradient
        - jnp.mean(scaled_gradient, axis=1, keepdims=True)
        - normalized_input * jnp.mean(scaled_gradient * normalized_input, axis=1, keepdims=True)
    )


def gelu_value(u):
    return 0.5 * u * (1.0 + jnp.tanh(GELU_C * (u + GELU_A * u * u * u)))


def gelu_slope(u):
    inner = jnp.tanh(GELU_C * (u + GELU_A * u * u * u))
    return 0.5 * (1.0 + inner) + 0.5 * u * (1.0 - inner * inner) * GELU_C * (
        1.0 + 3.0 * GELU_A * u * u
    )


def block_positions(block_order, rows, half):
    slots = jnp.arange(block_order.shape[0], dtype=jnp.int32)
    picked = jnp.where((rows // half)[:, None] == slots[None, :], block_order[None, :], 0)
    return jnp.sum(picked, axis=1) * half + rows % half


def fetch_weights(qkv_weight, out_weight, up_weight, down_weight, ln_gains, ln_shifts):
    return (
        lax.all_gather(qkv_weight, "dp", axis=1, tiled=True),
        lax.all_gather(out_weight, "dp", axis=1, tiled=True),
        lax.all_gather(up_weight, "dp", axis=0, tiled=True),
        lax.all_gather(down_weight, "dp", axis=1, tiled=True),
        lax.all_gather(ln_gains, "dp", axis=1, tiled=True),
        lax.all_gather(ln_shifts, "dp", axis=1, tiled=True),
    )


def body(
    hidden_in,
    prefix,
    block_order,
    qkv_weight,
    out_weight,
    up_weight,
    down_weight,
    ln_gains,
    ln_shifts,
    cotangent,
):
    micro = hidden_in.shape[0]
    tokens = hidden_in.shape[2]
    width = hidden_in.shape[3]
    local_width = qkv_weight.shape[2]
    head_dim = HEAD_DIM
    local_heads = local_width // head_dim
    seq_len = tokens * lax.axis_size("ctx")
    half = tokens // 2
    branch = DEPTH ** (-0.5)
    scale = head_dim ** (-0.5)
    block_rows = min(tokens, ROW_BLOCK)
    blocks = tokens // block_rows
    query_rows = lax.axis_index("ctx") * tokens + jnp.arange(tokens, dtype=jnp.int32)
    key_rows = jnp.arange(seq_len, dtype=jnp.int32)
    query_pos = block_positions(block_order, query_rows, half)
    key_pos = block_positions(block_order, key_rows, half)
    acc_qkv = jnp.zeros((3, width, local_width), jnp.float32)
    acc_out = jnp.zeros((local_width, width), jnp.float32)
    acc_up = jnp.zeros((width, up_weight.shape[1]), jnp.float32)
    acc_down = jnp.zeros((down_weight.shape[0], width), jnp.float32)
    acc_gains = jnp.zeros((2, width), jnp.float32)
    acc_shifts = jnp.zeros((2, width), jnp.float32)
    results = []
    input_gradient_list = []
    for index in range(micro):
        full = fetch_weights(qkv_weight, out_weight, up_weight, down_weight, ln_gains, ln_shifts)
        qkv_full, out_full, up_full, down_full, gains_full, shifts_full = full
        norm_gains = gains_full.astype(jnp.float32)
        norm_shifts = shifts_full.astype(jnp.float32)
        input_rows = hidden_in[index, 0].astype(jnp.float32)
        allowed = (key_pos[None, :] <= query_pos[:, None]) | (key_pos[None, :] < prefix[index, 0])
        first_normed, normalized_first1, inverse_deviation1 = apply_layer_norm(
            input_rows, norm_gains[0], norm_shifts[0]
        )
        h1 = first_normed.astype(jnp.bfloat16)
        qkv = jnp.einsum("td,kde->kte", h1, qkv_full, preferred_element_type=jnp.float32).astype(
            jnp.bfloat16
        )
        keys_flat, values_flat = (
            lax.all_gather(qkv[1], "ctx", axis=0, tiled=True),
            lax.all_gather(qkv[2], "ctx", axis=0, tiled=True),
        )
        keys = keys_flat.reshape(seq_len, local_heads, head_dim)
        values = values_flat.reshape(seq_len, local_heads, head_dim)
        q_blocks = qkv[0].reshape(blocks, block_rows, local_heads, head_dim)
        a_blocks = allowed.reshape(blocks, block_rows, seq_len)

        def attend(item):
            q_blk, allow_blk = item
            scores = (
                jnp.einsum("qhd,khd->hqk", q_blk, keys, preferred_element_type=jnp.float32) * scale
            )
            scores = jnp.where(allow_blk[None], scores, NEG)
            top = jnp.max(scores, axis=2, keepdims=True)
            expd = jnp.exp(scores - top)
            total = jnp.sum(expd, axis=2, keepdims=True)
            prob = (expd / total).astype(jnp.bfloat16)
            mixed = jnp.einsum("hqk,khd->qhd", prob, values, preferred_element_type=jnp.float32)
            return (mixed.astype(jnp.bfloat16), (top + jnp.log(total))[:, :, 0])

        heads_out, logsum = lax.map(attend, (q_blocks, a_blocks))
        heads = heads_out.reshape(tokens, local_width)
        attn_part = jnp.dot(heads, out_full, preferred_element_type=jnp.float32)
        attn = lax.psum(attn_part, "tp")
        middle_state = input_rows + branch * attn
        second_normed, normalized_second2, inverse_deviation2 = apply_layer_norm(
            middle_state, norm_gains[1], norm_shifts[1]
        )
        h2 = second_normed.astype(jnp.bfloat16)
        up = jnp.dot(h2, up_full, preferred_element_type=jnp.float32)
        act = gelu_value(up).astype(jnp.bfloat16)
        mlp_part = jnp.dot(act, down_full, preferred_element_type=jnp.float32)
        mlp = lax.psum(mlp_part, "tp")
        results.append((middle_state + branch * mlp).astype(jnp.bfloat16))
        qkv_full, out_full, up_full, down_full, gains_full, shifts_full = fetch_weights(
            qkv_weight, out_weight, up_weight, down_weight, ln_gains, ln_shifts
        )
        upstream_gradient = cotangent[index, 0].astype(jnp.float32)
        d_mlp = (branch * upstream_gradient).astype(jnp.bfloat16)
        grad_down = jnp.einsum("tf,td->fd", act, d_mlp, preferred_element_type=jnp.float32)
        d_act = jnp.einsum("td,fd->tf", d_mlp, down_full, preferred_element_type=jnp.float32)
        d_up = (d_act * gelu_slope(up)).astype(jnp.bfloat16)
        grad_up = jnp.einsum("td,tf->df", h2, d_up, preferred_element_type=jnp.float32)
        n2_back = jnp.einsum("tf,df->td", d_up, up_full, preferred_element_type=jnp.float32)
        second_norm_gradient = lax.psum(n2_back, "tp")
        middle_gradient = upstream_gradient + norm_backward(
            second_norm_gradient, normalized_second2, inverse_deviation2, norm_gains[1]
        )
        d_attn = (branch * middle_gradient).astype(jnp.bfloat16)
        grad_out = jnp.einsum("te,td->ed", heads, d_attn, preferred_element_type=jnp.float32)
        d_heads = jnp.einsum(
            "td,ed->te", d_attn, out_full, preferred_element_type=jnp.float32
        ).astype(jnp.bfloat16)
        dh_blocks = d_heads.reshape(blocks, block_rows, local_heads, head_dim)

        def attend_back(carry, item):
            key_sum, value_sum = carry
            q_blk, allow_blk, lse_blk, dh_blk = item
            scores = (
                jnp.einsum("qhd,khd->hqk", q_blk, keys, preferred_element_type=jnp.float32) * scale
            )
            scores = jnp.where(allow_blk[None], scores, NEG)
            prob = jnp.exp(scores - lse_blk[:, :, None])
            prob_low = prob.astype(jnp.bfloat16)
            d_prob = jnp.einsum("qhd,khd->hqk", dh_blk, values, preferred_element_type=jnp.float32)
            d_scores = (prob * (d_prob - jnp.sum(prob * d_prob, axis=2, keepdims=True))).astype(
                jnp.bfloat16
            )
            d_query = (
                jnp.einsum("hqk,khd->qhd", d_scores, keys, preferred_element_type=jnp.float32)
                * scale
            ).astype(jnp.bfloat16)
            key_sum = (
                key_sum
                + jnp.einsum("hqk,qhd->khd", d_scores, q_blk, preferred_element_type=jnp.float32)
                * scale
            )
            value_sum = value_sum + jnp.einsum(
                "hqk,qhd->khd", prob_low, dh_blk, preferred_element_type=jnp.float32
            )
            return ((key_sum, value_sum), d_query)

        zero_kv = jnp.zeros((seq_len, local_heads, head_dim), jnp.float32)
        (key_sum, value_sum), d_query = lax.scan(
            attend_back, (zero_kv, zero_kv), (q_blocks, a_blocks, logsum, dh_blocks)
        )
        d_keys, d_values = (
            lax.psum_scatter(
                key_sum.reshape(seq_len, local_width), "ctx", scatter_dimension=0, tiled=True
            ),
            lax.psum_scatter(
                value_sum.reshape(seq_len, local_width), "ctx", scatter_dimension=0, tiled=True
            ),
        )
        d_qkv = jnp.stack(
            [
                d_query.reshape(tokens, local_width),
                d_keys.astype(jnp.bfloat16),
                d_values.astype(jnp.bfloat16),
            ]
        )
        grad_qkv = jnp.einsum("td,kte->kde", h1, d_qkv, preferred_element_type=jnp.float32)
        n1_back = jnp.einsum("kte,kde->td", d_qkv, qkv_full, preferred_element_type=jnp.float32)
        first_norm_gradient = lax.psum(n1_back, "tp")
        input_gradient_list.append(
            middle_gradient
            + norm_backward(
                first_norm_gradient, normalized_first1, inverse_deviation1, norm_gains[0]
            )
        )
        acc_gains = acc_gains + jnp.stack(
            [
                jnp.sum(first_norm_gradient * normalized_first1, axis=0),
                jnp.sum(second_norm_gradient * normalized_second2, axis=0),
            ]
        )
        acc_shifts = acc_shifts + jnp.stack(
            [jnp.sum(first_norm_gradient, axis=0), jnp.sum(second_norm_gradient, axis=0)]
        )
        acc_qkv = acc_qkv + grad_qkv
        acc_out = acc_out + grad_out
        acc_up = acc_up + grad_up
        acc_down = acc_down + grad_down
    whole_qkv, whole_out, whole_up, whole_down, whole_gains, whole_shifts = lax.psum(
        (acc_qkv, acc_out, acc_up, acc_down, acc_gains, acc_shifts), "ctx"
    )
    owned = (
        lax.psum_scatter(whole_qkv, "dp", scatter_dimension=1, tiled=True),
        lax.psum_scatter(whole_out, "dp", scatter_dimension=1, tiled=True),
        lax.psum_scatter(whole_up, "dp", scatter_dimension=0, tiled=True),
        lax.psum_scatter(whole_down, "dp", scatter_dimension=1, tiled=True),
        lax.psum_scatter(whole_gains, "dp", scatter_dimension=1, tiled=True),
        lax.psum_scatter(whole_shifts, "dp", scatter_dimension=1, tiled=True),
    )
    block_out = jnp.stack(results)[:, None]
    grad_in = jnp.stack(input_gradient_list)[:, None]
    return (block_out, grad_in, owned[0], owned[1], owned[2], owned[3], owned[4], owned[5])


def solution(mesh):
    in_specs = (
        P(None, "dp", "ctx", None),
        P(None, "dp"),
        P(),
        P(None, "dp", "tp"),
        P("tp", "dp"),
        P("dp", "tp"),
        P("tp", "dp"),
        P(None, "dp"),
        P(None, "dp"),
        P(None, "dp", "ctx", None),
    )
    out_specs = (
        P(None, "dp", "ctx", None),
        P(None, "dp", "ctx", None),
        P(None, "dp", "tp"),
        P("tp", "dp"),
        P("dp", "tp"),
        P("tp", "dp"),
        P(None, "dp"),
        P(None, "dp"),
    )
    return jax.shard_map(body, mesh=mesh, in_specs=in_specs, out_specs=out_specs, check_vma=False)
```

profile of v0, /device:TPU:0, one launch (start us, length us, event | category | flops | bytes accessed | tf_op | source)
XLA Modules:
  0.0 766.0 jit_solution(9417610063547408217)
XLA Ops:
  10.2 5.5 all_gather.20
  15.7 4.5 all_gather.21
  22.8 5.9 all_gather.49
  28.7 9.4 %all_gather.22 = bf16[3,768,192]{1,2,0:T(8,128)(2,1)S(1)} all-gather(bf16[3,384,192]{1,2,0:T(8,128)(2,1)S(1)} %copy-done.43), channel_id=1, replica_groups=mesh['dp'=2,'ctx'=4,'tp'=4] {'dp'}, dimensions={1}, use_global_device_ids=true | all-gather | bytes 1327104 | tf_op jit(solution)/shard_map/all_gather | solution.py:55
  39.8 19.5 %all-gather.3 = bf16[1,2048,192]{1,2,0:T(8,128)(2,1)S(1)} all-gather(bf16[1,512,192]{1,2,0:T(8,128)(2,1)S(1)} %get-tuple-element.187), channel_id=5, replica_groups=mesh['dp'=2,'ctx'=4,'tp'=4] {'ctx'}, dimensions={1}, use_global_device_ids=true | all-gather | bytes 983040 | tf_op jit(solution)/shard_map/all_gather | solution.py:115
  59.3 17.9 %all-gather.2 = bf16[1,2048,192]{1,2,0:T(8,128)(2,1)S(1)} all-gather(bf16[1,512,192]{1,2,0:T(8,128)(2,1)S(1)} %get-tuple-element.189), channel_id=4, replica_groups=mesh['dp'=2,'ctx'=4,'tp'=4] {'ctx'}, dimensions={1}, use_global_device_ids=true | all-gather | bytes 983040 | tf_op jit(solution)/shard_map/all_gather | solution.py:116
  78.2 17.1 %all-gather.1 = bf16[1,2048,192]{1,2,0:T(8,128)(2,1)S(1)} all-gather(bf16[1,512,192]{1,2,0:T(8,128)(2,1)S(1)} %get-tuple-element.184), channel_id=3, replica_groups=mesh['dp'=2,'ctx'=4,'tp'=4] {'ctx'}, dimensions={1}, use_global_device_ids=true | all-gather | bytes 983040 | tf_op jit(solution)/shard_map/all_gather | solution.py:115
  95.3 15.7 %all-gather = bf16[1,2048,192]{1,2,0:T(8,128)(2,1)S(1)} all-gather(bf16[1,512,192]{1,2,0:T(8,128)(2,1)S(1)} %get-tuple-element.186), channel_id=2, replica_groups=mesh['dp'=2,'ctx'=4,'tp'=4] {'ctx'}, dimensions={1}, use_global_device_ids=true | all-gather | bytes 983040 | tf_op jit(solution)/shard_map/all_gather | solution.py:116
  121.7 3.3 fusion.65
  139.9 67.9 %all-reduce.14.cloned.1.call-done = (f32[512,768]{1,0:T(8,128)}, f32[512,768]{1,0:T(8,128)}) async-done(((f32[512,768]{1,0:T(8,128)}, f32[512,768]{1,0:T(8,128)}), (f32[512,768]{1,0:T(8,128)}, f32[512,768]{1,0:T(8,128)})) %all-reduce.14.cloned.1.call-update) | async-done | bytes 3145744 | tf_op jit(solution)/shard_map/psum | solution.py:139
  211.5 3.9 fusion.114
  217.5 3.6 fusion.56
  226.7 68.7 %all-reduce.12.cloned.1.call-done = (f32[512,768]{1,0:T(8,128)}, f32[512,768]{1,0:T(8,128)}) async-done(((f32[512,768]{1,0:T(8,128)}, f32[512,768]{1,0:T(8,128)}), (f32[512,768]{1,0:T(8,128)}, f32[512,768]{1,0:T(8,128)})) %all-reduce.12.cloned.1.call-update) | async-done | bytes 3145744 | tf_op jit(solution)/shard_map/psum | solution.py:160
  295.4 3.8 multiply_reduce_fusion.3
  303.3 7.9 %fusion.6 = f32[3,64,2048]{2,1,0:T(8,128)} fusion(bf16[512,3,64]{0,2,1:T(8,128)(2,1)S(1)} %bitcast.237, f32[3,512,2048]{2,1,0:T(8,128)} %copy-done, f32[3,512]{1,0:T(4,128)S(1)} %log_add_fusion.1), kind=kOutput, calls=%fused_computation.17 | convolution fusion | flops 408944640 | bytes 14358528 | tf_op jit(solution)/shard_map/while/body/eval_jaxpr/hqk,qhd->khd/dot_general | solution.py:193
  313.7 8.2 %fusion.4 = f32[3,64,2048]{2,1,0:T(8,128)} fusion(bf16[512,3,64]{0,2,1:T(8,128)(2,1)S(1)} %bitcast.239, f32[3,512,2048]{2,1,0:T(8,128)} %copy-done.1, f32[3,512]{1,0:T(4,128)S(1)} %log_add_fusion), kind=kOutput, calls=%fused_computation.16 | convolution fusion | flops 408944640 | bytes 14358528 | tf_op jit(solution)/shard_map/while/body/eval_jaxpr/hqk,qhd->khd/dot_general | solution.py:193
  322.8 6.6 multiply_reduce_fusion
  329.4 6.5 multiply_convert_fusion
  339.9 6.6 multiply_reduce_fusion.1
  346.5 6.4 multiply_convert_fusion.1
  356.4 4.1 fusion.112
  360.6 3.9 fusion.111
  364.5 5.6 fusion.63
  373.8 10.2 %reduce-scatter.21.cloned.1.call-done = f32[512,192]{0,1:T(8,128)} async-done(((f32[2048,192]{0,1:T(8,128)}), f32[512,192]{0,1:T(8,128)}) %reduce-scatter.21.cloned.1.call-update) | async-done | bytes 393232 | tf_op jit(solution)/shard_map/reduce_scatter | solution.py:206
  385.1 35.6 %reduce-scatter.19.cloned.1.call-done = f32[512,192]{0,1:T(8,128)} async-done(((f32[2048,192]{0,1:T(8,128)}), f32[512,192]{0,1:T(8,128)}) %reduce-scatter.19.cloned.1.call-update) | async-done | bytes 393232 | tf_op jit(solution)/shard_map/reduce_scatter | solution.py:203
  425.6 31.6 %reduce-scatter.15.cloned.1.call-done = f32[512,192]{0,1:T(8,128)} async-done(((f32[2048,192]{0,1:T(8,128)}), f32[512,192]{0,1:T(8,128)}) %reduce-scatter.15.cloned.1.call-update) | async-done | bytes 393232 | tf_op jit(solution)/shard_map/reduce_scatter | solution.py:203
  459.0 3.3 convolution_bitcast_fusion.1
  483.4 97.4 %all-reduce.10.cloned.1.call-done = (f32[512,768]{1,0:T(8,128)}, f32[512,768]{1,0:T(8,128)}, f32[512,768]{1,0:T(8,128)}, f32[512,768]{1,0:T(8,128)}) async-done(((f32[512,768]{1,0:T(8,128)}, f32[512,768]{1,0:T(8,128)}, f32[512,768]{1,0:T(8,128)}, f32[512,768]{1,0:T(8,128)}), (f32[512,768]{1,0:T(8,128)}, f32[512,768]{1,0:T(8,128)}, f32[512,768]{1,0:T(8,128)}, ...) | async-done | bytes 6291472 | tf_op jit(solution)/shard_map/psum | solution.py:148
  595.4 5.8 reduce-scatter.33.cloned.1.call-done
  602.2 15.0 %reduce-scatter.31.cloned.1.call-done = f32[384,2]{1,0:T(8,128)} async-done(((f32[768,2]{1,0:T(8,128)}), f32[384,2]{1,0:T(8,128)}) %reduce-scatter.31.cloned.1.call-update) | async-done | bytes 3088
  618.2 12.6 %all-reduce.3 = (f32[2,384]{1,0:T(2,128)}, f32[2,384]{1,0:T(2,128)}) all-reduce(f32[2,384]{1,0:T(2,128)S(1)} %copy.25, f32[2,384]{1,0:T(2,128)S(1)} %copy.27), channel_id=1, replica_groups=mesh['dp'=2,'ctx'=4,'tp'=4] {'ctx'}, use_global_device_ids=true, to_apply=%region_48.49 | all-reduce | flops 1536 | bytes 12288 | tf_op jit(solution)/shard_map/psum | solution.py:239
  630.8 122.6 %all-reduce.16.cloned.1.call-done = (f32[3,384,192]{1,2,0:T(8,128)}, f32[192,384]{1,0:T(8,128)}, f32[384,768]{1,0:T(8,128)}, f32[768,384]{1,0:T(8,128)}) async-done(((f32[3,384,192]{1,2,0:T(8,128)}, f32[192,384]{1,0:T(8,128)}, f32[384,768]{1,0:T(8,128)}, f32[768,384]{1,0:T(8,128)}), (f32[3,384,192]{1,2,0:T(8,128)}, f32[192,384]{1,0:T(8,128)}, f32[384,768]{1,0:T(8,128)}, ...) | async-done | bytes 3538960 | tf_op jit(solution)/shard_map/psum | solution.py:239
  (305 shorter events, 112.4 us)
Async XLA Ops:
  8.0 199.9 %all-reduce.14.cloned.1.call-start = ((), (), s32[]{:S(2)}) async-start(), calls=%async_computation.24 | async-start | bytes 6291456 | tf_op jit(solution)/shard_map/psum | solution.py:139
  20.2 56.9 %copy-start.73 = (f32[768]{0:T(1024)}, f32[768]{0:T(1024)S(1)}, u32[]{:S(2)}) copy-start(f32[768]{0:T(1024)S(1)} %get-tuple-element.159) | copy-start | bytes 9220
  20.3 195.2 %copy-start.67 = (f32[768]{0:T(1024)}, f32[768]{0:T(1024)S(1)}, u32[]{:S(2)}) copy-start(f32[768]{0:T(1024)S(1)} %get-tuple-element.158) | copy-start | bytes 9220
  22.0 16.1 %copy-start.54 = (f32[512]{0:T(512)}, f32[512]{0:T(512)S(1)}, u32[]{:S(2)}) copy-start(f32[512]{0:T(512)S(1)} %broadcast_multiply_fusion.9) | copy-start | bytes 6148
  22.7 54.5 %copy-start.60 = (f32[512]{0:T(512)}, f32[512]{0:T(512)S(1)}, u32[]{:S(2)}) copy-start(f32[512]{0:T(512)S(1)} %add_rsqrt_fusion.3) | copy-start | bytes 6148
  22.7 16.3 %copy-start.62 = (f32[512]{0:T(512)}, f32[512]{0:T(512)S(1)}, u32[]{:S(2)}) copy-start(f32[512]{0:T(512)S(1)} %add_rsqrt_fusion.1) | copy-start | bytes 6148
  38.1 39.1 %copy-start.32 = (bf16[3,768,192]{1,2,0:T(8,128)(2,1)}, bf16[3,768,192]{1,2,0:T(8,128)(2,1)S(1)}, u32[]{:S(2)}) copy-start(bf16[3,768,192]{1,2,0:T(8,128)(2,1)S(1)} %all_gather.22) | copy-start | bytes 2654212
  59.3 67.3 %copy-start.17 = (bf16[1,2048,192]{1,2,0:T(8,128)(2,1)}, bf16[1,2048,192]{1,2,0:T(8,128)(2,1)S(1)}, u32[]{:S(2)}) copy-start(bf16[1,2048,192]{1,2,0:T(8,128)(2,1)S(1)} %all-gather.3) | copy-start | bytes 2359300
  77.2 54.0 %copy-start.16 = (bf16[1,2048,192]{1,2,0:T(8,128)(2,1)}, bf16[1,2048,192]{1,2,0:T(8,128)(2,1)S(1)}, u32[]{:S(2)}) copy-start(bf16[1,2048,192]{1,2,0:T(8,128)(2,1)S(1)} %all-gather.2) | copy-start | bytes 2359300
  78.2 36.3 %copy-start.39 = (bf16[1,512,192]{1,2,0:T(8,128)(2,1)}, bf16[1,512,192]{1,2,0:T(8,128)(2,1)S(1)}, u32[]{:S(2)}) copy-start(bf16[1,512,192]{1,2,0:T(8,128)(2,1)S(1)} %get-tuple-element.185) | copy-start | bytes 589828
  95.3 21.9 %copy-start.19 = (bf16[1,2048,192]{1,2,0:T(8,128)(2,1)}, bf16[1,2048,192]{1,2,0:T(8,128)(2,1)S(1)}, u32[]{:S(2)}) copy-start(bf16[1,2048,192]{1,2,0:T(8,128)(2,1)S(1)} %all-gather.1) | copy-start | bytes 2359300
  138.5 73.0 %all-gather.7.cloned.1.call-start = ((), (), s32[]{:S(2)}) async-start(), calls=%async_computation.10 | async-start | bytes 1769472 | tf_op jit(solution)/shard_map/all_gather | solution.py:57
  139.0 78.4 %all-gather.9.cloned.1.call-start = ((), (), s32[]{:S(2)}) async-start(), calls=%async_computation.11 | async-start | bytes 1769472 | tf_op jit(solution)/shard_map/all_gather | solution.py:58
  139.6 155.7 %all-reduce.12.cloned.1.call-start = ((), (), s32[]{:S(2)}) async-start(), calls=%async_computation.23 | async-start | bytes 6291456 | tf_op jit(solution)/shard_map/psum | solution.py:160
  210.3 88.9 %copy-start.56 = (f32[512]{0:T(512)}, f32[512]{0:T(512)S(1)}, u32[]{:S(2)}) copy-start(f32[512]{0:T(512)S(1)} %broadcast_multiply_fusion.10) | copy-start | bytes 6148
  211.4 87.8 %copy-start.58 = (f32[512]{0:T(512)}, f32[512]{0:T(512)S(1)}, u32[]{:S(2)}) copy-start(f32[512]{0:T(512)S(1)} %add_rsqrt_fusion) | copy-start | bytes 6148
  211.5 87.8 %copy-start.65 = (f32[512]{0:T(512)}, f32[512]{0:T(512)S(1)}, u32[]{:S(2)}) copy-start(f32[512]{0:T(512)S(1)} %add_rsqrt_fusion.2) | copy-start | bytes 6148
  226.6 146.2 %reduce-scatter.17.cloned.1.call-start = ((), (), s32[]{:S(2)}) async-start(), calls=%async_computation.13 | async-start | bytes 1966080 | tf_op jit(solution)/shard_map/reduce_scatter | solution.py:206
  311.3 72.8 %reduce-scatter.21.cloned.1.call-start = ((), (), s32[]{:S(2)}) async-start(), calls=%async_computation.15 | async-start | bytes 1966080 | tf_op jit(solution)/shard_map/reduce_scatter | solution.py:206
  321.9 98.8 %reduce-scatter.19.cloned.1.call-start = ((), (), s32[]{:S(2)}) async-start(), calls=%async_computation.14 | async-start | bytes 1966080 | tf_op jit(solution)/shard_map/reduce_scatter | solution.py:203
  339.0 118.3 %reduce-scatter.15.cloned.1.call-start = ((), (), s32[]{:S(2)}) async-start(), calls=%async_computation.12 | async-start | bytes 1966080 | tf_op jit(solution)/shard_map/reduce_scatter | solution.py:203
  356.2 224.7 %all-reduce.10.cloned.1.call-start = ((), (), s32[]{:S(2)}) async-start(), calls=%async_computation.22 | async-start | bytes 12582912 | tf_op jit(solution)/shard_map/psum | solution.py:148
  373.8 84.5 %copy-start.45 = (bf16[1,512,192]{1,2,0:T(8,128)(2,1)}, bf16[1,512,192]{1,2,0:T(8,128)(2,1)S(1)}, u32[]{:S(2)}) copy-start(bf16[1,512,192]{1,2,0:T(8,128)(2,1)S(1)} %convert_bitcast_fusion.6) | copy-start | bytes 589828
  385.1 40.5 %copy-start.47 = (bf16[1,512,192]{1,2,0:T(8,128)(2,1)}, bf16[1,512,192]{1,2,0:T(8,128)(2,1)S(1)}, u32[]{:S(2)}) copy-start(bf16[1,512,192]{1,2,0:T(8,128)(2,1)S(1)} %convert_bitcast_fusion.4) | copy-start | bytes 589828
  462.3 123.6 %reduce-scatter.25.cloned.1.call-start = ((), (), s32[]{:S(2)}) async-start(), calls=%async_computation.17 | async-start | bytes 884736 | tf_op jit(solution)/shard_map/reduce_scatter | solution.py:244
  466.3 119.7 %reduce-scatter.27.cloned.1.call-start = ((), (), s32[]{:S(2)}) async-start(), calls=%async_computation.18 | async-start | bytes 3538944 | tf_op jit(solution)/shard_map/reduce_scatter | solution.py:245
  472.0 114.0 %reduce-scatter.29.cloned.1.call-start = ((), (), s32[]{:S(2)}) async-start(), calls=%async_computation.19 | async-start | bytes 3538944 | tf_op jit(solution)/shard_map/reduce_scatter | solution.py:246
  477.7 108.3 %reduce-scatter.23.cloned.1.call-start = ((), (), s32[]{:S(2)}) async-start(), calls=%async_computation.16 | async-start | bytes 2654208 | tf_op jit(solution)/shard_map/reduce_scatter | solution.py:243
  482.7 98.1 %copy-start.64 = (f32[512]{0:T(512)S(1)}, f32[512]{0:T(512)}, u32[]{:S(2)}) copy-start(f32[512]{0:T(512)} %copy-done.62) | copy-start | bytes 6148
  482.8 118.4 %reduce-scatter.33.cloned.1.call-start = ((), (), s32[]{:S(2)}) async-start(), calls=%async_computation.21 | async-start | bytes 589824
  584.8 32.4 %reduce-scatter.31.cloned.1.call-start = ((), (), s32[]{:S(2)}) async-start(), calls=%async_computation.20 | async-start | bytes 589824
  585.9 167.6 %all-reduce.16.cloned.1.call-start = ((), (), s32[]{:S(2)}) async-start(), calls=%async_computation.25 | async-start | bytes 7077888 | tf_op jit(solution)/shard_map/psum | solution.py:239
  (69 other events, 228.5 us)
Sparse Core Ops, SparseCore 0:
  138.6 69.2 all-reduce.13
  226.8 68.5 all-reduce.11
  462.4 118.4 all-reduce.9
Sparse Core Ops, SparseCore 1:
  140.5 23.4 all-gather.6
  165.3 22.6 all-gather.8
  311.4 35.5 reduce-scatter.16
  349.8 34.2 reduce-scatter.20
  386.4 34.2 reduce-scatter.18
  423.0 34.2 reduce-scatter.14
  466.4 14.0 reduce-scatter.24
  483.1 34.7 reduce-scatter.26
  520.0 34.7 reduce-scatter.28
  557.0 28.2 reduce-scatter.22
  588.0 13.1 reduce-scatter.32
  604.0 13.1 reduce-scatter.30
  619.7 133.7 all-reduce.15
where the time goes:
time: 774 us; the launch traced here: 766 us
  waiting for transfers between devices  457 us (59%)
  matrix products  110 us (14%)
  blocking collectives  108 us (14%)
  other arithmetic  46.1 us (6%)
  local copies, waits for them, and re-layouts  26.6 us (3%)
  between operations  16.9 us (2%)
    psum x1, waiting for transfers between devices, body(): lax.psum((acc_qkv, acc_out, acc_up, acc_down, acc_gains, acc_shifts), 'ctx')  123 us
    psum x1, waiting for transfers between devices, body(): mlp = lax.psum(mlp_part, 'tp')  97.4 us
    psum x1, waiting for transfers between devices, body(): second_norm_gradient = lax.psum(n2_back, 'tp')  68.7 us
    psum x1, waiting for transfers between devices, body(): attn = lax.psum(attn_part, 'tp')  67.9 us
    reduce_scatter x2, waiting for transfers between devices, body(): lax.psum_scatter(key_sum.reshape(seq_len, local_width), 'ctx', scatter_di...  67.2 us
    all_gather x2, blocking collectives, body(): lax.all_gather(qkv[1], 'ctx', axis=0, tiled=True)  36.6 us
    all_gather x2, blocking collectives, body(): lax.all_gather(qkv[2], 'ctx', axis=0, tiled=True)  33.6 us
    unnamed x178, local copies, waits for them, and re-layouts  24.4 us
  transfers between devices with their start and end apart: 16, of which 9 were waited for; matrix products, arithmetic and copies ran while one was open for 14% of the time, Pallas kernels for 0%

commit v1 on v0

v1 whole, which is shorter than its diff:
```python
import functools

import jax
import jax.numpy as jnp
from jax import lax
from jax.experimental import pallas as pl
from jax.experimental.pallas import tpu as pltpu
from jax.sharding import PartitionSpec as P

HEAD_DIM = 64
DEPTH = 12
EPS = 1e-05
GELU_C = 0.7978845608028654
GELU_A = 0.044715
NEG = -1e30
BRANCH = DEPTH ** (-0.5)
MESH = pl.DeviceIdType.MESH
F32 = jnp.float32
BF16 = jnp.bfloat16
VMEM_LIMIT = 60 * 1024 * 1024


def gelu_value(u):
    return 0.5 * u * (1.0 + jnp.tanh(GELU_C * (u + GELU_A * u * u * u)))


def gelu_slope(u):
    inner = jnp.tanh(GELU_C * (u + GELU_A * u * u * u))
    return 0.5 * (1.0 + inner) + 0.5 * u * (1.0 - inner * inner) * GELU_C * (
        1.0 + 3.0 * GELU_A * u * u
    )


def normalize(x):
    centered = x - jnp.mean(x, axis=1, keepdims=True)
    inv = lax.rsqrt(jnp.mean(centered * centered, axis=1, keepdims=True) + EPS)
    return centered * inv, inv


def dot_nn(a, b):
    return lax.dot_general(a, b, (((1,), (0,)), ((), ())), preferred_element_type=F32)


def dot_nt(a, b):
    return lax.dot_general(a, b, (((1,), (1,)), ((), ())), preferred_element_type=F32)


def dot_tn(a, b):
    return lax.dot_general(a, b, (((0,), (0,)), ((), ())), preferred_element_type=F32)


def remote(src, dst, send, recv, **ids):
    return pltpu.make_async_remote_copy(
        src_ref=src, dst_ref=dst, send_sem=send, recv_sem=recv, device_id=ids, device_id_type=MESH
    )


class Place:
    def __init__(self, n_ctx):
        self.n = n_ctx
        self.c = lax.axis_index("ctx")
        self.d = lax.axis_index("dp")
        tp = lax.axis_index("tp")
        self.core = lax.rem(tp, 2)
        self.mate = tp + 1 - 2 * self.core
        chip = lax.div(tp, 2)
        self.across = (1 - chip) * 2 + self.core

    def barrier(self, dp, tp, ctx):
        sem = pltpu.get_barrier_semaphore()

        def hello(**ids):
            pl.semaphore_signal(sem, inc=1, device_id=ids, device_id_type=MESH)

        count = 0
        if dp:
            hello(dp=1 - self.d)
            count += 1
        if tp:
            hello(tp=self.mate)
            hello(tp=self.across)
            count += 2
        if ctx:
            pl.when(self.c > 0)(lambda: hello(ctx=self.c - 1))
            pl.when(self.c < self.n - 1)(lambda: hello(ctx=self.c + 1))
        if ctx:
            count = count + jnp.minimum(self.c, 1) + jnp.minimum(self.n - 1 - self.c, 1)
        pl.semaphore_wait(sem, count)


class TpSum:
    def __init__(self, place, half, mine, out_half, in_half, out_sum, in_sum, total, send, recv):
        self.p, self.half = place, half
        self.mine, self.out_half, self.in_half = mine, out_half, in_half
        self.out_sum, self.in_sum, self.total = out_sum, in_sum, total
        self.send, self.recv = send, recv

    def rows(self, core):
        return pl.ds(pl.multiple_of(core * self.half, self.half), self.half)

    def c1(self):
        return remote(self.out_half, self.in_half, self.send.at[0], self.recv.at[0], tp=self.p.mate)

    def c2(self):
        return remote(self.out_sum, self.in_sum, self.send.at[1], self.recv.at[1], tp=self.p.across)

    def c3(self, core):
        part = self.total.at[self.rows(core)]
        return remote(part, part, self.send.at[2], self.recv.at[2], tp=self.p.mate)

    def start(self, partial):
        self.out_half[...] = partial(self.rows(1 - self.p.core)).astype(BF16)
        self.c1().start()
        self.mine[...] = partial(self.rows(self.p.core))

    def step2(self):
        self.c1().wait_recv()
        self.out_sum[...] = (self.mine[...] + self.in_half[...].astype(F32)).astype(BF16)
        self.c2().start()

    def step3(self):
        self.c2().wait_recv()
        both = self.out_sum[...].astype(F32) + self.in_sum[...].astype(F32)
        self.total[self.rows(self.p.core), :] = both.astype(BF16)
        self.c3(self.p.core).start()

    def finish(self):
        self.c3(1 - self.p.core).wait_recv()

    def drain(self):
        self.c1().wait_send()
        self.c2().wait_send()
        self.c3(self.p.core).wait_send()


def tp_scratch(sets, half, width):
    return [
        pltpu.VMEM((sets, half, width), F32),
        pltpu.VMEM((sets, half, width), BF16),
        pltpu.VMEM((sets, half, width), BF16),
        pltpu.VMEM((sets, half, width), BF16),
        pltpu.VMEM((sets, half, width), BF16),
        pltpu.SemaphoreType.DMA((sets, 3)),
        pltpu.SemaphoreType.DMA((sets, 3)),
    ]


def tp_set(place, half, scratch, index, total):
    mine, out_half, in_half, out_sum, in_sum, send, recv = scratch
    return TpSum(
        place, half, mine.at[index], out_half.at[index], in_half.at[index], out_sum.at[index],
        in_sum.at[index], total, send.at[index], recv.at[index],
    )


def query_limits(border, prefix, m, c, rows):
    half = rows // 2
    lane = lax.broadcasted_iota(jnp.int32, (1, rows), 1)
    pos = jnp.where(lane < half, border[2 * c] * half + lane, border[2 * c + 1] * half + lane - half)
    return jnp.maximum(pos, prefix[m, 0] - 1)


def key_positions(border, block, half):
    return border[block] * half + lax.broadcasted_iota(jnp.int32, (half, 1), 0)


def forward_kernel(
    n_ctx, exchange, prefix, border, hid, *refs
):
    if exchange:
        (wp_s, wo_s, wu_s, wd_s, ln_s) = refs[:5]
        refs = refs[5:]
        (attn, heads, lse, o_t, qs, kv, h1, wp, wo, wu, wd, ln) = refs[:12]
        refs = refs[12:]
    else:
        (wp, wo, wu, wd, ln) = refs[:5]
        refs = refs[5:]
        (attn, heads, lse, o_t, qs, kv, h1) = refs[:7]
        refs = refs[7:]
    (m_row, l_row, o_acc, heads_t, ks, kr, ws, wr) = refs[:8]
    tp_refs = refs[8:15]
    p = Place(n_ctx)
    c, n = p.c, n_ctx
    micro, rows, width = hid.shape
    half = rows // 2
    p.barrier(exchange, True, True)

    def pairs():
        size = wp_s.shape[0]
        span = pl.ds(pl.multiple_of(p.d * size, size), size)
        usize = wu_s.shape[0]
        uspan = pl.ds(pl.multiple_of(p.d * usize, usize), usize)
        return (
            (ln_s, ln.at[p.d]), (wp_s, wp.at[span]), (wo_s, wo.at[p.d]),
            (wu_s, wu.at[uspan]), (wd_s, wd.at[p.d]),
        )

    def weight_copy(i, src, dst):
        return remote(src, dst, ws.at[i], wr.at[i], dp=1 - p.d)

    if exchange:
        for i, (src, dst) in enumerate(pairs()):
            weight_copy(i, src, dst).start()
        for i, (src, dst) in enumerate(pairs()):
            dst[...] = src[...]
        weight_copy(0, *pairs()[0]).wait_recv()
    gain = jnp.concatenate([ln[i, 0:1, :] for i in range(ln.shape[0])], axis=1)
    shift = jnp.concatenate([ln[i, 2:3, :] for i in range(ln.shape[0])], axis=1)

    for m in range(micro):
        @pl.loop(0, rows // 128)
        def _(i):
            span = pl.ds(pl.multiple_of(i * 128, 128), 128)
            xhat, _ = normalize(hid[m, span, :].astype(F32))
            h1[m, span, :] = (xhat * gain + shift).astype(BF16)

    def kv_copy(m, way, s):
        j, to = (c - s, c + 1) if way == 0 else (c + s, c - 1)
        block = kv.at[m, j]
        return remote(block, block, ks.at[m, way, s], kr.at[m, way, s + 1], ctx=to)

    def kv_arrival(m, way, s):
        j = c - s if way == 0 else c + s
        to = c - 1 if way == 0 else c + 1
        block = kv.at[m, j]
        return remote(block, block, ks.at[m, way, s], kr.at[m, way, s], ctx=to)

    def has(way, s):
        return c - s >= 0 if way == 0 else c + s < n

    def sends(way, s):
        if way == 0:
            return jnp.logical_and(c - s >= 0, c + 1 < n)
        return jnp.logical_and(c + s < n, c - 1 >= 0)

    if exchange:
        weight_copy(1, *pairs()[1]).wait_recv()
    for m in range(micro):
        @pl.loop(0, rows // 128)
        def _(i):
            span = pl.ds(pl.multiple_of(i * 128, 128), 128)
            packed = dot_nn(h1[m, span, :], wp[...])
            qs[m, span, :] = (packed[:, 0:256].astype(BF16).astype(F32) * HEAD_DIM ** (-0.5)).astype(BF16)
            kv[m, c, span, :] = packed[:, 256:640].astype(BF16)

        if m == 0:
            for way in range(2):
                pl.when(sends(way, 0))(lambda way=way: kv_copy(0, way, 0).start())
    pl.when(c == 0)(lambda: kv_copy(1, 0, 0).start())
    pl.when(c == n - 1)(lambda: kv_copy(1, 1, 0).start())

    def attend(m, j, limits):
        lanes = lax.broadcasted_iota(jnp.int32, (rows, 128), 1)
        q01 = qs[m, :, 0:128]
        zero = jnp.zeros_like(q01)
        q_heads = (
            jnp.where(lanes < 64, q01, zero), jnp.where(lanes < 64, zero, q01), qs[m, :, 128:256]
        )
        for b in range(2):
            span = pl.ds(b * half, half)
            k01 = kv[m, j, span, 0:128]
            k2v0 = kv[m, j, span, 128:256]
            v12 = kv[m, j, span, 256:384]
            t0 = k2v0.T
            t12 = v12.T
            allowed = key_positions(border, 2 * j + b, half) <= limits
            for h in range(3):
                scores = dot_nt(k2v0 if h == 2 else k01, q_heads[h])
                scores = jnp.where(allowed, scores, NEG)
                old = m_row[h]
                top = jnp.maximum(old, jnp.max(scores, axis=0, keepdims=True))
                prob = jnp.exp(scores - top)
                fade = jnp.exp(old - top)
                m_row[h] = top
                l_row[h] = l_row[h] * fade + jnp.sum(prob, axis=0, keepdims=True)
                v_t = t0[64:128] if h == 0 else t12[(h - 1) * 64 : h * 64]
                o_acc[h] = o_acc[h] * fade + dot_nn(v_t, prob.astype(BF16))

    tops = [tp_set(p, half, tp_refs, m, attn.at[m]) for m in range(micro)]
    for m in range(micro):
        limits = query_limits(border, prefix, m, c, rows)
        m_row[...] = jnp.full(m_row.shape, NEG, F32)
        l_row[...] = jnp.zeros(l_row.shape, F32)
        o_acc[...] = jnp.zeros(o_acc.shape, F32)

        @pl.loop(0, 2 * n - 1)
        def _(t, m=m, limits=limits):
            s = lax.div(t + 1, 2)
            right = lax.rem(t, 2) == 1
            left = jnp.logical_and(lax.rem(t, 2) == 0, t > 0)

            def arrive(way):
                kv_arrival(m, way, s).wait_recv()
                pl.when(sends(way, s))(lambda: kv_copy(m, way, s).start())
                if m == 0:
                    last = c if way == 0 else n - 1 - c
                    pl.when(jnp.logical_and(s == last, sends(way, 0)))(
                        lambda: kv_copy(1, way, 0).start()
                    )

            pl.when(jnp.logical_and(right, has(0, s)))(lambda: arrive(0))
            pl.when(jnp.logical_and(left, has(1, s)))(lambda: arrive(1))
            j = jnp.where(right, c - s, c + s)

            @pl.when(jnp.logical_and(j >= 0, j < n))
            def _():
                attend(m, j, limits)

            if m == 1:
                pl.when(t == 0)(tops[0].step2)
                pl.when(t == 3)(tops[0].step3)

        for h in range(3):
            norm = o_acc[h] / l_row[h]
            o_t[m, h] = norm
            lse[m, h : h + 1, :] = m_row[h] + jnp.log(l_row[h])
            at = 192 if h == 0 else (h - 1) * 64
            heads_t[at : at + 64, :] = norm
        heads_t[128:192, :] = jnp.zeros((64, rows), F32)
        heads[m] = heads_t[...].T.astype(BF16)
        if exchange and m == 0:
            weight_copy(2, *pairs()[2]).wait_recv()

        def project(span, m=m):
            left = heads[m, span, :]
            return jnp.concatenate([dot_nn(left, wo[i]) for i in range(wo.shape[0])], axis=1)

        tops[m].start(project)
    tops[0].finish()
    tops[1].step2()
    tops[1].step3()
    tops[1].finish()
    if exchange:
        for i in range(3, 5):
            weight_copy(i, *pairs()[i]).wait_recv()
        for i in range(5):
            weight_copy(i, *pairs()[i]).wait_send()
    for m in range(micro):
        for way in range(2):
            for s in range(n - 1):
                pl.when(sends(way, s))(lambda m=m, way=way, s=s: kv_copy(m, way, s).wait_send())
        tops[m].drain()


def vmem_specs(k):
    return [pl.BlockSpec(memory_space=pltpu.VMEM)] * k


def run_forward(n_ctx, exchange, prefix, border, hid, weights):
    micro, rows, width = hid.shape
    half = rows // 2
    sds = jax.ShapeDtypeStruct
    outs = [
        sds((micro, rows, width), BF16),
        sds((micro, rows, 256), BF16),
        sds((micro, 8, rows), F32),
        sds((micro, 3, 64, rows), F32),
        sds((micro, rows, 256), BF16),
        sds((micro, n_ctx, rows, 384), BF16),
        sds((micro, rows, width), BF16),
    ]
    if exchange:
        wp, wo, wu, wd, ln = weights
        outs += [
            sds((2 * wp.shape[0], wp.shape[1]), BF16),
            sds((2,) + wo.shape, BF16),
            sds((2 * wu.shape[0], wu.shape[1]), BF16),
            sds((2,) + wd.shape, BF16),
            sds((2,) + ln.shape, F32),
        ]
    scratch = [
        pltpu.VMEM((3, 1, rows), F32),
        pltpu.VMEM((3, 1, rows), F32),
        pltpu.VMEM((3, 64, rows), F32),
        pltpu.VMEM((256, rows), F32),
        pltpu.SemaphoreType.DMA((micro, 2, n_ctx + 1)),
        pltpu.SemaphoreType.DMA((micro, 2, n_ctx + 1)),
        pltpu.SemaphoreType.DMA((5,)),
        pltpu.SemaphoreType.DMA((5,)),
    ] + tp_scratch(micro, half, width)
    smem = pl.BlockSpec(memory_space=pltpu.SMEM)
    out = pl.pallas_call(
        functools.partial(forward_kernel, n_ctx, exchange),
        out_shape=outs,
        in_specs=[smem, smem] + vmem_specs(1 + len(weights)),
        out_specs=vmem_specs(len(outs)),
        scratch_shapes=scratch,
        compiler_params=pltpu.CompilerParams(
            collective_id=0, has_side_effects=True, vmem_limit_bytes=VMEM_LIMIT
        ),
        name="attention_forward",
    )(prefix, border, hid, *weights)
    return out if exchange else list(out) + list(weights)


def apply_layer_norm(values, norm_gain, norm_shift):
    normalized, inv = normalize(values)
    return (normalized * norm_gain + norm_shift, normalized, inv)


def norm_backward(normed_gradient, normalized_input, inverse_deviation, norm_gain):
    scaled_gradient = normed_gradient * norm_gain
    return inverse_deviation * (
        scaled_gradient
        - jnp.mean(scaled_gradient, axis=1, keepdims=True)
        - normalized_input * jnp.mean(scaled_gradient * normalized_input, axis=1, keepdims=True)
    )


def pack_weights(qkv_weight, out_weight, up_weight, down_weight, ln_gains, ln_shifts, exchange):
    q, k, v = qkv_weight[0], qkv_weight[1], qkv_weight[2]
    pad = jnp.zeros((q.shape[0], 64), BF16)
    wp = jnp.concatenate([q, pad, k, v], axis=1)
    wo = jnp.concatenate(
        [out_weight[64:], jnp.zeros((64, out_weight.shape[1]), BF16), out_weight[:64]], axis=0
    )
    ln = jnp.concatenate([ln_gains, ln_shifts], axis=0).astype(F32)
    ln = jnp.pad(ln, ((0, 4), (0, 0)))
    if exchange:
        return [wp, wo, up_weight, down_weight, ln]
    gather = functools.partial(lax.all_gather, axis_name="dp", tiled=True)
    return [
        gather(wp, axis=0), gather(wo, axis=1)[None], gather(up_weight, axis=0),
        gather(down_weight, axis=1)[None], gather(ln, axis=1)[None],
    ]


def side_by_side(stack):
    return jnp.concatenate([stack[i] for i in range(stack.shape[0])], axis=-1)


def body(
    hidden_in, prefix, block_order, qkv_weight, out_weight, up_weight, down_weight, ln_gains,
    ln_shifts, cotangent,
):
    micro, _, tokens, width = hidden_in.shape
    local_width = qkv_weight.shape[2]
    heads_n = local_width // HEAD_DIM
    n_ctx = lax.axis_size("ctx")
    n_dp = lax.axis_size("dp")
    exchange = n_dp == 2
    seq_len = tokens * n_ctx
    half = tokens // 2
    scale = HEAD_DIM ** (-0.5)
    weights = pack_weights(
        qkv_weight, out_weight, up_weight, down_weight, ln_gains, ln_shifts, exchange
    )
    (attn, heads, lse, o_t, qs, kv, h1, wp, wo, wu, wd, ln) = run_forward(
        n_ctx, exchange, prefix, block_order, hidden_in[:, 0], weights
    )
    out_full = side_by_side(wo)
    down_full = side_by_side(wd)
    ln_full = side_by_side(ln)
    gains, shifts = ln_full[0:2], ln_full[2:4]

    cuts = jnp.arange(seq_len, dtype=jnp.int32)
    key_pos = jnp.repeat(block_order, half, total_repeat_length=seq_len) * half + cuts % half
    query_pos = lax.dynamic_slice_in_dim(key_pos, lax.axis_index("ctx") * tokens, tokens)
    acc = None
    results, grads_in = [], []
    for m in range(micro):
        x = hidden_in[m, 0].astype(F32)
        allowed = (key_pos[None, :] <= query_pos[:, None]) | (key_pos[None, :] < prefix[m, 0])
        xhat1, inv1 = normalize(x)
        mid = x + BRANCH * attn[m].astype(F32)
        n2, xhat2, inv2 = apply_layer_norm(mid, gains[1], shifts[1])
        h2 = n2.astype(BF16)
        up = dot_nn(h2, wu)
        act = gelu_value(up).astype(BF16)
        mlp = lax.psum(dot_nn(act, down_full), "tp")
        results.append((mid + BRANCH * mlp).astype(BF16))
        g = cotangent[m, 0].astype(F32)
        d_mlp = (BRANCH * g).astype(BF16)
        grad_down = dot_tn(act, d_mlp)
        d_up = (dot_nt(d_mlp, down_full) * gelu_slope(up)).astype(BF16)
        grad_up = dot_tn(h2, d_up)
        d_n2 = lax.psum(dot_nt(d_up, wu), "tp")
        d_mid = g + norm_backward(d_n2, xhat2, inv2, gains[1])
        d_attn = (BRANCH * d_mid).astype(BF16)
        grad_out = dot_tn(heads[m], d_attn)
        d_heads = dot_nt(d_attn, out_full).astype(BF16)
        q = qs[m][:, :local_width].reshape(tokens, heads_n, HEAD_DIM)
        flat = kv[m].reshape(seq_len, 2 * local_width)
        keys = flat[:, :local_width].reshape(seq_len, heads_n, HEAD_DIM)
        values = flat[:, local_width:].reshape(seq_len, heads_n, HEAD_DIM)
        dh = jnp.concatenate([d_heads[:, 192:], d_heads[:, :128]], axis=1)
        dh = dh.reshape(tokens, heads_n, HEAD_DIM)
        scores = jnp.einsum("qhd,khd->hqk", q, keys, preferred_element_type=F32)
        scores = jnp.where(allowed[None], scores, NEG)
        prob = jnp.exp(scores - lse[m, :heads_n][:, :, None])
        d_prob = jnp.einsum("qhd,khd->hqk", dh, values, preferred_element_type=F32)
        d_scores = (prob * (d_prob - jnp.sum(prob * d_prob, axis=2, keepdims=True))).astype(BF16)
        d_q = jnp.einsum("hqk,khd->qhd", d_scores, keys, preferred_element_type=F32) * scale
        d_k = jnp.einsum("hqk,qhd->khd", d_scores, q, preferred_element_type=F32)
        d_v = jnp.einsum("hqk,qhd->khd", prob.astype(BF16), dh, preferred_element_type=F32)
        d_kv = jnp.concatenate(
            [d_k.reshape(seq_len, local_width), d_v.reshape(seq_len, local_width)], axis=1
        )
        d_kv = lax.psum_scatter(d_kv, "ctx", scatter_dimension=0, tiled=True)
        d_pack = jnp.concatenate(
            [d_q.reshape(tokens, local_width), jnp.zeros((tokens, 64), F32), d_kv], axis=1
        ).astype(BF16)
        grad_pack = dot_tn(h1[m], d_pack)
        d_n1 = lax.psum(dot_nt(d_pack, wp), "tp")
        grads_in.append(d_mid + norm_backward(d_n1, xhat1, inv1, gains[0]))
        new = (
            grad_pack, grad_out, grad_up, grad_down,
            jnp.stack([jnp.sum(d_n1 * xhat1, axis=0), jnp.sum(d_n2 * xhat2, axis=0)]),
            jnp.stack([jnp.sum(d_n1, axis=0), jnp.sum(d_n2, axis=0)]),
        )
        acc = new if acc is None else jax.tree.map(jnp.add, acc, new)
    pack, g_out, g_up, g_down, g_gains, g_shifts = acc
    g_qkv = jnp.stack([pack[:, 0:192], pack[:, 256:448], pack[:, 448:640]])
    g_out = jnp.concatenate([g_out[192:], g_out[:128]], axis=0)
    whole = lax.psum((g_qkv, g_out, g_up, g_down, g_gains, g_shifts), "ctx")
    dims = (1, 1, 0, 1, 1, 1)
    owned = [
        lax.psum_scatter(v, "dp", scatter_dimension=d, tiled=True) for v, d in zip(whole, dims)
    ]
    return (jnp.stack(results)[:, None], jnp.stack(grads_in)[:, None], *owned)


def solution(mesh):
    in_specs = (
        P(None, "dp", "ctx", None), P(None, "dp"), P(), P(None, "dp", "tp"), P("tp", "dp"),
        P("dp", "tp"), P("tp", "dp"), P(None, "dp"), P(None, "dp"), P(None, "dp", "ctx", None),
    )
    out_specs = (
        P(None, "dp", "ctx", None), P(None, "dp", "ctx", None), P(None, "dp", "tp"),
        P("tp", "dp"), P("dp", "tp"), P("tp", "dp"), P(None, "dp"), P(None, "dp"),
    )
    return jax.shard_map(body, mesh=mesh, in_specs=in_specs, out_specs=out_specs, check_vma=False)
```

time: 774 us -> 778 us (level)
  blocking collectives: 108 us -> 12.7 us
  Pallas kernels: 0 us -> 95.1 us
  matrix products: 110 us -> 77.9 us
  local copies, waits for them, and re-layouts: 26.6 us -> 50.1 us
  other arithmetic: 46.1 us -> 59.6 us
    reduce_scatter x8 -> x6, waiting for transfers between devices: 77.5 us -> 185 us  [the longest x4 116 us: body(): lax.psum_scatter(v, 'dp', scatter_dimension=d, tiled=True)]
    psum x4 -> x3, waiting for transfers between devices: 357 us -> 253 us  [the longest x1 123 us: body(): whole = lax.psum((g_qkv, g_out, g_up, g_down, g_gains, g_shifts), 'ctx')]
    all_gather x8 -> x0, blocking collectives: 95.4 us -> none  [the longest x2 36.6 us: body(): lax.all_gather(qkv[1], 'ctx', axis=0, tiled=True)]
    pallas_call x0 -> x1, Pallas kernels: none -> 95.1 us  [run_forward(): pl.pallas_call(functools.partial(forward_kernel, n_ctx, exchange), out_sh...]
    dot_general x34 -> x30, matrix products: 108 us -> 77.9 us  [the longest x8 15.6 us: dot_tn(): lax.dot_general(a, b, (((0,), (0,)), ((), ())), preferred_element_type=F32)]
    slice x5 -> x21, local copies, waits for them, and re-layouts: 2.16 us -> 21.6 us  [the longest x4 9.52 us: body(): values = flat[:, local_width:].reshape(seq_len, heads_n, HEAD_DIM)]
    reduce_sum x10 -> x5, other arithmetic: 16.5 us -> 13.3 us  [the longest x1 4.8 us: body(): jnp.sum(d_n1 * xhat1, axis=0)]
    unnamed x178 -> x194, local copies, waits for them, and re-layouts: 24.4 us -> 23.3 us
  transfers between devices with their start and end apart: 16 -> 11, of which waited for: 9 -> 11; matrix products, arithmetic and copies ran while one was open for 14% -> 15% of each run, Pallas kernels for 0% -> 0%
where the time goes in v1:
time: 778 us; the launch traced here: 772 us
  waiting for transfers between devices  460 us (59%)
  Pallas kernels  95.1 us (12%)
  matrix products  77.9 us (10%)
  other arithmetic  59.6 us (8%)
  local copies, waits for them, and re-layouts  50.1 us (6%)
  between operations  15.4 us (2%)
  blocking collectives  12.7 us (2%)
    psum x1, waiting for transfers between devices, body(): whole = lax.psum((g_qkv, g_out, g_up, g_down, g_gains, g_shifts), 'ctx')  123 us
    reduce_scatter x4, waiting for transfers between devices, body(): lax.psum_scatter(v, 'dp', scatter_dimension=d, tiled=True)  116 us
    psum x1, waiting for transfers between devices, body(): mlp = lax.psum(dot_nn(act, down_full), 'tp')  99.8 us
    pallas_call x1, Pallas kernels, run_forward(): pl.pallas_call(functools.partial(forward_kernel, n_ctx, exchange), out_sh...  95.1 us
    reduce_scatter x2, waiting for transfers between devices, body(): d_kv = lax.psum_scatter(d_kv, 'ctx', scatter_dimension=0, tiled=True)  68 us
    psum x1, waiting for transfers between devices, body(): d_n2 = lax.psum(dot_nt(d_up, wu), 'tp')  30.3 us
    unnamed x194, local copies, waits for them, and re-layouts  23.3 us
    unnamed x13, waiting for transfers between devices  22.6 us
  transfers between devices with their start and end apart: 11, of which 11 were waited for; matrix products, arithmetic and copies ran while one was open for 15% of the time, Pallas kernels for 0%

profile of v1, /device:TPU:0, one launch (start us, length us, event | category | flops | bytes accessed | tf_op | source)
XLA Modules:
  0.0 771.9 jit_solution(4305833894081768113)
XLA Ops:
  12.3 95.1 %attention_forward.1 = (bf16[2,512,768]{2,1,0:T(8,128)(2,1)}, bf16[2,512,256]{2,1,0:T(8,128)(2,1)}, f32[2,8,512]{2,1,0:T(8,128)}, f32[2,3,64,512]{3,2,1,0:T(8,12...) custom-call(s32[2,1]{1,0:T(2,128)} %copy.47.prefix, ...), custom_call_target="tpu_custom_call" | custom-call | tf_op jit(solution)/shard_map/attention_forward/pallas_call | solution.py:382
  126.0 6.1 broadcast_compare_fusion.1
  133.9 3.4 fusion.118
  149.0 3.5 compare_or_fusion.1
  152.5 6.4 fusion.125
  158.8 30.3 %all-reduce.11.cloned.1.call-done = (f32[512,768]{1,0:T(8,128)}, f32[512,768]{1,0:T(8,128)}) async-done(((f32[512,768]{1,0:T(8,128)}, f32[512,768]{1,0:T(8,128)}), (f32[512,768]{1,0:T(8,128)}, f32[512,768]{1,0:T(8,128)})) %all-reduce.11.cloned.1.call-update) | async-done | bytes 3145744 | tf_op jit(solution)/shard_map/psum | solution.py:477
  189.2 4.4 multiply_reduce_fusion.3
  199.8 3.1 fusion.4
  202.9 6.8 multiply_reduce_fusion.1
  209.7 6.9 multiply_convert_fusion.1
  221.2 3.4 fusion.120
  230.1 3.1 fusion.128
  234.7 6.8 multiply_reduce_fusion
  241.5 6.7 multiply_convert_fusion
  252.1 3.1 fusion.2
  257.7 4.2 fusion.111
  264.1 4.9 fusion.56
  271.8 10.1 %reduce-scatter.13.cloned.1.call-done = f32[512,384]{0,1:T(8,128)} async-done(((f32[2048,384]{0,1:T(8,128)}), f32[512,384]{0,1:T(8,128)}) %reduce-scatter.13.cloned.1.call-update) | async-done | bytes 786448 | tf_op jit(solution)/shard_map/reduce_scatter | solution.py:499
  283.8 3.3 fusion.75
  287.1 58.0 %reduce-scatter.15.cloned.1.call-done = f32[512,384]{0,1:T(8,128)} async-done(((f32[2048,384]{0,1:T(8,128)}), f32[512,384]{0,1:T(8,128)}) %reduce-scatter.15.cloned.1.call-update) | async-done | bytes 786448 | tf_op jit(solution)/shard_map/reduce_scatter | solution.py:499
  346.3 3.4 fusion.74
  358.1 2.9 fusion.67
  369.6 99.8 %all-reduce.9.cloned.1.call-done = (f32[512,768]{1,0:T(8,128)}, f32[512,768]{1,0:T(8,128)}, f32[512,768]{1,0:T(8,128)}, f32[512,768]{1,0:T(8,128)}) async-done(((f32[512,768]{1,0:T(8,128)}, f32[512,768]{1,0:T(8,128)}, f32[512,768]{1,0:T(8,128)}, f32[512,768]{1,0:T(8,128)}), (f32[512,768]{1,0:T(8,128)}, f32[512,768]{1,0:T(8,128)}, f32[512,768]{1,0:T(8,128)}, ...) | async-done | bytes 6291472 | tf_op jit(solution)/shard_map/psum | solution.py:470
  469.4 4.8 fusion.38
  476.3 11.3 %reduce-scatter.19.cloned.1.call-done = f32[192,384]{1,0:T(8,128)} async-done(((f32[192,768]{1,0:T(8,128)}), f32[192,384]{1,0:T(8,128)}) %reduce-scatter.19.cloned.1.call-update) | async-done | bytes 294928 | tf_op jit(solution)/shard_map/reduce_scatter | solution.py:518
  487.7 37.5 %reduce-scatter.21.cloned.1.call-done = f32[384,768]{1,0:T(8,128)} async-done(((f32[768,768]{1,0:T(8,128)}), f32[384,768]{1,0:T(8,128)}) %reduce-scatter.21.cloned.1.call-update) | async-done | bytes 1179664 | tf_op jit(solution)/shard_map/reduce_scatter | solution.py:518
  525.1 37.1 %reduce-scatter.23.cloned.1.call-done = f32[768,384]{1,0:T(8,128)} async-done(((f32[768,768]{1,0:T(8,128)}), f32[768,384]{1,0:T(8,128)}) %reduce-scatter.23.cloned.1.call-update) | async-done | bytes 1179664 | tf_op jit(solution)/shard_map/reduce_scatter | solution.py:518
  562.2 30.6 %reduce-scatter.17.cloned.1.call-done = f32[3,384,192]{1,2,0:T(8,128)} async-done(((f32[3,768,192]{1,2,0:T(8,128)}), f32[3,384,192]{1,2,0:T(8,128)}) %reduce-scatter.17.cloned.1.call-update) | async-done | bytes 884752 | tf_op jit(solution)/shard_map/reduce_scatter | solution.py:518
  600.2 8.1 %reduce-scatter.27.cloned.1.call-done = f32[384,2]{1,0:T(8,128)} async-done(((f32[768,2]{1,0:T(8,128)}), f32[384,2]{1,0:T(8,128)}) %reduce-scatter.27.cloned.1.call-update) | async-done | bytes 3088
  609.3 14.3 %reduce-scatter.25.cloned.1.call-done = f32[384,2]{1,0:T(8,128)} async-done(((f32[768,2]{1,0:T(8,128)}), f32[384,2]{1,0:T(8,128)}) %reduce-scatter.25.cloned.1.call-update) | async-done | bytes 3088
  624.6 12.7 %all-reduce.3 = (f32[2,384]{1,0:T(2,128)}, f32[2,384]{1,0:T(2,128)}) all-reduce(f32[2,384]{1,0:T(2,128)S(1)} %copy.57, f32[2,384]{1,0:T(2,128)S(1)} %copy.59), channel_id=1, replica_groups=mesh['dp'=2,'ctx'=4,'tp'=4] {'ctx'}, use_global_device_ids=true, to_apply=%region_38.39 | all-reduce | flops 1536 | bytes 12288 | tf_op jit(solution)/shard_map/psum | solution.py:515
  637.3 122.9 %all-reduce.13.cloned.1.call-done = (f32[3,384,192]{1,2,0:T(8,128)}, f32[192,384]{1,0:T(8,128)}, f32[384,768]{1,0:T(8,128)}, f32[768,384]{1,0:T(8,128)}) async-done(((f32[3,384,192]{1,2,0:T(8,128)}, f32[192,384]{1,0:T(8,128)}, f32[384,768]{1,0:T(8,128)}, f32[768,384]{1,0:T(8,128)}), (f32[3,384,192]{1,2,0:T(8,128)}, f32[192,384]{1,0:T(8,128)}, f32[384,768]{1,0:T(8,128)}, ...) | async-done | bytes 3538960 | tf_op jit(solution)/shard_map/psum | solution.py:515
  (311 shorter events, 101.8 us)
Async XLA Ops:
  7.2 181.9 %all-reduce.11.cloned.1.call-start = ((), (), s32[]{:S(2)}) async-start(), calls=%async_computation.17 | async-start | bytes 6291456 | tf_op jit(solution)/shard_map/psum | solution.py:477
  12.3 95.1 %copy-start.2 = (bf16[2,1,512,768]{3,2,1,0:T(8,128)(2,1)S(1)}, bf16[2,1,512,768]{3,2,1,0:T(8,128)(2,1)}, u32[]{:S(2)}) copy-start(bf16[2,1,512,768]{3,2,1,0:T(8,128)(2,1)} %param.12) | copy-start | bytes 4718596
  109.6 8.4 %copy-start.44 = (f32[512]{0:T(512)}, f32[512]{0:T(512)S(1)}, u32[]{:S(2)}) copy-start(f32[512]{0:T(512)S(1)} %get-tuple-element.157) | copy-start | bytes 6148
  111.6 8.0 %copy-start.31 = (bf16[768,384]{1,0:T(8,128)(2,1)}, bf16[768,384]{1,0:T(8,128)(2,1)S(1)}, u32[]{:S(2)}) copy-start(bf16[768,384]{1,0:T(8,128)(2,1)S(1)} %get-tuple-element.128) | copy-start | bytes 1769476
  111.6 8.0 %copy-start.33 = (bf16[768,384]{1,0:T(8,128)(2,1)}, bf16[768,384]{1,0:T(8,128)(2,1)S(1)}, u32[]{:S(2)}) copy-start(bf16[768,384]{1,0:T(8,128)(2,1)S(1)} %get-tuple-element.129) | copy-start | bytes 1769476
  112.2 5.7 copy-start.41
  112.2 5.7 copy-start.64
  124.1 157.7 %reduce-scatter.13.cloned.1.call-start = ((), (), s32[]{:S(2)}) async-start(), calls=%async_computation.8 | async-start | bytes 3932160 | tf_op jit(solution)/shard_map/reduce_scatter | solution.py:499
  139.1 5.3 copy-start.72
  146.7 5.8 copy-start.13
  189.1 4.5 copy-start.53
  189.1 4.5 copy-start.56
  189.1 4.5 copy-start.63
  189.1 8.1 %copy-start.20 = (bf16[256,384]{1,0:T(8,128)(2,1)S(1)}, bf16[256,384]{1,0:T(8,128)(2,1)}, u32[]{:S(2)}) copy-start(bf16[256,384]{1,0:T(8,128)(2,1)} %get-tuple-element.136) | copy-start | bytes 589828
  193.6 5.7 copy-start
  221.2 123.9 %reduce-scatter.15.cloned.1.call-start = ((), (), s32[]{:S(2)}) async-start(), calls=%async_computation.9 | async-start | bytes 3932160 | tf_op jit(solution)/shard_map/reduce_scatter | solution.py:499
  257.2 212.2 %all-reduce.9.cloned.1.call-start = ((), (), s32[]{:S(2)}) async-start(), calls=%async_computation.16 | async-start | bytes 12582912 | tf_op jit(solution)/shard_map/psum | solution.py:470
  257.7 11.3 %slice-start = ((s8[6291456]{0:T(1024)(128)(4,1)}), s8[4194304]{0:T(1024)(128)(4,1)S(1)}, s32[]{:S(2)}) async-start(s8[6291456]{0:T(1024)(128)(4,1)} %bitcast.271), calls=%async_computation.19 | async-start | bytes 8388608
  261.9 7.2 slice-start.1
  264.1 4.9 copy-start.15
  269.1 14.0 %copy-start.39 = (bf16[3,64,512]{2,1,0:T(8,128)(2,1)}, bf16[3,64,512]{2,1,0:T(8,128)(2,1)S(1)}, u32[]{:S(2)}) copy-start(bf16[3,64,512]{2,1,0:T(8,128)(2,1)S(1)} %fusion.56) | copy-start | bytes 589828
  269.1 14.7 %copy-start.60 = (bf16[640]{0:T(1024)(128)(2,1)S(1)}, bf16[640]{0:T(1024)(128)(2,1)}, u32[]{:S(2)}) copy-start(bf16[640]{0:T(1024)(128)(2,1)} %copy-done.59) | copy-start | bytes 3844
  349.7 137.9 %reduce-scatter.19.cloned.1.call-start = ((), (), s32[]{:S(2)}) async-start(), calls=%async_computation.11 | async-start | bytes 884736 | tf_op jit(solution)/shard_map/reduce_scatter | solution.py:518
  353.2 171.9 %reduce-scatter.21.cloned.1.call-start = ((), (), s32[]{:S(2)}) async-start(), calls=%async_computation.12 | async-start | bytes 3538944 | tf_op jit(solution)/shard_map/reduce_scatter | solution.py:518
  358.0 204.2 %reduce-scatter.23.cloned.1.call-start = ((), (), s32[]{:S(2)}) async-start(), calls=%async_computation.13 | async-start | bytes 3538944 | tf_op jit(solution)/shard_map/reduce_scatter | solution.py:518
  363.7 229.1 %reduce-scatter.17.cloned.1.call-start = ((), (), s32[]{:S(2)}) async-start(), calls=%async_computation.10 | async-start | bytes 2654208 | tf_op jit(solution)/shard_map/reduce_scatter | solution.py:518
  368.8 100.6 %copy-start.48 = (f32[768]{0:T(1024)S(1)}, f32[768]{0:T(1024)}, u32[]{:S(2)}) copy-start(f32[768]{0:T(1024)} %get-tuple-element.94) | copy-start | bytes 9220
  368.8 100.6 %copy-start.50 = (f32[512]{0:T(512)S(1)}, f32[512]{0:T(512)}, u32[]{:S(2)}) copy-start(f32[512]{0:T(512)} %copy-done.49) | copy-start | bytes 6148
  368.8 100.5 %copy-start.51 = (f32[512]{0:T(512)S(1)}, f32[512]{0:T(512)}, u32[]{:S(2)}) copy-start(f32[512]{0:T(512)} %broadcast_multiply_fusion.7) | copy-start | bytes 6148
  368.9 239.4 %reduce-scatter.27.cloned.1.call-start = ((), (), s32[]{:S(2)}) async-start(), calls=%async_computation.15 | async-start | bytes 589824
  475.2 148.4 %reduce-scatter.25.cloned.1.call-start = ((), (), s32[]{:S(2)}) async-start(), calls=%async_computation.14 | async-start | bytes 589824
  476.3 284.0 %all-reduce.13.cloned.1.call-start = ((), (), s32[]{:S(2)}) async-start(), calls=%async_computation.18 | async-start | bytes 7077888 | tf_op jit(solution)/shard_map/psum | solution.py:515
  (72 other events, 162.2 us)
Sparse Core Ops, SparseCore 0:
  124.2 64.8 all-reduce.10
  221.3 60.4 reduce-scatter.12
  284.7 60.2 reduce-scatter.14
  349.8 119.5 all-reduce.8
  472.1 15.5 reduce-scatter.18
  490.3 34.7 reduce-scatter.20
  527.4 34.7 reduce-scatter.22
  564.5 28.2 reduce-scatter.16
  595.0 13.1 reduce-scatter.26
  610.4 13.1 reduce-scatter.24
  626.3 133.9 all-reduce.12

commit v2 on v1

--- a/solution.py
+++ b/solution.py
@@ -393,20 +393,6 @@
     return out if exchange else list(out) + list(weights)
 
 
-def apply_layer_norm(values, norm_gain, norm_shift):
-    normalized, inv = normalize(values)
-    return (normalized * norm_gain + norm_shift, normalized, inv)
-
-
-def norm_backward(normed_gradient, normalized_input, inverse_deviation, norm_gain):
-    scaled_gradient = normed_gradient * norm_gain
-    return inverse_deviation * (
-        scaled_gradient
-        - jnp.mean(scaled_gradient, axis=1, keepdims=True)
-        - normalized_input * jnp.mean(scaled_gradient * normalized_input, axis=1, keepdims=True)
-    )
-
-
 def pack_weights(qkv_weight, out_weight, up_weight, down_weight, ln_gains, ln_shifts, exchange):
     q, k, v = qkv_weight[0], qkv_weight[1], qkv_weight[2]
     pad = jnp.zeros((q.shape[0], 64), BF16)
@@ -425,8 +411,512 @@
     ]
 
 
-def side_by_side(stack):
-    return jnp.concatenate([stack[i] for i in range(stack.shape[0])], axis=-1)
+def wide(ref_stack, fn):
+    return jnp.concatenate([fn(ref_stack[i]) for i in range(ref_stack.shape[0])], axis=1)
+
+
+def narrow(ref_stack, value):
+    size = ref_stack.shape[2]
+    total = dot_nt(value[:, 0:size], ref_stack[0])
+    for i in range(1, ref_stack.shape[0]):
+        total += dot_nt(value[:, i * size : (i + 1) * size], ref_stack[i])
+    return total
+
+
+def norm_back(dn, xhat, inv, gain):
+    e = dn * gain
+    return inv * (
+        e - jnp.mean(e, axis=1, keepdims=True) - xhat * jnp.mean(e * xhat, axis=1, keepdims=True)
+    )
+
+
+def ln_row(ln, row):
+    return jnp.concatenate([ln[i, row : row + 1, :] for i in range(ln.shape[0])], axis=1)
+
+
+def column_sums(value):
+    return jnp.sum(value, axis=0, keepdims=True)
+
+
+def mlp_kernel(
+    n_ctx, n_dp, hid, attn, cot, heads, wu, wd, ln, d_mid, d_attn, mlp, grads, stats,
+    act, d_mlp, d_up, h2, total, *tp_refs
+):
+    p = Place(n_ctx)
+    micro, rows, width = hid.shape
+    half = rows // 2
+    p.barrier(False, True, False)
+    gain, shift = ln_row(ln, 1), ln_row(ln, 3)
+    sums = [tp_set(p, half, tp_refs, m, total.at[m]) for m in range(micro)]
+    ff = wu.shape[1]
+    part = width // n_dp
+
+    def middle(m, span):
+        return hid[m, span, :].astype(F32) + BRANCH * attn[m, span, :].astype(F32)
+
+    for m in range(micro):
+        @pl.loop(0, rows // 128)
+        def _(i, m=m):
+            span = pl.ds(pl.multiple_of(i * 128, 128), 128)
+            flat = pl.ds(pl.multiple_of(m * rows + i * 128, 128), 128)
+            xhat, _ = normalize(middle(m, span))
+            normed = (xhat * gain + shift).astype(BF16)
+            h2[flat, :] = normed
+            up = dot_nn(normed, wu[...])
+            active = gelu_value(up).astype(BF16)
+            act[flat, :] = active
+            down_grad = (BRANCH * cot[m, span, :].astype(F32)).astype(BF16)
+            d_mlp[flat, :] = down_grad
+            d_up[flat, :] = (narrow(wd, down_grad) * gelu_slope(up)).astype(BF16)
+            mlp[m, span, :] = wide(wd, lambda w: dot_nn(active, w)).astype(BF16)
+            if m == 1:
+                pl.when(i == 1)(sums[0].step2)
+
+        sums[m].start(
+            lambda span, m=m: dot_nt(d_up[pl.ds(m * rows + span.start, half), :], wu[...])
+        )
+    parts = grads.shape[0]
+    cols = grads.shape[2]
+
+    @pl.loop(0, ff // 256)
+    def _(i):
+        left = act[:, pl.ds(pl.multiple_of(i * 256, 256), 256)]
+        to = pl.ds(pl.multiple_of(i * 256, 256), 256)
+        for k in range(parts):
+            grads[k, to, :] = dot_tn(left, d_mlp[:, k * cols : (k + 1) * cols]).astype(BF16)
+
+    sums[1].step2()
+    own_rows = width // parts
+    for k in range(parts):
+        @pl.loop(0, own_rows // 128)
+        def _(i, k=k):
+            left = h2[:, pl.ds(pl.multiple_of(k * own_rows + i * 128, 128), 128)]
+            block = dot_tn(left, d_up[...]).astype(BF16)
+            for q in range(ff // cols):
+                to = pl.ds(pl.multiple_of(ff + q * own_rows + i * 128, 128), 128)
+                grads[k, to, :] = block[:, q * cols : (q + 1) * cols]
+
+    stats[...] = jnp.zeros(stats.shape, F32)
+    for m in range(micro):
+        if m == 0:
+            sums[0].step3()
+            sums[0].finish()
+            sums[1].step3()
+        else:
+            sums[1].finish()
+
+        @pl.loop(0, rows // 128)
+        def _(i, m=m):
+            span = pl.ds(pl.multiple_of(i * 128, 128), 128)
+            flat = pl.ds(pl.multiple_of(m * rows + i * 128, 128), 128)
+            xhat, inv = normalize(middle(m, span))
+            dn = total[m, span, :].astype(F32)
+            grad = cot[m, span, :].astype(F32) + norm_back(dn, xhat, inv, gain)
+            d_mid[m, span, :] = grad
+            d_attn[flat, :] = (BRANCH * grad).astype(BF16)
+            stats[0:1, :] += column_sums(dn * xhat)
+            stats[1:2, :] += column_sums(dn)
+
+    at = ff + own_rows * (ff // cols)
+    for k in range(parts):
+        grads[k, at : at + 256, :] = dot_tn(
+            heads[...], d_attn[:, k * cols : (k + 1) * cols]
+        ).astype(BF16)
+    for m in range(micro):
+        sums[m].drain()
+
+
+def run_mlp(n_ctx, exchange, hid, attn, cot, heads, wu, wd, ln):
+    micro, rows, width = hid.shape
+    ff = wu.shape[1]
+    parts = 2 if exchange else 1
+    sds = jax.ShapeDtypeStruct
+    cols = width // parts
+    grad_rows = ff + (width // parts) * (ff // cols) + 256
+    outs = [
+        sds((micro, rows, width), F32),
+        sds((micro * rows, width), BF16),
+        sds((micro, rows, width), BF16),
+        sds((parts, grad_rows, cols), BF16),
+        sds((8, width), F32),
+    ]
+    scratch = [pltpu.VMEM((micro * rows, w), BF16) for w in (ff, width, ff, width)]
+    scratch += [pltpu.VMEM((micro, rows, width), BF16)] + tp_scratch(micro, rows // 2, width)
+    return pl.pallas_call(
+        functools.partial(mlp_kernel, n_ctx, parts),
+        out_shape=outs,
+        in_specs=vmem_specs(7),
+        out_specs=vmem_specs(len(outs)),
+        scratch_shapes=scratch,
+        compiler_params=pltpu.CompilerParams(
+            collective_id=1, has_side_effects=True, vmem_limit_bytes=VMEM_LIMIT
+        ),
+        name="mlp_both_ways",
+    )(hid, attn, cot, heads.reshape(micro * rows, 256), wu, wd, ln)
+
+
+class GradSum:
+    def __init__(self, place, peer, own, from_dp, up, from_up, from_mid, out, send, recv):
+        self.p = place
+        self.peer, self.own, self.from_dp, self.up = peer, own, from_dp, up
+        self.from_up, self.from_mid, self.out = from_up, from_mid, out
+        self.send, self.recv = send, recv
+        c, n = place.c, place.n
+        low = c < n // 2
+        self.toward = jnp.where(low, c + 1, c - 1)
+        self.away = jnp.where(low, c - 1, c + 1)
+        self.end = jnp.logical_or(c == 0, c == n - 1)
+        self.inner = jnp.logical_or(c == n // 2 - 1, c == n // 2)
+
+    def dp_copy(self):
+        return remote(self.peer, self.from_dp, self.send.at[0], self.recv.at[0], dp=1 - self.p.d)
+
+    def up_copy(self):
+        return remote(self.up, self.from_up, self.send.at[1], self.recv.at[1], ctx=self.toward)
+
+    def mid_copy(self):
+        return remote(self.up, self.from_mid, self.send.at[2], self.recv.at[2], ctx=self.toward)
+
+    def down_copy(self):
+        return remote(self.out, self.out, self.send.at[3], self.recv.at[3], ctx=self.away)
+
+    def s0(self):
+        self.dp_copy().start()
+
+    def s1(self):
+        self.dp_copy().wait_recv()
+
+        @pl.when(self.end)
+        def _():
+            self.up[...] = (self.own[...].astype(F32) + self.from_dp[...].astype(F32)).astype(BF16)
+
+        @pl.when(jnp.logical_not(self.end))
+        def _():
+            self.up_copy().wait_recv()
+            self.up[...] = (
+                self.own[...].astype(F32) + self.from_dp[...].astype(F32)
+                + self.from_up[...].astype(F32)
+            ).astype(BF16)
+
+        pl.when(self.inner)(lambda: self.mid_copy().start())
+        pl.when(jnp.logical_not(self.inner))(lambda: self.up_copy().start())
+
+    def s2(self):
+        @pl.when(self.inner)
+        def _():
+            self.mid_copy().wait_recv()
+            self.out[...] = (self.up[...].astype(F32) + self.from_mid[...].astype(F32)).astype(BF16)
+            pl.when(jnp.logical_not(self.end))(lambda: self.down_copy().start())
+
+    def s3(self):
+        @pl.when(jnp.logical_not(self.inner))
+        def _():
+            self.down_copy().wait_recv()
+            pl.when(jnp.logical_not(self.end))(lambda: self.down_copy().start())
+
+    def drain(self):
+        self.dp_copy().wait_send()
+        pl.when(self.inner)(lambda: self.mid_copy().wait_send())
+        pl.when(jnp.logical_not(self.inner))(lambda: self.up_copy().wait_send())
+        pl.when(jnp.logical_not(self.end))(lambda: self.down_copy().wait_send())
+
+
+PIECES = 4
+
+
+def backward_kernel(n_ctx, exchange, *refs):
+    (prefix, border, hid, attn, d_mid, d_attn, mlp, h1, qs, kv, o_t, lse, wo, wp, ln, grads, stats1) = refs[:17]
+    refs = refs[17:]
+    if exchange:
+        (block, grad_in, ga, gb, gs) = refs[:5]
+        refs = refs[5:]
+    else:
+        (block, grad_in, gb, gs) = refs[:4]
+        refs = refs[4:]
+    (sbuf, rbuf, acc, qh, doh, dq_t, delta, d_pack, total, stats0, kvs, kvr) = refs[:12]
+    tp_refs = refs[12:19]
+    refs = refs[19:]
+    p = Place(n_ctx)
+    c, n = p.c, n_ctx
+    micro, rows, width = hid.shape
+    half = rows // 2
+    p.barrier(exchange, True, True)
+    pieces, pack_sum, stat_sum = [], None, None
+    if exchange:
+        (g_dp, g_up, g_fu, g_fm, b_buf, b_dp, b_up, b_fu, b_fm, s_buf, s_dp, s_up, s_fu, s_fm, gsend, grecv) = refs
+        count = ga.shape[0] // PIECES
+        for i in range(PIECES):
+            cut = pl.ds(i * count, count)
+            pieces.append(GradSum(
+                p, grads.at[1 - p.d, cut], grads.at[p.d, cut], g_dp.at[cut], g_up.at[cut],
+                g_fu.at[cut], g_fm.at[cut], ga.at[cut], gsend.at[i], grecv.at[i],
+            ))
+        pack_sum = GradSum(
+            p, b_buf.at[1 - p.d], b_buf.at[p.d], b_dp, b_up, b_fu, b_fm, gb,
+            gsend.at[PIECES], grecv.at[PIECES],
+        )
+        stat_sum = GradSum(
+            p, s_buf.at[1 - p.d], s_buf.at[p.d], s_dp, s_up, s_fu, s_fm, gs,
+            gsend.at[PIECES + 1], grecv.at[PIECES + 1],
+        )
+        for piece in pieces:
+            piece.s0()
+    mlp_sums = [tp_set(p, half, tp_refs, m, block.at[m]) for m in range(micro)]
+    n1_sums = [tp_set(p, half, tp_refs, micro + m, total.at[m]) for m in range(micro)]
+    for m in range(micro):
+        mlp_sums[m].start(lambda span, m=m: mlp[m, span, :].astype(F32))
+
+    def kv_copy(m, way, j):
+        slot = j + 1 - way
+        to = c + 1 if way == 0 else c - 1
+        return remote(sbuf.at[m, j], rbuf.at[m, slot], kvs.at[m, way, j], kvr.at[m, way, j], ctx=to)
+
+    def kv_landed(m, way, j):
+        slot = j + 1 - way
+        to = c - 1 if way == 0 else c + 1
+        return remote(sbuf.at[m, j], rbuf.at[m, slot], kvs.at[m, way, j], kvr.at[m, way, j], ctx=to)
+
+    def upstream(way):
+        return c > 0 if way == 0 else c < n - 1
+
+    def attend_back(m, j, limits):
+        for b in range(2):
+            span = pl.ds(b * half, half)
+            k01 = kv[m, j, span, 0:128]
+            k2v0 = kv[m, j, span, 128:256]
+            v12 = kv[m, j, span, 256:384]
+            t01 = k01.T
+            t2 = k2v0.T
+            allowed = key_positions(border, 2 * j + b, half) <= limits
+            sums = {}
+            for h in range(3):
+                scores = dot_nt(k2v0 if h == 2 else k01, qh[h])
+                prob = jnp.exp(jnp.where(allowed, scores, NEG) - lse[m, h : h + 1, :])
+                d_prob = dot_nt(k2v0 if h == 0 else v12, doh[h])
+                d_scores = (prob * (d_prob - delta[h])).astype(BF16)
+                dk = dot_nn(d_scores, qh[h])
+                dv = dot_nn(prob.astype(BF16), doh[h])
+                k_at, v_at = (1 if h == 2 else 0), (1 if h == 0 else 2)
+                sums[k_at] = dk if k_at not in sums else sums[k_at] + dk
+                sums[v_at] = dv if v_at not in sums else sums[v_at] + dv
+                k_t = t2[0:64] if h == 2 else t01[h * 64 : (h + 1) * 64]
+                dq_t[h * 64 : (h + 1) * 64, :] += dot_nn(k_t, d_scores)
+            for k in range(3):
+                acc[span, k * 128 : (k + 1) * 128] = sums[k]
+
+    lanes = lax.broadcasted_iota(jnp.int32, (rows, 128), 1)
+
+    def halves(value):
+        zero = jnp.zeros_like(value)
+        return jnp.where(lanes < 64, value, zero), jnp.where(lanes < 64, zero, value)
+
+    def write_block(m):
+        @pl.loop(0, rows // 128)
+        def _(i):
+            span = pl.ds(pl.multiple_of(i * 128, 128), 128)
+            mid = hid[m, span, :].astype(F32) + BRANCH * attn[m, span, :].astype(F32)
+            block[m, span, :] = (mid + BRANCH * block[m, span, :].astype(F32)).astype(BF16)
+
+    def side_work(m, t):
+        jobs = {}
+        if m == 0:
+            jobs[0] = [s.step2 for s in mlp_sums]
+            jobs[4] = [s.step3 for s in mlp_sums]
+            if exchange:
+                jobs[2] = [pieces[0].s1, pieces[1].s1]
+                jobs[5] = [pieces[2].s1, pieces[3].s1]
+                jobs[6] = [pieces[0].s2, pieces[1].s2]
+        else:
+            jobs[0] = [n1_sums[0].step2]
+            jobs[4] = [n1_sums[0].step3]
+            if exchange:
+                jobs[1] = [pieces[2].s2, pieces[3].s2]
+                jobs[5] = [piece.s3 for piece in pieces]
+        for at, work in jobs.items():
+            @pl.when(t == min(at, 2 * n - 2))
+            def _(work=work):
+                for job in work:
+                    job()
+
+    for m in range(micro):
+        flat = pl.ds(m * rows, rows)
+        limits = query_limits(border, prefix, m, c, rows)
+        upper = d_attn[flat, :]
+        d_heads = narrow(wo, upper).astype(BF16)
+        doh[0] = d_heads[:, 128:256]
+        doh[1], doh[2] = halves(d_heads[:, 0:128])
+        size = wo.shape[2]
+        d_heads_t = dot_nt(wo[0], upper[:, 0:size])
+        for i in range(1, wo.shape[0]):
+            d_heads_t += dot_nt(wo[i], upper[:, i * size : (i + 1) * size])
+        for h in range(3):
+            at = 192 if h == 0 else (h - 1) * 64
+            delta[h] = jnp.sum(d_heads_t[at : at + 64] * o_t[m, h], axis=0, keepdims=True)
+        qh[0], qh[1] = halves(qs[m, :, 0:128])
+        qh[2] = qs[m, :, 128:256]
+        dq_t[...] = jnp.zeros(dq_t.shape, F32)
+
+        @pl.loop(0, 2 * n - 1)
+        def _(t, m=m, limits=limits):
+            s = n - 1 - lax.div(t, 2)
+            own = t == 2 * n - 2
+            right = jnp.logical_and(lax.rem(t, 2) == 0, jnp.logical_not(own))
+            j = jnp.where(right, c + s, c - s)
+
+            @pl.when(jnp.logical_and(j >= 0, j < n))
+            def _():
+                attend_back(m, j, limits)
+
+                def pass_on(way):
+                    @pl.when(upstream(way))
+                    def _():
+                        kv_landed(m, way, j).wait_recv()
+                        sbuf[m, j] = (acc[...] + rbuf[m, j + 1 - way].astype(F32)).astype(BF16)
+
+                    @pl.when(jnp.logical_not(upstream(way)))
+                    def _():
+                        sbuf[m, j] = acc[...].astype(BF16)
+
+                    kv_copy(m, way, j).start()
+
+                pl.when(right)(lambda: pass_on(0))
+                pl.when(jnp.logical_and(jnp.logical_not(right), jnp.logical_not(own)))(
+                    lambda: pass_on(1)
+                )
+
+            side_work(m, t)
+
+        @pl.when(upstream(0))
+        def _():
+            kv_landed(m, 0, c).wait_recv()
+            acc[...] += rbuf[m, c + 1].astype(F32)
+
+        @pl.when(upstream(1))
+        def _():
+            kv_landed(m, 1, c).wait_recv()
+            acc[...] += rbuf[m, c].astype(F32)
+
+        d_pack[flat, 256:640] = acc[...].astype(BF16)
+        d_pack[flat, 0:256] = (dq_t[...].T * HEAD_DIM ** (-0.5)).astype(BF16)
+        n1_sums[m].start(
+            lambda span, m=m: dot_nt(d_pack[pl.ds(m * rows + span.start, half), :], wp[...])
+        )
+        if m == 0:
+            for k in range(micro):
+                mlp_sums[k].finish()
+                mlp_sums[k].drain()
+                write_block(k)
+
+    parts = 2 if exchange else 1
+    own_rows = width // parts
+
+    def pack_part(k, to):
+        @pl.loop(0, own_rows // 128)
+        def _(i):
+            left = h1[:, pl.ds(pl.multiple_of(k * own_rows + i * 128, 128), 128)]
+            span = pl.ds(pl.multiple_of(i * 128, 128), 128)
+            to[span, :] = dot_tn(left, d_pack[...]).astype(to.dtype)
+
+    def finish_rows(m):
+        gain = ln_row(ln, 0)
+
+        @pl.loop(0, rows // 128)
+        def _(i):
+            span = pl.ds(pl.multiple_of(i * 128, 128), 128)
+            xhat, inv = normalize(hid[m, span, :].astype(F32))
+            dn = total[m, span, :].astype(F32)
+            grad_in[m, span, :] = d_mid[m, span, :] + norm_back(dn, xhat, inv, gain)
+            stats0[0:1, :] += column_sums(dn * xhat)
+            stats0[1:2, :] += column_sums(dn)
+
+    stats0[...] = jnp.zeros(stats0.shape, F32)
+    if exchange:
+        pack_part(1 - p.d, b_buf.at[1 - p.d])
+        pack_sum.s0()
+        n1_sums[1].step2()
+        pack_part(p.d, b_buf.at[p.d])
+        n1_sums[0].finish()
+        finish_rows(0)
+        pack_sum.s1()
+        n1_sums[1].step3()
+        pack_sum.s2()
+        n1_sums[1].finish()
+        finish_rows(1)
+        for k in range(2):
+            cut = slice(k * own_rows, (k + 1) * own_rows)
+            s_buf[k] = jnp.concatenate(
+                [stats0[0:1, cut], stats1[0:1, cut], stats0[1:2, cut], stats1[1:2, cut],
+                 jnp.zeros((12, own_rows), F32)], axis=0,
+            ).astype(BF16)
+        stat_sum.s0()
+        stat_sum.s1()
+        pack_sum.s3()
+        stat_sum.s2()
+        stat_sum.s3()
+        for piece in pieces + [pack_sum, stat_sum]:
+            piece.drain()
+    else:
+        pack_part(0, gb)
+        n1_sums[1].step2()
+        n1_sums[0].finish()
+        finish_rows(0)
+        n1_sums[1].step3()
+        n1_sums[1].finish()
+        finish_rows(1)
+        gs[...] = jnp.concatenate(
+            [stats0[0:1, :], stats1[0:1, :], stats0[1:2, :], stats1[1:2, :],
+             jnp.zeros((4, width), F32)], axis=0,
+        )
+    for m in range(micro):
+        for j in range(n):
+            pl.when(c < j)(lambda m=m, j=j: kv_copy(m, 0, j).wait_send())
+            pl.when(c > j)(lambda m=m, j=j: kv_copy(m, 1, j).wait_send())
+        n1_sums[m].drain()
+
+
+def run_backward(n_ctx, exchange, prefix, border, tensors):
+    (hid, attn, d_mid, d_attn, mlp, h1, qs, kv, o_t, lse, wo, wp, ln, grads, stats) = tensors
+    micro, rows, width = hid.shape
+    own_rows = width // 2
+    sds = jax.ShapeDtypeStruct
+    outs = [sds((micro, rows, width), BF16), sds((micro, rows, width), F32)]
+    if exchange:
+        outs += [
+            sds(grads.shape[1:], BF16), sds((own_rows, 640), BF16), sds((16, own_rows), BF16)
+        ]
+    else:
+        outs += [sds((width, 640), F32), sds((8, width), F32)]
+    scratch = [
+        pltpu.VMEM((micro, n_ctx, rows, 384), BF16),
+        pltpu.VMEM((micro, n_ctx + 1, rows, 384), BF16),
+        pltpu.VMEM((rows, 384), F32),
+        pltpu.VMEM((3, rows, 128), BF16),
+        pltpu.VMEM((3, rows, 128), BF16),
+        pltpu.VMEM((256, rows), F32),
+        pltpu.VMEM((3, 1, rows), F32),
+        pltpu.VMEM((micro * rows, 640), BF16),
+        pltpu.VMEM((micro, rows, width), BF16),
+        pltpu.VMEM((8, width), F32),
+        pltpu.SemaphoreType.DMA((micro, 2, n_ctx)),
+        pltpu.SemaphoreType.DMA((micro, 2, n_ctx)),
+    ] + tp_scratch(2 * micro, rows // 2, width)
+    if exchange:
+        scratch += [pltpu.VMEM(grads.shape[1:], BF16)] * 4
+        scratch += [pltpu.VMEM((2, own_rows, 640), BF16)] + [pltpu.VMEM((own_rows, 640), BF16)] * 4
+        scratch += [pltpu.VMEM((2, 16, own_rows), BF16)] + [pltpu.VMEM((16, own_rows), BF16)] * 4
+        scratch += [pltpu.SemaphoreType.DMA((PIECES + 2, 4))] * 2
+    smem = pl.BlockSpec(memory_space=pltpu.SMEM)
+    return pl.pallas_call(
+        functools.partial(backward_kernel, n_ctx, exchange),
+        out_shape=outs,
+        in_specs=[smem, smem] + vmem_specs(len(tensors)),
+        out_specs=vmem_specs(len(outs)),
+        scratch_shapes=scratch,
+        compiler_params=pltpu.CompilerParams(
+            collective_id=2, has_side_effects=True, vmem_limit_bytes=67043328
+        ),
+        name="attention_backward",
+    )(prefix, border, *tensors)
 
 
 def body(
@@ -434,90 +924,54 @@
     ln_shifts, cotangent,
 ):
     micro, _, tokens, width = hidden_in.shape
-    local_width = qkv_weight.shape[2]
-    heads_n = local_width // HEAD_DIM
     n_ctx = lax.axis_size("ctx")
-    n_dp = lax.axis_size("dp")
-    exchange = n_dp == 2
-    seq_len = tokens * n_ctx
-    half = tokens // 2
-    scale = HEAD_DIM ** (-0.5)
+    exchange = lax.axis_size("dp") == 2 and n_ctx % 2 == 0
     weights = pack_weights(
         qkv_weight, out_weight, up_weight, down_weight, ln_gains, ln_shifts, exchange
     )
+    hid, cot = hidden_in[:, 0], cotangent[:, 0]
     (attn, heads, lse, o_t, qs, kv, h1, wp, wo, wu, wd, ln) = run_forward(
-        n_ctx, exchange, prefix, block_order, hidden_in[:, 0], weights
+        n_ctx, exchange, prefix, block_order, hid, weights
     )
-    out_full = side_by_side(wo)
-    down_full = side_by_side(wd)
-    ln_full = side_by_side(ln)
-    gains, shifts = ln_full[0:2], ln_full[2:4]
-
-    cuts = jnp.arange(seq_len, dtype=jnp.int32)
-    key_pos = jnp.repeat(block_order, half, total_repeat_length=seq_len) * half + cuts % half
-    query_pos = lax.dynamic_slice_in_dim(key_pos, lax.axis_index("ctx") * tokens, tokens)
-    acc = None
-    results, grads_in = [], []
-    for m in range(micro):
-        x = hidden_in[m, 0].astype(F32)
-        allowed = (key_pos[None, :] <= query_pos[:, None]) | (key_pos[None, :] < prefix[m, 0])
-        xhat1, inv1 = normalize(x)
-        mid = x + BRANCH * attn[m].astype(F32)
-        n2, xhat2, inv2 = apply_layer_norm(mid, gains[1], shifts[1])
-        h2 = n2.astype(BF16)
-        up = dot_nn(h2, wu)
-        act = gelu_value(up).astype(BF16)
-        mlp = lax.psum(dot_nn(act, down_full), "tp")
-        results.append((mid + BRANCH * mlp).astype(BF16))
-        g = cotangent[m, 0].astype(F32)
-        d_mlp = (BRANCH * g).astype(BF16)
-        grad_down = dot_tn(act, d_mlp)
-        d_up = (dot_nt(d_mlp, down_full) * gelu_slope(up)).astype(BF16)
-        grad_up = dot_tn(h2, d_up)
-        d_n2 = lax.psum(dot_nt(d_up, wu), "tp")
-        d_mid = g + norm_backward(d_n2, xhat2, inv2, gains[1])
-        d_attn = (BRANCH * d_mid).astype(BF16)
-        grad_out = dot_tn(heads[m], d_attn)
-        d_heads = dot_nt(d_attn, out_full).astype(BF16)
-        q = qs[m][:, :local_width].reshape(tokens, heads_n, HEAD_DIM)
-        flat = kv[m].reshape(seq_len, 2 * local_width)
-        keys = flat[:, :local_width].reshape(seq_len, heads_n, HEAD_DIM)
-        values = flat[:, local_width:].reshape(seq_len, heads_n, HEAD_DIM)
-        dh = jnp.concatenate([d_heads[:, 192:], d_heads[:, :128]], axis=1)
-        dh = dh.reshape(tokens, heads_n, HEAD_DIM)
-        scores = jnp.einsum("qhd,khd->hqk", q, keys, preferred_element_type=F32)
-        scores = jnp.where(allowed[None], scores, NEG)
-        prob = jnp.exp(scores - lse[m, :heads_n][:, :, None])
-        d_prob = jnp.einsum("qhd,khd->hqk", dh, values, preferred_element_type=F32)
-        d_scores = (prob * (d_prob - jnp.sum(prob * d_prob, axis=2, keepdims=True))).astype(BF16)
-        d_q = jnp.einsum("hqk,khd->qhd", d_scores, keys, preferred_element_type=F32) * scale
-        d_k = jnp.einsum("hqk,qhd->khd", d_scores, q, preferred_element_type=F32)
-        d_v = jnp.einsum("hqk,qhd->khd", prob.astype(BF16), dh, preferred_element_type=F32)
-        d_kv = jnp.concatenate(
-            [d_k.reshape(seq_len, local_width), d_v.reshape(seq_len, local_width)], axis=1
+    d_mid, d_attn, mlp, grads, stats = run_mlp(n_ctx, exchange, hid, attn, cot, heads, wu, wd, ln)
+    tensors = (
+        hid, attn, d_mid, d_attn, mlp, h1.reshape(micro * tokens, width), qs, kv, o_t, lse, wo, wp,
+        ln, grads, stats,
+    )
+    out = run_backward(n_ctx, exchange, prefix, block_order, tensors)
+    block, grad_in = out[:2]
+    ff = up_weight.shape[1]
+    if exchange:
+        ga, gb, gs = (v.astype(F32) for v in out[2:])
+        cols = ga.shape[1]
+        g_down = ga[:ff]
+        rest = ga[ff:]
+        own_rows = width // 2
+        g_up = jnp.concatenate(
+            [rest[k * own_rows : (k + 1) * own_rows] for k in range(ff // cols)], axis=1
         )
-        d_kv = lax.psum_scatter(d_kv, "ctx", scatter_dimension=0, tiled=True)
-        d_pack = jnp.concatenate(
-            [d_q.reshape(tokens, local_width), jnp.zeros((tokens, 64), F32), d_kv], axis=1
-        ).astype(BF16)
-        grad_pack = dot_tn(h1[m], d_pack)
-        d_n1 = lax.psum(dot_nt(d_pack, wp), "tp")
-        grads_in.append(d_mid + norm_backward(d_n1, xhat1, inv1, gains[0]))
-        new = (
-            grad_pack, grad_out, grad_up, grad_down,
-            jnp.stack([jnp.sum(d_n1 * xhat1, axis=0), jnp.sum(d_n2 * xhat2, axis=0)]),
-            jnp.stack([jnp.sum(d_n1, axis=0), jnp.sum(d_n2, axis=0)]),
+        g_out = rest[own_rows * (ff // cols) :]
+        owned = [
+            jnp.stack([gb[:, 0:192], gb[:, 256:448], gb[:, 448:640]]),
+            jnp.concatenate([g_out[192:], g_out[:128]], axis=0), g_up, g_down, gs[0:2], gs[2:4],
+        ]
+    else:
+        gb, gs = out[2:]
+        ga = grads[0].astype(F32)
+        g_out = ga[ff + width :]
+        g_up = ga[ff : ff + width]
+        whole = lax.psum(
+            (
+                jnp.stack([gb[:, 0:192], gb[:, 256:448], gb[:, 448:640]]),
+                jnp.concatenate([g_out[192:], g_out[:128]], axis=0), g_up, ga[:ff], gs[0:2], gs[2:4],
+            ),
+            "ctx",
         )
-        acc = new if acc is None else jax.tree.map(jnp.add, acc, new)
-    pack, g_out, g_up, g_down, g_gains, g_shifts = acc
-    g_qkv = jnp.stack([pack[:, 0:192], pack[:, 256:448], pack[:, 448:640]])
-    g_out = jnp.concatenate([g_out[192:], g_out[:128]], axis=0)
-    whole = lax.psum((g_qkv, g_out, g_up, g_down, g_gains, g_shifts), "ctx")
-    dims = (1, 1, 0, 1, 1, 1)
-    owned = [
-        lax.psum_scatter(v, "dp", scatter_dimension=d, tiled=True) for v, d in zip(whole, dims)
-    ]
-    return (jnp.stack(results)[:, None], jnp.stack(grads_in)[:, None], *owned)
+        owned = [
+            lax.psum_scatter(v, "dp", scatter_dimension=d, tiled=True)
+            for v, d in zip(whole, (1, 1, 0, 1, 1, 1))
+        ]
+    return (block[:, None], grad_in[:, None], *owned)
 
 
 def solution(mesh):

time: 778 us -> 315 us (0.40)
  waiting for transfers between devices: 460 us -> 0 us
  Pallas kernels: 95.1 us -> 293 us
  matrix products: 77.9 us -> 0 us
  other arithmetic: 59.6 us -> 5 us
  local copies, waits for them, and re-layouts: 50.1 us -> 15.3 us
  between operations: 15.4 us -> 0.75 us
  blocking collectives: 12.7 us -> 0 us
    psum x3 -> x0, waiting for transfers between devices: 253 us -> none  [the longest x1 123 us: body(): whole = lax.psum((g_qkv, g_out, g_up, g_down, g_gains, g_shifts), 'ctx')]
    pallas_call x0 -> x2, Pallas kernels: none -> 199 us  [the longest x1 161 us: run_backward(): pl.pallas_call(functools.partial(backward_kernel, n_ctx, exchange), out_s...]
    reduce_scatter x6 -> x0, waiting for transfers between devices: 185 us -> none  [the longest x4 116 us: body(): lax.psum_scatter(v, 'dp', scatter_dimension=d, tiled=True)]
    dot_general x30 -> x0, matrix products: 77.9 us -> none  [the longest x8 15.6 us: dot_tn(): lax.dot_general(a, b, (((0,), (0,)), ((), ())), preferred_element_type=F32)]
    unnamed x13 -> x0, waiting for transfers between devices: 22.6 us -> none
    slice x16 -> x5, local copies, waits for them, and re-layouts: 20.4 us -> 4.23 us  [the longest x1 1.35 us: body(): gs[2:4]]
    unnamed x194 -> x15, local copies, waits for them, and re-layouts: 23.3 us -> 7.98 us
    convert_element_type x2 -> x1, other arithmetic: 13.5 us -> 0.07 us  [body(): ga, gb, gs = (v.astype(F32) for v in out[2:])]
  transfers between devices with their start and end apart: 11 -> 0, of which waited for: 11 -> 0; matrix products, arithmetic and copies ran while one was open for 15% -> 0% of each run, Pallas kernels for 0% -> 0%
where the time goes in v2:
time: 315 us; the launch traced here: 314 us
  Pallas kernels  293 us (93%)
  local copies, waits for them, and re-layouts  15.3 us (5%)
  other arithmetic  5 us (2%)
    pallas_call x1, Pallas kernels, run_backward(): pl.pallas_call(functools.partial(backward_kernel, n_ctx, exchange), out_s...  161 us
    pallas_call x1, Pallas kernels, run_forward(): pl.pallas_call(functools.partial(forward_kernel, n_ctx, exchange), out_sh...  94.5 us
    pallas_call x1, Pallas kernels, run_mlp(): pl.pallas_call(functools.partial(mlp_kernel, n_ctx, parts), out_shape=out...  38.2 us
    unnamed x15, local copies, waits for them, and re-layouts  7.98 us

profile of v2, /device:TPU:0, one launch (start us, length us, event | category | flops | bytes accessed | tf_op | source)
XLA Modules:
  0.0 314.3 jit_solution(15692832584219671566)
XLA Ops:
  0.7 1.3 copy.22.prefix.refs_0_
  2.0 0.1 pad.21.clone
  2.0 1.3 fusion.3.refs_4_
  3.3 0.8 slice.56
  4.1 0.9 slice.55
  5.0 0.8 pad_maximum_fusion.4.refs_1_
  5.8 1.1 fusion.5
  6.9 0.1 copy.26
  7.1 0.1 copy.27
  7.2 0.1 copy.28
  7.4 0.9 pad_maximum_fusion.2.refs_0_
  8.3 94.5 %attention_forward.1 = (bf16[2,512,768]{2,1,0:T(8,128)(2,1)}, bf16[2,512,256]{2,1,0:T(8,128)(2,1)}, f32[2,8,512]{2,1,0:T(8,128)}, f32[2,3,64,512]{3,2,1,0:T(8,12...) custom-call(s32[2,1]{1,0:T(2,128)} %copy.22.prefix.refs_0_, ...), custom_call_target="tpu_custom_call" | custom-call | tf_op jit(solution)/shard_map/attention_forward/pallas_call | solution.py:382
  102.8 38.2 %mlp_both_ways.1 = (f32[2,512,768]{2,1,0:T(8,128)}, bf16[1024,768]{1,0:T(8,128)(2,1)}, bf16[2,512,768]{2,1,0:T(8,128)(2,1)}, bf16[2,1792,384]{2,1,0:T(8,128)(2,1)}, f32[8,768]{1,0:T(8,128)}) custom-call(bf16[2,512,768]{2,1,0:T(8,128)(2,1)} %bitcast.20, bf16[2,512,768]{2,1,0:T(8,128)(2,1)} %get-tuple-element.30.attn.refs_3_, bf16[2,512,768]{2,1,0:T(8,128)(2,1)} %bitcast.25, ...), custom_call_target="tpu_custom_call" | custom-call | tf_op jit(solution)/shard_map/mlp_both_ways/pallas_call | solution.py:545
  141.0 160.6 %attention_backward.1 = (bf16[2,512,768]{2,1,0:T(8,128)(2,1)}, f32[2,512,768]{2,1,0:T(8,128)}, bf16[1792,384]{1,0:T(8,128)(2,1)}, bf16[384,640]{1,0:T(8,128)(2,1)}, bf16[16,384]{1,0:T(8,128)(2,1)}) custom-call(s32[2,1]{1,0:T(2,128)} %copy.22.prefix.refs_0_, s32[8]{0:T(128)} %refs_1_.1, bf16[2,512,768]{2,1,0:T(8,128)(2,1)} %bitcast.21, ...), custom_call_target="tpu_custom_call" | custom-call | tf_op jit(solution)/shard_map/attention_backward/pallas_call | solution.py:909
  301.6 0.0 copy-start.3
  301.6 1.4 fusion.6
  303.0 0.8 slice.70
  303.8 0.9 slice.71
  304.7 0.7 pad_maximum_fusion.3
  305.4 0.1 convert_element_type.12
  305.5 0.2 slice_bitcast_fusion.2
  305.7 0.1 pad_maximum_fusion
  305.8 0.0 copy-start
  305.8 1.3 copy.25
  307.0 0.1 copy-done
  307.2 1.1 slice.74
  308.3 0.1 fusion.4
  308.4 1.1 pad_maximum_fusion.1
  309.4 0.7 copy-done.2
  310.2 1.1 copy.31
  311.3 1.3 copy-done.1
  312.6 1.7 copy.32
  (5 shorter events, 0.0 us)
Async XLA Ops:
  301.6 3.8 %copy-start.3 = (bf16[384,640]{1,0:T(8,128)(2,1)S(1)}, bf16[384,640]{1,0:T(8,128)(2,1)}, u32[]{:S(2)}) copy-start(bf16[384,640]{1,0:T(8,128)(2,1)} %get-tuple-element.49) | copy-start | bytes 1474564
  305.8 1.4 copy-start
  308.3 1.8 copy-start.2
  310.2 2.5 copy-start.1

commit v3 on v1

v3 whole, which is shorter than its diff:
```python
import functools

import jax
import jax.numpy as jnp
from jax import lax
from jax.experimental import pallas as pl
from jax.experimental.pallas import tpu as pltpu
from jax.sharding import PartitionSpec as P

HEAD_DIM = 64
DEPTH = 12
EPS = 1e-05
GELU_C = 0.7978845608028654
GELU_A = 0.044715
NEG = -1e30
BRANCH = DEPTH ** (-0.5)
MESH = pl.DeviceIdType.MESH
F32 = jnp.float32
BF16 = jnp.bfloat16


def gelu_value(u):
    return 0.5 * u * (1.0 + jnp.tanh(GELU_C * (u + GELU_A * u * u * u)))


def gelu_slope(u):
    inner = jnp.tanh(GELU_C * (u + GELU_A * u * u * u))
    return 0.5 * (1.0 + inner) + 0.5 * u * (1.0 - inner * inner) * GELU_C * (
        1.0 + 3.0 * GELU_A * u * u
    )


def normalize(x):
    centered = x - jnp.mean(x, axis=1, keepdims=True)
    inv = lax.rsqrt(jnp.mean(centered * centered, axis=1, keepdims=True) + EPS)
    return centered * inv, inv


def dot_nn(a, b):
    return lax.dot_general(a, b, (((1,), (0,)), ((), ())), preferred_element_type=F32)


def dot_nt(a, b):
    return lax.dot_general(a, b, (((1,), (1,)), ((), ())), preferred_element_type=F32)


def dot_tn(a, b):
    return lax.dot_general(a, b, (((0,), (0,)), ((), ())), preferred_element_type=F32)


def remote(src, dst, send, recv, **ids):
    return pltpu.make_async_remote_copy(
        src_ref=src, dst_ref=dst, send_sem=send, recv_sem=recv, device_id=ids, device_id_type=MESH
    )


class Place:
    def __init__(self, n_ctx):
        self.n = n_ctx
        self.c = lax.axis_index("ctx")
        self.d = lax.axis_index("dp")
        tp = lax.axis_index("tp")
        self.core = lax.rem(tp, 2)
        self.mate = tp + 1 - 2 * self.core
        chip = lax.div(tp, 2)
        self.across = (1 - chip) * 2 + self.core

    def barrier(self, dp, tp, ctx):
        sem = pltpu.get_barrier_semaphore()

        def hello(**ids):
            pl.semaphore_signal(sem, inc=1, device_id=ids, device_id_type=MESH)

        count = 0
        if dp:
            hello(dp=1 - self.d)
            count += 1
        if tp:
            hello(tp=self.mate)
            hello(tp=self.across)
            count += 2
        if ctx:
            pl.when(self.c > 0)(lambda: hello(ctx=self.c - 1))
            pl.when(self.c < self.n - 1)(lambda: hello(ctx=self.c + 1))
        if ctx:
            count = count + jnp.minimum(self.c, 1) + jnp.minimum(self.n - 1 - self.c, 1)
        pl.semaphore_wait(sem, count)


class TpSum:
    def __init__(self, place, half, mine, out_half, in_half, in_sum, total, send, recv):
        self.p, self.half = place, half
        self.mine, self.out_half, self.in_half = mine, out_half, in_half
        self.in_sum, self.total = in_sum, total
        self.send, self.recv = send, recv

    def rows(self, core):
        return pl.ds(pl.multiple_of(core * self.half, self.half), self.half)

    def c1(self):
        return remote(self.out_half, self.in_half, self.send.at[0], self.recv.at[0], tp=self.p.mate)

    def c2(self):
        return remote(self.mine, self.in_sum, self.send.at[1], self.recv.at[1], tp=self.p.across)

    def c3(self, core):
        part = self.total.at[self.rows(core)]
        return remote(part, part, self.send.at[2], self.recv.at[2], tp=self.p.mate)

    def start(self, partial):
        self.out_half[...] = partial(self.rows(1 - self.p.core)).astype(BF16)
        self.c1().start()
        self.mine[...] = partial(self.rows(self.p.core)).astype(BF16)

    def step2(self):
        self.c1().wait_recv()
        self.mine[...] = (self.mine[...].astype(F32) + self.in_half[...].astype(F32)).astype(BF16)
        self.c2().start()

    def step3(self):
        self.c2().wait_recv()
        both = self.mine[...].astype(F32) + self.in_sum[...].astype(F32)
        self.total[self.rows(self.p.core), :] = both.astype(BF16)
        self.c3(self.p.core).start()

    def finish(self):
        self.c3(1 - self.p.core).wait_recv()

    def drain(self):
        self.c1().wait_send()
        self.c2().wait_send()
        self.c3(self.p.core).wait_send()


def query_limits(border, prefix, m, c, rows):
    half = rows // 2
    lane = lax.broadcasted_iota(jnp.int32, (1, rows), 1)
    pos = jnp.where(lane < half, border[2 * c] * half + lane, border[2 * c + 1] * half + lane - half)
    return jnp.maximum(pos, prefix[m, 0] - 1)


def key_positions(border, block, half):
    return border[block] * half + lax.broadcasted_iota(jnp.int32, (half, 1), 0)


def vmem_specs(k):
    return [pl.BlockSpec(memory_space=pltpu.VMEM)] * k


def pack_weights(qkv_weight, out_weight, up_weight, down_weight, ln_gains, ln_shifts):
    q, k, v = qkv_weight[0], qkv_weight[1], qkv_weight[2]
    pad = jnp.zeros((q.shape[0], 64), BF16)
    wp = jnp.concatenate([q, pad, k, v], axis=1)
    wo = jnp.concatenate(
        [out_weight[64:], jnp.zeros((64, out_weight.shape[1]), BF16), out_weight[:64]], axis=0
    )
    ln = jnp.concatenate([ln_gains, ln_shifts], axis=0).astype(F32)
    ln = jnp.pad(ln, ((0, 4), (0, 0)))
    gather = functools.partial(lax.all_gather, axis_name="dp", tiled=True)
    return [
        gather(wp, axis=0), gather(wo, axis=1)[None], gather(up_weight, axis=0),
        gather(down_weight, axis=1)[None], gather(ln, axis=1)[None],
    ]


def wide(ref_stack, fn):
    return jnp.concatenate([fn(ref_stack[i]) for i in range(ref_stack.shape[0])], axis=1)


def narrow(ref_stack, value):
    size = ref_stack.shape[2]
    total = dot_nt(value[:, 0:size], ref_stack[0])
    for i in range(1, ref_stack.shape[0]):
        total += dot_nt(value[:, i * size : (i + 1) * size], ref_stack[i])
    return total


def norm_back(dn, xhat, inv, gain):
    e = dn * gain
    return inv * (
        e - jnp.mean(e, axis=1, keepdims=True) - xhat * jnp.mean(e * xhat, axis=1, keepdims=True)
    )


def ln_row(ln, row):
    return jnp.concatenate([ln[i, row : row + 1, :] for i in range(ln.shape[0])], axis=1)


def column_sums(value):
    return jnp.sum(value, axis=0, keepdims=True)


class GradSum:
    def __init__(self, place, peer, own, out, from_up, from_mid, send, recv):
        self.p = place
        self.peer, self.own, self.from_dp, self.up = peer, own, out, own
        self.from_up, self.from_mid, self.out = from_up, from_mid, out
        self.send, self.recv = send, recv
        c, n = place.c, place.n
        low = c < n // 2
        self.toward = jnp.where(low, c + 1, c - 1)
        self.away = jnp.where(low, c - 1, c + 1)
        self.end = jnp.logical_or(c == 0, c == n - 1)
        self.inner = jnp.logical_or(c == n // 2 - 1, c == n // 2)

    def dp_copy(self):
        return remote(self.peer, self.from_dp, self.send.at[0], self.recv.at[0], dp=1 - self.p.d)

    def up_copy(self):
        return remote(self.up, self.from_up, self.send.at[1], self.recv.at[1], ctx=self.toward)

    def mid_copy(self):
        return remote(self.up, self.from_mid, self.send.at[2], self.recv.at[2], ctx=self.toward)

    def down_copy(self):
        return remote(self.out, self.out, self.send.at[3], self.recv.at[3], ctx=self.away)

    def s0(self):
        self.dp_copy().start()

    def s1(self):
        self.dp_copy().wait_recv()

        @pl.when(self.end)
        def _():
            self.up[...] = (self.own[...].astype(F32) + self.from_dp[...].astype(F32)).astype(BF16)

        @pl.when(jnp.logical_not(self.end))
        def _():
            self.up_copy().wait_recv()
            self.up[...] = (
                self.own[...].astype(F32) + self.from_dp[...].astype(F32)
                + self.from_up[...].astype(F32)
            ).astype(BF16)

        pl.when(self.inner)(lambda: self.mid_copy().start())
        pl.when(jnp.logical_not(self.inner))(lambda: self.up_copy().start())

    def s2(self):
        @pl.when(self.inner)
        def _():
            self.mid_copy().wait_recv()
            self.out[...] = (self.up[...].astype(F32) + self.from_mid[...].astype(F32)).astype(BF16)
            pl.when(jnp.logical_not(self.end))(lambda: self.down_copy().start())

    def s3(self):
        @pl.when(jnp.logical_not(self.inner))
        def _():
            self.down_copy().wait_recv()
            pl.when(jnp.logical_not(self.end))(lambda: self.down_copy().start())

    def drain(self):
        self.dp_copy().wait_send()
        pl.when(self.inner)(lambda: self.mid_copy().wait_send())
        pl.when(jnp.logical_not(self.inner))(lambda: self.up_copy().wait_send())
        pl.when(jnp.logical_not(self.end))(lambda: self.down_copy().wait_send())


A_SUM, N2_SUM, MLP_SUM, N1_SUM = 0, 2, 4, 6
B_CUT = 128


def cuts_of(rows):
    at, cuts = 0, []
    while at < rows:
        size = min(512, rows - at)
        cuts.append((at, size))
        at += size
    return cuts


def block_kernel(n_ctx, exchange, prefix, border, hid, cot, *refs):
    if exchange:
        (qkv_s, out_s, up_s, down_s, gain_s, shift_s) = refs[:6]
        (block, grad_in, ga, gb, gs) = refs[6:11]
        (wp, wo, wu, wd, ln, grads, gb_buf, gs_buf, b_fu, b_fm, a_fu, a_fm, s_fu, s_fm,
         wsend, wrecv, gsend, grecv) = refs[11:29]
        refs = refs[29:]
    else:
        (wp, wo, wu, wd, ln) = refs[:5]
        (block, grad_in, grads, gb, gs) = refs[5:10]
        refs = refs[10:]
    (attn, heads, lse, o_t, qs, kv, h1, m_row, l_row, o_acc, act, d_mlp, d_up, h2, n2_tot, d_attn,
     sbuf, rbuf, acc, qh, doh, dq_t, delta, d_pack, stats, ks, kr, kvs, kvr,
     t_mine, t_out, t_in, t_sum, tsend, trecv) = refs
    p = Place(n_ctx)
    c, n = p.c, n_ctx
    micro, rows, width = hid.shape
    half = rows // 2
    ff = wu.shape[1]
    parts = 2 if exchange else 1
    cols = width // parts
    own_rows = width // parts
    tiles = rows // 128
    p.barrier(exchange, True, True)

    def tp_sum(kind, m, total):
        i = kind + m
        return TpSum(
            p, half, t_mine.at[i], t_out.at[i], t_in.at[i], t_sum.at[i], total, tsend.at[i],
            trecv.at[i],
        )

    a_sums = [tp_sum(A_SUM, m, attn.at[m]) for m in range(micro)]
    n2_sums = [tp_sum(N2_SUM, m, n2_tot.at[m]) for m in range(micro)]
    mlp_sums = [tp_sum(MLP_SUM, m, block.at[m]) for m in range(micro)]
    n1_sums = [tp_sum(N1_SUM, m, n2_tot.at[m]) for m in range(micro)]

    def tile(i, base=0):
        return pl.ds(pl.multiple_of(base + i * 128, 128), 128)

    if exchange:
        mine = pl.ds(pl.multiple_of(p.d * own_rows, own_rows), own_rows)
        places = (ln.at[p.d], wp.at[mine], wo.at[p.d], wu.at[mine], wd.at[p.d])
        sources = (ln.at[p.d], wp.at[mine], wo.at[p.d], up_s, down_s)

        def weight_copy(i):
            return remote(sources[i], places[i], wsend.at[i], wrecv.at[i], dp=1 - p.d)

        ln[p.d] = jnp.concatenate(
            [gain_s[...].astype(F32), shift_s[...].astype(F32), jnp.zeros((4, cols), F32)], axis=0
        )
        weight_copy(0).start()
        wp[mine, 0:256] = jnp.concatenate(
            [qkv_s[0], jnp.zeros((own_rows, 64), BF16)], axis=1
        )
        wp[mine, 256:640] = jnp.concatenate([qkv_s[1], qkv_s[2]], axis=1)
        weight_copy(1).start()
        wo[p.d, 0:128, :] = out_s[64:192, :]
        wo[p.d, 128:192, :] = jnp.zeros((64, cols), BF16)
        wo[p.d, 192:256, :] = out_s[0:64, :]
        for i in range(2, 5):
            weight_copy(i).start()
        wu[mine, :] = up_s[...]
        wd[p.d] = down_s[...]

    def weight_wait(*which):
        if exchange:
            for i in which:
                weight_copy(i).wait_recv()

    weight_wait(0)
    gain0, gain1, shift0, shift1 = (ln_row(ln, i) for i in range(4))
    for m in range(micro):
        @pl.loop(0, tiles)
        def _(i, m=m):
            xhat, _ = normalize(hid[m, tile(i), :].astype(F32))
            h1[tile(i, m * rows), :] = (xhat * gain0 + shift0).astype(BF16)

    def kv_copy(m, way, s):
        j, to = (c - s, c + 1) if way == 0 else (c + s, c - 1)
        piece = kv.at[m, j]
        return remote(piece, piece, ks.at[m, way, s], kr.at[m, way, s + 1], ctx=to)

    def kv_arrival(m, way, s):
        j, to = (c - s, c - 1) if way == 0 else (c + s, c + 1)
        piece = kv.at[m, j]
        return remote(piece, piece, ks.at[m, way, s], kr.at[m, way, s], ctx=to)

    def has(way, s):
        return c - s >= 0 if way == 0 else c + s < n

    def sends(way, s):
        if way == 0:
            return jnp.logical_and(c - s >= 0, c + 1 < n)
        return jnp.logical_and(c + s < n, c - 1 >= 0)

    weight_wait(1)
    for m in range(micro):
        @pl.loop(0, tiles)
        def _(i, m=m):
            packed = dot_nn(h1[tile(i, m * rows), :], wp[...])
            q = packed[:, 0:256].astype(BF16).astype(F32) * HEAD_DIM ** (-0.5)
            qs[m, tile(i), :] = q.astype(BF16)
            kv[m, c, tile(i), :] = packed[:, 256:640].astype(BF16)

        if m == 0:
            for way in range(2):
                pl.when(sends(way, 0))(lambda way=way: kv_copy(0, way, 0).start())
    pl.when(c == 0)(lambda: kv_copy(1, 0, 0).start())
    pl.when(c == n - 1)(lambda: kv_copy(1, 1, 0).start())

    lanes = lax.broadcasted_iota(jnp.int32, (rows, 128), 1)

    def halves(value):
        zero = jnp.zeros_like(value)
        return jnp.where(lanes < 64, value, zero), jnp.where(lanes < 64, zero, value)

    def split_queries(m):
        qh[0], qh[1] = halves(qs[m, :, 0:128])
        qh[2] = qs[m, :, 128:256]

    def attend(m, j, limits):
        for b in range(2):
            span = pl.ds(b * half, half)
            k01 = kv[m, j, span, 0:128]
            k2v0 = kv[m, j, span, 128:256]
            t0 = k2v0.T
            t12 = kv[m, j, span, 256:384].T
            allowed = key_positions(border, 2 * j + b, half) <= limits
            for h in range(3):
                scores = dot_nt(k2v0 if h == 2 else k01, qh[h])
                scores = jnp.where(allowed, scores, NEG)
                old = m_row[h]
                top = jnp.maximum(old, jnp.max(scores, axis=0, keepdims=True))
                prob = jnp.exp(scores - top)
                fade = jnp.exp(old - top)
                m_row[h] = top
                l_row[h] = l_row[h] * fade + jnp.sum(prob, axis=0, keepdims=True)
                v_t = t0[64:128] if h == 0 else t12[(h - 1) * 64 : h * 64]
                o_acc[h] = o_acc[h] * fade + dot_nn(v_t, prob.astype(BF16))

    def at_step(t, at, jobs):
        @pl.when(t == min(at, 2 * n - 2))
        def _():
            for job in jobs:
                job()

    def forward(m, side):
        limits = query_limits(border, prefix, m, c, rows)
        split_queries(m)
        m_row[...] = jnp.full(m_row.shape, NEG, F32)
        l_row[...] = jnp.zeros(l_row.shape, F32)
        o_acc[...] = jnp.zeros(o_acc.shape, F32)

        @pl.loop(0, 2 * n - 1)
        def _(t):
            s = lax.div(t + 1, 2)
            right = lax.rem(t, 2) == 1
            left = jnp.logical_and(lax.rem(t, 2) == 0, t > 0)

            def arrive(way):
                kv_arrival(m, way, s).wait_recv()
                pl.when(sends(way, s))(lambda: kv_copy(m, way, s).start())
                if m == 0:
                    last = c if way == 0 else n - 1 - c
                    pl.when(jnp.logical_and(s == last, sends(way, 0)))(
                        lambda: kv_copy(1, way, 0).start()
                    )

            pl.when(jnp.logical_and(right, has(0, s)))(lambda: arrive(0))
            pl.when(jnp.logical_and(left, has(1, s)))(lambda: arrive(1))
            j = jnp.where(right, c - s, c + s)

            @pl.when(jnp.logical_and(j >= 0, j < n))
            def _():
                attend(m, j, limits)

            for at, jobs in side.items():
                at_step(t, at, jobs)

        flat = pl.ds(m * rows, rows)
        dq_t[128:192, :] = jnp.zeros((64, rows), F32)
        for h in range(3):
            norm = o_acc[h] / l_row[h]
            o_t[m, h] = norm
            lse[m, h : h + 1, :] = m_row[h] + jnp.log(l_row[h])
            at = 192 if h == 0 else (h - 1) * 64
            dq_t[at : at + 64, :] = norm
        heads[flat, :] = dq_t[...].T.astype(BF16)
        if m == 0:
            weight_wait(2)
        a_sums[m].start(
            lambda span: wide(wo, lambda w: dot_nn(heads[pl.ds(m * rows + span.start, half), :], w))
        )

    def middle(m, i):
        return hid[m, tile(i), :].astype(F32) + BRANCH * attn[m, tile(i), :].astype(F32)

    def mlp_tiles(m, first, last):
        @pl.loop(first, last)
        def _(i):
            flat = tile(i, m * rows)
            xhat, _ = normalize(middle(m, i))
            normed = (xhat * gain1 + shift1).astype(BF16)
            h2[flat, :] = normed
            up = dot_nn(normed, wu[...])
            active = gelu_value(up).astype(BF16)
            act[flat, :] = active
            down_grad = (BRANCH * cot[m, tile(i), :].astype(F32)).astype(BF16)
            d_mlp[flat, :] = down_grad
            d_up[flat, :] = (narrow(wd, down_grad) * gelu_slope(up)).astype(BF16)
            block[m, tile(i), :] = wide(wd, lambda w: dot_nn(active, w)).astype(BF16)

    def n2_start(m):
        n2_sums[m].start(
            lambda span: dot_nt(d_up[pl.ds(m * rows + span.start, half), :], wu[...])
        )

    def mlp_start(m):
        mlp_sums[m].start(lambda span: block[m, span, :])

    def middle_gradient(m):
        @pl.loop(0, tiles)
        def _(i):
            xhat, inv = normalize(middle(m, i))
            dn = n2_tot[m, tile(i), :].astype(F32)
            grad = cot[m, tile(i), :].astype(F32) + norm_back(dn, xhat, inv, gain1)
            grad_in[m, tile(i), :] = grad
            d_attn[tile(i, m * rows), :] = (BRANCH * grad).astype(BF16)
            stats[1:2, :] += column_sums(dn * xhat)
            stats[3:4, :] += column_sums(dn)

    def write_block(m):
        mlp_sums[m].finish()
        mlp_sums[m].drain()

        @pl.loop(0, tiles)
        def _(i):
            out = middle(m, i) + BRANCH * block[m, tile(i), :].astype(F32)
            block[m, tile(i), :] = out.astype(BF16)

    def down_gradient():
        @pl.loop(0, ff // 256)
        def _(i):
            to = pl.ds(pl.multiple_of(i * 256, 256), 256)
            left = act[:, to]
            for k in range(parts):
                grads[k, to, :] = dot_tn(left, d_mlp[:, k * cols : (k + 1) * cols]).astype(BF16)

    def up_gradient():
        for k in range(parts):
            @pl.loop(0, own_rows // 128)
            def _(i, k=k):
                value = dot_tn(h2[:, tile(i, k * own_rows)], d_up[...]).astype(BF16)
                for q in range(ff // cols):
                    grads[k, tile(i, ff + q * own_rows), :] = value[:, q * cols : (q + 1) * cols]

    def out_gradient():
        at = ff + own_rows * (ff // cols)
        for k in range(parts):
            grads[k, at : at + 256, :] = dot_tn(
                heads[...], d_attn[:, k * cols : (k + 1) * cols]
            ).astype(BF16)

    early, late, last = [], [], []
    if exchange:
        for i, (at, size) in enumerate(cuts_of(grads.shape[1])):
            cut = pl.ds(at, size)
            early.append(GradSum(
                p, grads.at[1 - p.d, cut], grads.at[p.d, cut], ga.at[cut], a_fu.at[cut],
                a_fm.at[cut], gsend.at[i], grecv.at[i],
            ))
        for i in range(own_rows // B_CUT):
            cut, k = pl.ds(i * B_CUT, B_CUT), len(early) + i
            late.append(GradSum(
                p, gb_buf.at[1 - p.d, cut], gb_buf.at[p.d, cut], gb.at[cut], b_fu.at[cut],
                b_fm.at[cut], gsend.at[k], grecv.at[k],
            ))
        k = len(early) + len(late)
        last = [GradSum(
            p, gs_buf.at[1 - p.d], gs_buf.at[p.d], gs, s_fu, s_fm, gsend.at[k], grecv.at[k]
        )]

    def stage(group, name):
        return [getattr(piece, name) for piece in group]

    def dkv_copy(m, way, j):
        to = c + 1 if way == 0 else c - 1
        return remote(
            sbuf.at[j], rbuf.at[m, j + 1 - way], kvs.at[m, way, j], kvr.at[m, way, j], ctx=to
        )

    def dkv_landed(m, way, j):
        to = c - 1 if way == 0 else c + 1
        return remote(
            sbuf.at[j], rbuf.at[m, j + 1 - way], kvs.at[m, way, j], kvr.at[m, way, j], ctx=to
        )

    def upstream(way):
        return c > 0 if way == 0 else c < n - 1

    def attend_back(m, j, limits):
        for b in range(2):
            span = pl.ds(b * half, half)
            k01 = kv[m, j, span, 0:128]
            k2v0 = kv[m, j, span, 128:256]
            v12 = kv[m, j, span, 256:384]
            t01 = k01.T
            t2 = k2v0.T
            allowed = key_positions(border, 2 * j + b, half) <= limits
            sums = {}
            for h in range(3):
                scores = dot_nt(k2v0 if h == 2 else k01, qh[h])
                prob = jnp.exp(jnp.where(allowed, scores, NEG) - lse[m, h : h + 1, :])
                d_prob = dot_nt(k2v0 if h == 0 else v12, doh[h])
                d_scores = (prob * (d_prob - delta[h])).astype(BF16)
                dk = dot_nn(d_scores, qh[h])
                dv = dot_nn(prob.astype(BF16), doh[h])
                k_at, v_at = (1 if h == 2 else 0), (1 if h == 0 else 2)
                sums[k_at] = dk if k_at not in sums else sums[k_at] + dk
                sums[v_at] = dv if v_at not in sums else sums[v_at] + dv
                k_t = t2[0:64] if h == 2 else t01[h * 64 : (h + 1) * 64]
                dq_t[h * 64 : (h + 1) * 64, :] += dot_nn(k_t, d_scores)
            for k in range(3):
                acc[span, k * 128 : (k + 1) * 128] = sums[k]

    def backward(m, side):
        flat = pl.ds(m * rows, rows)
        limits = query_limits(border, prefix, m, c, rows)
        upper = d_attn[flat, :]
        d_heads = narrow(wo, upper).astype(BF16)
        doh[0] = d_heads[:, 128:256]
        doh[1], doh[2] = halves(d_heads[:, 0:128])
        size = wo.shape[2]
        d_heads_t = dot_nt(wo[0], upper[:, 0:size])
        for i in range(1, wo.shape[0]):
            d_heads_t += dot_nt(wo[i], upper[:, i * size : (i + 1) * size])
        for h in range(3):
            at = 192 if h == 0 else (h - 1) * 64
            delta[h] = jnp.sum(d_heads_t[at : at + 64] * o_t[m, h], axis=0, keepdims=True)
        split_queries(m)
        dq_t[...] = jnp.zeros(dq_t.shape, F32)

        @pl.loop(0, 2 * n - 1)
        def _(t):
            s = n - 1 - lax.div(t, 2)
            own = t == 2 * n - 2
            right = jnp.logical_and(lax.rem(t, 2) == 0, jnp.logical_not(own))
            j = jnp.where(right, c + s, c - s)

            @pl.when(jnp.logical_and(j >= 0, j < n))
            def _():
                attend_back(m, j, limits)

                def pass_on(way):
                    if m > 0:
                        dkv_copy(m - 1, way, j).wait_send()

                    @pl.when(upstream(way))
                    def _():
                        dkv_landed(m, way, j).wait_recv()
                        sbuf[j] = (acc[...] + rbuf[m, j + 1 - way].astype(F32)).astype(BF16)

                    @pl.when(jnp.logical_not(upstream(way)))
                    def _():
                        sbuf[j] = acc[...].astype(BF16)

                    dkv_copy(m, way, j).start()

                pl.when(right)(lambda: pass_on(0))
                pl.when(jnp.logical_and(jnp.logical_not(right), jnp.logical_not(own)))(
                    lambda: pass_on(1)
                )

            for at, jobs in side.items():
                at_step(t, at, jobs)

        @pl.when(upstream(0))
        def _():
            dkv_landed(m, 0, c).wait_recv()
            acc[...] += rbuf[m, c + 1].astype(F32)

        @pl.when(upstream(1))
        def _():
            dkv_landed(m, 1, c).wait_recv()
            acc[...] += rbuf[m, c].astype(F32)

        d_pack[flat, 256:640] = acc[...].astype(BF16)
        d_pack[flat, 0:256] = (dq_t[...].T * HEAD_DIM ** (-0.5)).astype(BF16)
        n1_sums[m].start(
            lambda span: dot_nt(d_pack[pl.ds(m * rows + span.start, half), :], wp[...])
        )

    def finish_rows(m):
        @pl.loop(0, tiles)
        def _(i):
            xhat, inv = normalize(hid[m, tile(i), :].astype(F32))
            dn = n2_tot[m, tile(i), :].astype(F32)
            grad_in[m, tile(i), :] += norm_back(dn, xhat, inv, gain0)
            stats[0:1, :] += column_sums(dn * xhat)
            stats[2:3, :] += column_sums(dn)

    def pack_tile(k, i):
        return dot_tn(h1[:, tile(i, k * own_rows)], d_pack[...])

    def do(jobs):
        for job in jobs:
            job()

    stats[...] = jnp.zeros(stats.shape, F32)
    a0, a1 = a_sums
    x0, x1 = n2_sums
    u0, u1 = mlp_sums
    y0, y1 = n1_sums
    forward(0, {})
    forward(1, {
        0: [a0.step2],
        2: [a0.step3, a0.finish, lambda: weight_wait(3, 4), lambda: mlp_tiles(0, 0, tiles // 2)],
        4: [lambda: mlp_tiles(0, tiles // 2, tiles), lambda: n2_start(0)],
        6: [x0.step2],
    })
    a1.step2()
    x0.step3()
    x0.finish()
    middle_gradient(0)
    x0.drain()
    backward(0, {
        0: [lambda: mlp_start(0)],
        1: [a1.step3],
        2: [a1.finish, lambda: mlp_tiles(1, 0, tiles // 2)],
        3: [u0.step2, lambda: mlp_tiles(1, tiles // 2, tiles), lambda: n2_start(1)],
        4: [x1.step2, down_gradient] + stage(early[0:1], "s0"),
        5: [up_gradient] + stage(early[1:3], "s0"),
        6: [u0.step3, lambda: mlp_start(1), x1.step3],
    })
    x1.finish()
    middle_gradient(1)
    x1.drain()
    out_gradient()
    do(stage(early[3:], "s0"))
    backward(1, {
        0: [y0.step2, u1.step2],
        2: stage(early[0:1], "s1"),
        3: [y0.step3] + stage(early[1:2], "s1"),
        4: stage(early[2:3], "s1") + stage(early[0:1], "s2"),
        5: [u1.step3] + stage(early[3:], "s1") + stage(early[1:2], "s2"),
        6: stage(early[2:], "s2") + stage(early[0:2], "s3"),
    })
    if exchange:
        for i in range(len(late)):
            gb_buf[1 - p.d, i * B_CUT : (i + 1) * B_CUT, :] = pack_tile(1 - p.d, i).astype(BF16)
            late[i].s0()
        for i in range(len(late)):
            gb_buf[p.d, i * B_CUT : (i + 1) * B_CUT, :] = pack_tile(p.d, i).astype(BF16)
    else:
        @pl.loop(0, width // 128)
        def _(i):
            gb[tile(i), :] = pack_tile(0, i)
    y1.step2()
    y0.finish()
    finish_rows(0)
    do(stage(late[0:2], "s1"))
    write_block(0)
    do(stage(late[2:], "s1"))
    y1.step3()
    do(stage(late[0:2], "s2"))
    write_block(1)
    do(stage(late[2:], "s2"))
    y1.finish()
    finish_rows(1)
    if exchange:
        for k in range(2):
            cut = slice(k * cols, (k + 1) * cols)
            gs_buf[k] = jnp.concatenate([stats[:, cut], jnp.zeros((8, cols), F32)], axis=0).astype(BF16)
        do(stage(last, "s0"))
        do(stage(early[2:], "s3"))
        do(stage(last, "s1"))
        do(stage(late, "s3"))
        do(stage(last, "s2"))
        do(stage(last, "s3"))
        for piece in early + late + last:
            piece.drain()
        for i in range(5):
            weight_copy(i).wait_send()
    else:
        gs[...] = stats[...]
    for m in range(micro):
        for way in range(2):
            for s in range(n - 1):
                pl.when(sends(way, s))(lambda m=m, way=way, s=s: kv_copy(m, way, s).wait_send())
        a_sums[m].drain()
        n1_sums[m].drain()
    for j in range(n):
        pl.when(c < j)(lambda j=j: dkv_copy(micro - 1, 0, j).wait_send())
        pl.when(c > j)(lambda j=j: dkv_copy(micro - 1, 1, j).wait_send())


def run_block(n_ctx, exchange, prefix, border, hid, cot, weights, ff):
    micro, rows, width = hid.shape
    half = rows // 2
    total = micro * rows
    parts = 2 if exchange else 1
    cols = width // parts
    sds = jax.ShapeDtypeStruct
    vmem = pltpu.VMEM
    sems = pltpu.SemaphoreType.DMA
    grad_rows = ff + cols * (ff // cols) + 256
    outs = [sds((micro, rows, width), BF16), sds((micro, rows, width), F32)]
    scratch = []
    if exchange:
        outs += [sds((grad_rows, cols), BF16), sds((cols, 640), BF16), sds((16, cols), BF16)]
        pieces = len(cuts_of(grad_rows)) + cols // B_CUT + 1
        scratch += [
            vmem((width, 640), BF16), vmem((2, 256, cols), BF16), vmem((width, ff), BF16),
            vmem((2, ff, cols), BF16), vmem((2, 8, cols), F32),
            vmem((2, grad_rows, cols), BF16), vmem((2, cols, 640), BF16), vmem((2, 16, cols), BF16),
            vmem((cols, 640), BF16), vmem((cols, 640), BF16),
            vmem((grad_rows, cols), BF16), vmem((grad_rows, cols), BF16),
            vmem((16, cols), BF16), vmem((16, cols), BF16),
            sems((5,)), sems((5,)), sems((pieces, 4)), sems((pieces, 4)),
        ]
    else:
        outs += [
            sds((1, grad_rows, cols), BF16), sds((width, 640), F32), sds((8, width), F32)
        ]
    scratch += [
        vmem((micro, rows, width), BF16), vmem((total, 256), BF16), vmem((micro, 8, rows), F32),
        vmem((micro, 3, 64, rows), F32), vmem((micro, rows, 256), BF16),
        vmem((micro, n_ctx, rows, 384), BF16), vmem((total, width), BF16),
        vmem((3, 1, rows), F32), vmem((3, 1, rows), F32), vmem((3, 64, rows), F32),
        vmem((total, ff), BF16), vmem((total, width), BF16), vmem((total, ff), BF16),
        vmem((total, width), BF16), vmem((micro, rows, width), BF16), vmem((total, width), BF16),
        vmem((n_ctx, rows, 384), BF16), vmem((micro, n_ctx + 1, rows, 384), BF16),
        vmem((rows, 384), F32), vmem((3, rows, 128), BF16), vmem((3, rows, 128), BF16),
        vmem((256, rows), F32), vmem((3, 1, rows), F32), vmem((total, 640), BF16),
        vmem((8, width), F32),
        sems((micro, 2, n_ctx + 1)), sems((micro, 2, n_ctx + 1)),
        sems((micro, 2, n_ctx)), sems((micro, 2, n_ctx)),
    ]
    scratch += [vmem((8, half, width), BF16)] * 4 + [sems((8, 3))] * 2
    smem = pl.BlockSpec(memory_space=pltpu.SMEM)
    return pl.pallas_call(
        functools.partial(block_kernel, n_ctx, exchange),
        out_shape=outs,
        in_specs=[smem, smem] + vmem_specs(2 + len(weights)),
        out_specs=vmem_specs(len(outs)),
        scratch_shapes=scratch,
        compiler_params=pltpu.CompilerParams(
            collective_id=0, has_side_effects=True, vmem_limit_bytes=67043328
        ),
        name="block_both_ways",
    )(prefix, border, hid, cot, *weights)


def unpack_kernel(ff, ga, gb, gs, qkv, out, up, down, gains, shifts):
    rows, cols = qkv.shape[1], ga.shape[1]
    down[...] = ga[0:ff, :].astype(F32)
    for k in range(ff // cols):
        up[:, k * cols : (k + 1) * cols] = ga[ff + k * rows : ff + (k + 1) * rows, :].astype(F32)
    at = ff + rows * (ff // cols)
    out[0:64, :] = ga[at + 192 : at + 256, :].astype(F32)
    out[64:192, :] = ga[at : at + 128, :].astype(F32)
    qkv[0] = gb[:, 0:192].astype(F32)
    qkv[1] = gb[:, 256:448].astype(F32)
    qkv[2] = gb[:, 384:640].astype(F32)[:, 64:256]
    gains[...] = gs[...].astype(F32)[0:2]
    shifts[...] = gs[...].astype(F32)[2:4]


def body(
    hidden_in, prefix, block_order, qkv_weight, out_weight, up_weight, down_weight, ln_gains,
    ln_shifts, cotangent,
):
    micro, _, tokens, width = hidden_in.shape
    n_ctx = lax.axis_size("ctx")
    exchange = lax.axis_size("dp") == 2 and n_ctx % 2 == 0
    ff = up_weight.shape[1]
    params = (qkv_weight, out_weight, up_weight, down_weight, ln_gains, ln_shifts)
    weights = params if exchange else pack_weights(*params)
    hid, cot = hidden_in[:, 0], cotangent[:, 0]
    block, grad_in, ga, gb, gs = run_block(
        n_ctx, exchange, prefix, block_order, hid, cot, weights, ff
    )
    if exchange:
        owned = pl.pallas_call(
            functools.partial(unpack_kernel, ff),
            out_shape=[jax.ShapeDtypeStruct(w.shape, F32) for w in params],
            in_specs=vmem_specs(3),
            out_specs=vmem_specs(6),
            name="unpack_gradients",
        )(ga, gb, gs)
    else:
        ga = ga[0].astype(F32)
        g_out = ga[ff + width :]
        whole = lax.psum(
            (
                jnp.stack([gb[:, 0:192], gb[:, 256:448], gb[:, 448:640]]),
                jnp.concatenate([g_out[192:], g_out[:128]], axis=0), ga[ff : ff + width], ga[:ff],
                gs[0:2], gs[2:4],
            ),
            "ctx",
        )
        owned = [
            lax.psum_scatter(v, "dp", scatter_dimension=d, tiled=True)
            for v, d in zip(whole, (1, 1, 0, 1, 1, 1))
        ]
    return (block[:, None], grad_in[:, None], *owned)


def solution(mesh):
    in_specs = (
        P(None, "dp", "ctx", None), P(None, "dp"), P(), P(None, "dp", "tp"), P("tp", "dp"),
        P("dp", "tp"), P("tp", "dp"), P(None, "dp"), P(None, "dp"), P(None, "dp", "ctx", None),
    )
    out_specs = (
        P(None, "dp", "ctx", None), P(None, "dp", "ctx", None), P(None, "dp", "tp"),
        P("tp", "dp"), P("dp", "tp"), P("tp", "dp"), P(None, "dp"), P(None, "dp"),
    )
    return jax.shard_map(body, mesh=mesh, in_specs=in_specs, out_specs=out_specs, check_vma=False)
```

time: 778 us -> 270 us (0.35)
  waiting for transfers between devices: 460 us -> 0 us
  Pallas kernels: 95.1 us -> 259 us
  matrix products: 77.9 us -> 0 us
  other arithmetic: 59.6 us -> 0 us
  local copies, waits for them, and re-layouts: 50.1 us -> 10 us
  between operations: 15.4 us -> 0.65 us
  blocking collectives: 12.7 us -> 0 us
    psum x3 -> x0, waiting for transfers between devices: 253 us -> none  [the longest x1 123 us: body(): whole = lax.psum((g_qkv, g_out, g_up, g_down, g_gains, g_shifts), 'ctx')]
    reduce_scatter x6 -> x0, waiting for transfers between devices: 185 us -> none  [the longest x4 116 us: body(): lax.psum_scatter(v, 'dp', scatter_dimension=d, tiled=True)]
    pallas_call x1 -> x2, Pallas kernels: 95.1 us -> 259 us  [the longest x1 256 us: run_block(): pl.pallas_call(functools.partial(block_kernel, n_ctx, exchange), out_shap...]
    dot_general x30 -> x0, matrix products: 77.9 us -> none  [the longest x8 15.6 us: dot_tn(): lax.dot_general(a, b, (((0,), (0,)), ((), ())), preferred_element_type=F32)]
    unnamed x13 -> x0, waiting for transfers between devices: 22.6 us -> none
    slice x21 -> x0, local copies, waits for them, and re-layouts: 21.6 us -> none  [the longest x4 9.52 us: body(): values = flat[:, local_width:].reshape(seq_len, heads_n, HEAD_DIM)]
    convert_element_type x2 -> x0, other arithmetic: 13.5 us -> none  [body(): (prob * (d_prob - jnp.sum(prob * d_prob, axis=2, keepdims=True))).astype(...]
    reduce_sum x5 -> x0, other arithmetic: 13.3 us -> none  [the longest x1 4.8 us: body(): jnp.sum(d_n1 * xhat1, axis=0)]
  transfers between devices with their start and end apart: 11 -> 0, of which waited for: 11 -> 0; matrix products, arithmetic and copies ran while one was open for 15% -> 0% of each run, Pallas kernels for 0% -> 0%
where the time goes in v3:
time: 270 us
  Pallas kernels  259 us (96%)
  local copies, waits for them, and re-layouts  10 us (4%)
    pallas_call x1, Pallas kernels, run_block(): pl.pallas_call(functools.partial(block_kernel, n_ctx, exchange), out_shap...  256 us
    unnamed x9, local copies, waits for them, and re-layouts  10 us

profile of v3, /device:TPU:0, one launch (start us, length us, event | category | flops | bytes accessed | tf_op | source)
XLA Modules:
  0.0 269.9 jit_solution(10935469309484528175)
XLA Ops:
  0.6 1.3 copy.18.prefix
  1.9 2.1 copy.19.refs_0_
  4.0 255.7 %block_both_ways.1 = (bf16[2,512,768]{2,1,0:T(8,128)(2,1)}, f32[2,512,768]{2,1,0:T(8,128)}, bf16[1792,384]{1,0:T(8,128)(2,1)}, bf16[384,640]{1,0:T(8,128)(2,1)}, bf16[16,384]{1,0:T(8,128)(2,1)}) custom-call(s32[2,1]{1,0:T(2,128)} %copy.18.prefix, s32[8]{0:T(128)} %border.1, bf16[2,512,768]{2,1,0:T(8,128)(2,1)} %bitcast.10, bf16[2,512,768]{2,1,0:T(8,128)(2,1)} %bitcast.11, ...), custom_call_target="tpu_custom_call" | custom-call | tf_op jit(solution)/shard_map/block_both_ways/pallas_call | solution.py:813
  259.7 0.0 copy-start.1
  259.7 3.6 %unpack_gradients.1 = (f32[3,384,192]{2,1,0:T(8,128)}, f32[192,384]{1,0:T(8,128)}, f32[384,768]{1,0:T(8,128)}, f32[768,384]{1,0:T(8,128)}, f32[2,384]{1,0:T(2,128)}, /*index=5*/f32[2,384]{1,0:T(2,128)}) custom-call(bf16[1792,384]{1,0:T(8,128)(2,1)} %get-tuple-element.21.ga, bf16[384,640]{1,0:T(8,128)(2,1)} %get-tuple-element.22.gb, ...), custom_call_target="tpu_custom_call" | custom-call | tf_op jit(solution)/shard_map/unpack_gradients/pallas_call | solution.py:856
  263.3 2.5 copy.22
  265.8 0.0 copy-done.1
  265.8 0.0 copy-start
  265.8 1.1 copy.25
  266.9 1.3 copy-done
  268.2 1.7 copy.26
Async XLA Ops:
  259.7 6.1 %copy-start.1 = (bf16[2,512,768]{2,1,0:T(8,128)(2,1)S(1)}, bf16[2,512,768]{2,1,0:T(8,128)(2,1)}, u32[]{:S(2)}) copy-start(bf16[2,512,768]{2,1,0:T(8,128)(2,1)} %get-tuple-element.19) | copy-start | bytes 4718596
  265.8 2.5 copy-start

commit v4 on v3

--- a/solution.py
+++ b/solution.py
@@ -88,14 +88,14 @@
 
 
 class TpSum:
-    def __init__(self, place, half, mine, out_half, in_half, in_sum, total, send, recv):
-        self.p, self.half = place, half
+    def __init__(self, place, half, first, size, mine, out_half, in_half, in_sum, total, send, recv):
+        self.p, self.half, self.first, self.size = place, half, first, size
         self.mine, self.out_half, self.in_half = mine, out_half, in_half
         self.in_sum, self.total = in_sum, total
         self.send, self.recv = send, recv
 
     def rows(self, core):
-        return pl.ds(pl.multiple_of(core * self.half, self.half), self.half)
+        return pl.ds(pl.multiple_of(core * self.half + self.first, self.size), self.size)
 
     def c1(self):
         return remote(self.out_half, self.in_half, self.send.at[0], self.recv.at[0], tp=self.p.mate)
@@ -107,10 +107,16 @@
         part = self.total.at[self.rows(core)]
         return remote(part, part, self.send.at[2], self.recv.at[2], tp=self.p.mate)
 
-    def start(self, partial):
+    def start_other(self, partial):
         self.out_half[...] = partial(self.rows(1 - self.p.core)).astype(BF16)
         self.c1().start()
+
+    def start_own(self, partial):
         self.mine[...] = partial(self.rows(self.p.core)).astype(BF16)
+
+    def start(self, partial):
+        self.start_other(partial)
+        self.start_own(partial)
 
     def step2(self):
         self.c1().wait_recv()
@@ -136,7 +142,7 @@
     half = rows // 2
     lane = lax.broadcasted_iota(jnp.int32, (1, rows), 1)
     pos = jnp.where(lane < half, border[2 * c] * half + lane, border[2 * c + 1] * half + lane - half)
-    return jnp.maximum(pos, prefix[m, 0] - 1)
+    return jnp.maximum(pos, prefix[m] - 1)
 
 
 def key_positions(border, block, half):
@@ -148,17 +154,16 @@
 
 
 def pack_weights(qkv_weight, out_weight, up_weight, down_weight, ln_gains, ln_shifts):
-    q, k, v = qkv_weight[0], qkv_weight[1], qkv_weight[2]
-    pad = jnp.zeros((q.shape[0], 64), BF16)
-    wp = jnp.concatenate([q, pad, k, v], axis=1)
-    wo = jnp.concatenate(
-        [out_weight[64:], jnp.zeros((64, out_weight.shape[1]), BF16), out_weight[:64]], axis=0
-    )
+    turned = jnp.swapaxes(qkv_weight, 1, 2)
+    pad = jnp.zeros((64, turned.shape[2]), BF16)
+    wp = jnp.concatenate([turned[0], pad, turned[1], turned[2]], axis=0)
+    pad = jnp.zeros((64, out_weight.shape[1]), BF16)
+    wo = jnp.concatenate([out_weight[64:], pad, out_weight[:64]], axis=0)
     ln = jnp.concatenate([ln_gains, ln_shifts], axis=0).astype(F32)
     ln = jnp.pad(ln, ((0, 4), (0, 0)))
     gather = functools.partial(lax.all_gather, axis_name="dp", tiled=True)
     return [
-        gather(wp, axis=0), gather(wo, axis=1)[None], gather(up_weight, axis=0),
+        gather(wp, axis=1)[None], gather(wo, axis=1)[None], gather(up_weight, axis=0),
         gather(down_weight, axis=1)[None], gather(ln, axis=1)[None],
     ]
 
@@ -257,13 +262,12 @@
 
 
 A_SUM, N2_SUM, MLP_SUM, N1_SUM = 0, 2, 4, 6
-B_CUT = 128
-
-
-def cuts_of(rows):
+
+
+def cuts_of(rows, most):
     at, cuts = 0, []
     while at < rows:
-        size = min(512, rows - at)
+        size = min(most, rows - at)
         cuts.append((at, size))
         at += size
     return cuts
@@ -294,25 +298,36 @@
     tiles = rows // 128
     p.barrier(exchange, True, True)
 
-    def tp_sum(kind, m, total):
-        i = kind + m
-        return TpSum(
-            p, half, t_mine.at[i], t_out.at[i], t_in.at[i], t_sum.at[i], total, tsend.at[i],
-            trecv.at[i],
-        )
-
-    a_sums = [tp_sum(A_SUM, m, attn.at[m]) for m in range(micro)]
-    n2_sums = [tp_sum(N2_SUM, m, n2_tot.at[m]) for m in range(micro)]
-    mlp_sums = [tp_sum(MLP_SUM, m, block.at[m]) for m in range(micro)]
-    n1_sums = [tp_sum(N1_SUM, m, n2_tot.at[m]) for m in range(micro)]
+    size = half // 2
+
+    def tp_sums(kind, m, total):
+        pieces = []
+        for q in range(2):
+            i = 2 * (kind + m) + q
+            pieces.append(TpSum(
+                p, half, q * size, size, t_mine.at[i], t_out.at[i], t_in.at[i], t_sum.at[i], total,
+                tsend.at[i], trecv.at[i],
+            ))
+        return pieces
+
+    a_sums = [tp_sums(A_SUM, m, attn.at[m]) for m in range(micro)]
+    n2_sums = [tp_sums(N2_SUM, m, n2_tot.at[m]) for m in range(micro)]
+    mlp_sums = [tp_sums(MLP_SUM, m, block.at[m]) for m in range(micro)]
+    n1_sums = [tp_sums(N1_SUM, m, n2_tot.at[m]) for m in range(micro)]
+
+    def start_both(group, partial):
+        for piece in group:
+            piece.start_other(partial)
+        for piece in group:
+            piece.start_own(partial)
 
     def tile(i, base=0):
         return pl.ds(pl.multiple_of(base + i * 128, 128), 128)
 
     if exchange:
         mine = pl.ds(pl.multiple_of(p.d * own_rows, own_rows), own_rows)
-        places = (ln.at[p.d], wp.at[mine], wo.at[p.d], wu.at[mine], wd.at[p.d])
-        sources = (ln.at[p.d], wp.at[mine], wo.at[p.d], up_s, down_s)
+        places = (ln.at[p.d], wp.at[p.d], wo.at[p.d], wu.at[mine], wd.at[p.d])
+        sources = (ln.at[p.d], wp.at[p.d], wo.at[p.d], up_s, down_s)
 
         def weight_copy(i):
             return remote(sources[i], places[i], wsend.at[i], wrecv.at[i], dp=1 - p.d)
@@ -321,16 +336,13 @@
             [gain_s[...].astype(F32), shift_s[...].astype(F32), jnp.zeros((4, cols), F32)], axis=0
         )
         weight_copy(0).start()
-        wp[mine, 0:256] = jnp.concatenate(
-            [qkv_s[0], jnp.zeros((own_rows, 64), BF16)], axis=1
-        )
-        wp[mine, 256:640] = jnp.concatenate([qkv_s[1], qkv_s[2]], axis=1)
+        for i, at in enumerate((0, 256, 448)):
+            wp[p.d, at : at + 192, :] = qkv_s[i]
+        wp[p.d, 192:256, :] = jnp.zeros((64, cols), BF16)
         weight_copy(1).start()
         wo[p.d, 0:128, :] = out_s[64:192, :]
         wo[p.d, 128:192, :] = jnp.zeros((64, cols), BF16)
         wo[p.d, 192:256, :] = out_s[0:64, :]
-        for i in range(2, 5):
-            weight_copy(i).start()
         wu[mine, :] = up_s[...]
         wd[p.d] = down_s[...]
 
@@ -347,15 +359,22 @@
             xhat, _ = normalize(hid[m, tile(i), :].astype(F32))
             h1[tile(i, m * rows), :] = (xhat * gain0 + shift0).astype(BF16)
 
-    def kv_copy(m, way, s):
+    def block_rows(b):
+        return pl.ds(pl.multiple_of(b * half, half), half)
+
+    def kv_copy(m, way, s, b):
         j, to = (c - s, c + 1) if way == 0 else (c + s, c - 1)
-        piece = kv.at[m, j]
-        return remote(piece, piece, ks.at[m, way, s], kr.at[m, way, s + 1], ctx=to)
-
-    def kv_arrival(m, way, s):
+        piece = kv.at[m, j, block_rows(b)]
+        return remote(piece, piece, ks.at[m, way, s, b], kr.at[m, way, s + 1, b], ctx=to)
+
+    def kv_arrival(m, way, s, b):
         j, to = (c - s, c - 1) if way == 0 else (c + s, c + 1)
-        piece = kv.at[m, j]
-        return remote(piece, piece, ks.at[m, way, s], kr.at[m, way, s], ctx=to)
+        piece = kv.at[m, j, block_rows(b)]
+        return remote(piece, piece, ks.at[m, way, s, b], kr.at[m, way, s, b], ctx=to)
+
+    def send_own(m, way):
+        for b in range(2):
+            kv_copy(m, way, 0, b).start()
 
     def has(way, s):
         return c - s >= 0 if way == 0 else c + s < n
@@ -366,19 +385,22 @@
         return jnp.logical_and(c + s < n, c - 1 >= 0)
 
     weight_wait(1)
+    if exchange:
+        for i in range(2, 5):
+            weight_copy(i).start()
     for m in range(micro):
         @pl.loop(0, tiles)
         def _(i, m=m):
-            packed = dot_nn(h1[tile(i, m * rows), :], wp[...])
+            packed = narrow(wp, h1[tile(i, m * rows), :])
             q = packed[:, 0:256].astype(BF16).astype(F32) * HEAD_DIM ** (-0.5)
             qs[m, tile(i), :] = q.astype(BF16)
             kv[m, c, tile(i), :] = packed[:, 256:640].astype(BF16)
 
         if m == 0:
             for way in range(2):
-                pl.when(sends(way, 0))(lambda way=way: kv_copy(0, way, 0).start())
-    pl.when(c == 0)(lambda: kv_copy(1, 0, 0).start())
-    pl.when(c == n - 1)(lambda: kv_copy(1, 1, 0).start())
+                pl.when(sends(way, 0))(lambda way=way: send_own(0, way))
+    pl.when(c == 0)(lambda: send_own(1, 0))
+    pl.when(c == n - 1)(lambda: send_own(1, 1))
 
     lanes = lax.broadcasted_iota(jnp.int32, (rows, 128), 1)
 
@@ -390,28 +412,29 @@
         qh[0], qh[1] = halves(qs[m, :, 0:128])
         qh[2] = qs[m, :, 128:256]
 
-    def attend(m, j, limits):
-        for b in range(2):
-            span = pl.ds(b * half, half)
-            k01 = kv[m, j, span, 0:128]
-            k2v0 = kv[m, j, span, 128:256]
-            t0 = k2v0.T
-            t12 = kv[m, j, span, 256:384].T
-            allowed = key_positions(border, 2 * j + b, half) <= limits
-            for h in range(3):
-                scores = dot_nt(k2v0 if h == 2 else k01, qh[h])
-                scores = jnp.where(allowed, scores, NEG)
-                old = m_row[h]
-                top = jnp.maximum(old, jnp.max(scores, axis=0, keepdims=True))
-                prob = jnp.exp(scores - top)
-                fade = jnp.exp(old - top)
-                m_row[h] = top
-                l_row[h] = l_row[h] * fade + jnp.sum(prob, axis=0, keepdims=True)
-                v_t = t0[64:128] if h == 0 else t12[(h - 1) * 64 : h * 64]
-                o_acc[h] = o_acc[h] * fade + dot_nn(v_t, prob.astype(BF16))
+    def attend(m, j, b, limits):
+        span = block_rows(b)
+        k01 = kv[m, j, span, 0:128]
+        k2v0 = kv[m, j, span, 128:256]
+        t0 = k2v0.T
+        t12 = kv[m, j, span, 256:384].T
+        allowed = key_positions(border, 2 * j + b, half) <= limits
+        for h in range(3):
+            scores = dot_nt(k2v0 if h == 2 else k01, qh[h])
+            scores = jnp.where(allowed, scores, NEG)
+            old = m_row[h]
+            top = jnp.maximum(old, jnp.max(scores, axis=0, keepdims=True))
+            prob = jnp.exp(scores - top)
+            fade = jnp.exp(old - top)
+            m_row[h] = top
+            l_row[h] = l_row[h] * fade + jnp.sum(prob, axis=0, keepdims=True)
+            v_t = t0[64:128] if h == 0 else t12[(h - 1) * 64 : h * 64]
+            o_acc[h] = o_acc[h] * fade + dot_nn(v_t, prob.astype(BF16))
+
+    steps = 4 * (n - 1) + 2
 
     def at_step(t, at, jobs):
-        @pl.when(t == min(at, 2 * n - 2))
+        @pl.when(t == at)
         def _():
             for job in jobs:
                 job()
@@ -423,20 +446,21 @@
         l_row[...] = jnp.zeros(l_row.shape, F32)
         o_acc[...] = jnp.zeros(o_acc.shape, F32)
 
-        @pl.loop(0, 2 * n - 1)
+        @pl.loop(0, steps)
         def _(t):
-            s = lax.div(t + 1, 2)
-            right = lax.rem(t, 2) == 1
-            left = jnp.logical_and(lax.rem(t, 2) == 0, t > 0)
+            own = t < 2
+            s = jnp.where(own, 0, lax.div(t + 2, 4))
+            b = jnp.where(own, t, lax.rem(lax.div(t, 2) + 1, 2))
+            right = jnp.logical_and(jnp.logical_not(own), lax.rem(t, 2) == 0)
+            left = jnp.logical_and(jnp.logical_not(own), lax.rem(t, 2) == 1)
 
             def arrive(way):
-                kv_arrival(m, way, s).wait_recv()
-                pl.when(sends(way, s))(lambda: kv_copy(m, way, s).start())
+                kv_arrival(m, way, s, b).wait_recv()
+                pl.when(sends(way, s))(lambda: kv_copy(m, way, s, b).start())
                 if m == 0:
                     last = c if way == 0 else n - 1 - c
-                    pl.when(jnp.logical_and(s == last, sends(way, 0)))(
-                        lambda: kv_copy(1, way, 0).start()
-                    )
+                    ready = jnp.logical_and(jnp.logical_and(s == last, b == 1), sends(way, 0))
+                    pl.when(ready)(lambda: send_own(1, way))
 
             pl.when(jnp.logical_and(right, has(0, s)))(lambda: arrive(0))
             pl.when(jnp.logical_and(left, has(1, s)))(lambda: arrive(1))
@@ -444,9 +468,9 @@
 
             @pl.when(jnp.logical_and(j >= 0, j < n))
             def _():
-                attend(m, j, limits)
-
-            for at, jobs in side.items():
+                attend(m, j, b, limits)
+
+            for at, jobs in side:
                 at_step(t, at, jobs)
 
         flat = pl.ds(m * rows, rows)
@@ -460,16 +484,18 @@
         heads[flat, :] = dq_t[...].T.astype(BF16)
         if m == 0:
             weight_wait(2)
-        a_sums[m].start(
-            lambda span: wide(wo, lambda w: dot_nn(heads[pl.ds(m * rows + span.start, half), :], w))
+        start_both(
+            a_sums[m],
+            lambda span: wide(wo, lambda w: dot_nn(heads[pl.ds(m * rows + span.start, size), :], w)),
         )
 
     def middle(m, i):
         return hid[m, tile(i), :].astype(F32) + BRANCH * attn[m, tile(i), :].astype(F32)
 
-    def mlp_tiles(m, first, last):
-        @pl.loop(first, last)
-        def _(i):
+    def mlp_tiles(m, q):
+        @pl.loop(0, 2)
+        def _(core):
+            i = q + (tiles // 2) * core
             flat = tile(i, m * rows)
             xhat, _ = normalize(middle(m, i))
             normed = (xhat * gain1 + shift1).astype(BF16)
@@ -482,17 +508,19 @@
             d_up[flat, :] = (narrow(wd, down_grad) * gelu_slope(up)).astype(BF16)
             block[m, tile(i), :] = wide(wd, lambda w: dot_nn(active, w)).astype(BF16)
 
-    def n2_start(m):
-        n2_sums[m].start(
-            lambda span: dot_nt(d_up[pl.ds(m * rows + span.start, half), :], wu[...])
+        n2_sums[m][q].start(
+            lambda span: dot_nt(d_up[pl.ds(m * rows + span.start, size), :], wu[...])
         )
 
     def mlp_start(m):
-        mlp_sums[m].start(lambda span: block[m, span, :])
-
-    def middle_gradient(m):
-        @pl.loop(0, tiles)
-        def _(i):
+        start_both(mlp_sums[m], lambda span: block[m, span, :])
+
+    def middle_gradient(m, q):
+        n2_sums[m][q].finish()
+
+        @pl.loop(0, 2)
+        def _(core):
+            i = q + (tiles // 2) * core
             xhat, inv = normalize(middle(m, i))
             dn = n2_tot[m, tile(i), :].astype(F32)
             grad = cot[m, tile(i), :].astype(F32) + norm_back(dn, xhat, inv, gain1)
@@ -502,8 +530,9 @@
             stats[3:4, :] += column_sums(dn)
 
     def write_block(m):
-        mlp_sums[m].finish()
-        mlp_sums[m].drain()
+        for piece in mlp_sums[m]:
+            piece.finish()
+            piece.drain()
 
         @pl.loop(0, tiles)
         def _(i):
@@ -535,14 +564,14 @@
 
     early, late, last = [], [], []
     if exchange:
-        for i, (at, size) in enumerate(cuts_of(grads.shape[1])):
-            cut = pl.ds(at, size)
+        for i, (at, count) in enumerate(cuts_of(grads.shape[1], 512)):
+            cut = pl.ds(at, count)
             early.append(GradSum(
                 p, grads.at[1 - p.d, cut], grads.at[p.d, cut], ga.at[cut], a_fu.at[cut],
                 a_fm.at[cut], gsend.at[i], grecv.at[i],
             ))
-        for i in range(own_rows // B_CUT):
-            cut, k = pl.ds(i * B_CUT, B_CUT), len(early) + i
+        for i, (at, count) in enumerate(cuts_of(640, 256)):
+            cut, k = pl.ds(at, count), len(early) + i
             late.append(GradSum(
                 p, gb_buf.at[1 - p.d, cut], gb_buf.at[p.d, cut], gb.at[cut], b_fu.at[cut],
                 b_fm.at[cut], gsend.at[k], grecv.at[k],
@@ -555,45 +584,44 @@
     def stage(group, name):
         return [getattr(piece, name) for piece in group]
 
-    def dkv_copy(m, way, j):
-        to = c + 1 if way == 0 else c - 1
+    def dkv_message(m, way, j, b, to):
         return remote(
-            sbuf.at[j], rbuf.at[m, j + 1 - way], kvs.at[m, way, j], kvr.at[m, way, j], ctx=to
+            sbuf.at[j, block_rows(b)], rbuf.at[m, j + 1 - way, block_rows(b)],
+            kvs.at[m, way, j, b], kvr.at[m, way, j, b], ctx=to,
         )
 
-    def dkv_landed(m, way, j):
-        to = c - 1 if way == 0 else c + 1
-        return remote(
-            sbuf.at[j], rbuf.at[m, j + 1 - way], kvs.at[m, way, j], kvr.at[m, way, j], ctx=to
-        )
+    def dkv_copy(m, way, j, b):
+        return dkv_message(m, way, j, b, c + 1 if way == 0 else c - 1)
+
+    def dkv_landed(m, way, j, b):
+        return dkv_message(m, way, j, b, c - 1 if way == 0 else c + 1)
 
     def upstream(way):
         return c > 0 if way == 0 else c < n - 1
 
-    def attend_back(m, j, limits):
-        for b in range(2):
-            span = pl.ds(b * half, half)
-            k01 = kv[m, j, span, 0:128]
-            k2v0 = kv[m, j, span, 128:256]
-            v12 = kv[m, j, span, 256:384]
-            t01 = k01.T
-            t2 = k2v0.T
-            allowed = key_positions(border, 2 * j + b, half) <= limits
-            sums = {}
-            for h in range(3):
-                scores = dot_nt(k2v0 if h == 2 else k01, qh[h])
-                prob = jnp.exp(jnp.where(allowed, scores, NEG) - lse[m, h : h + 1, :])
-                d_prob = dot_nt(k2v0 if h == 0 else v12, doh[h])
-                d_scores = (prob * (d_prob - delta[h])).astype(BF16)
-                dk = dot_nn(d_scores, qh[h])
-                dv = dot_nn(prob.astype(BF16), doh[h])
-                k_at, v_at = (1 if h == 2 else 0), (1 if h == 0 else 2)
-                sums[k_at] = dk if k_at not in sums else sums[k_at] + dk
-                sums[v_at] = dv if v_at not in sums else sums[v_at] + dv
-                k_t = t2[0:64] if h == 2 else t01[h * 64 : (h + 1) * 64]
-                dq_t[h * 64 : (h + 1) * 64, :] += dot_nn(k_t, d_scores)
-            for k in range(3):
-                acc[span, k * 128 : (k + 1) * 128] = sums[k]
+    def attend_back(m, j, b, limits):
+        span = block_rows(b)
+        k01 = kv[m, j, span, 0:128]
+        k2v0 = kv[m, j, span, 128:256]
+        v12 = kv[m, j, span, 256:384]
+        t01 = k01.T
+        t2 = k2v0.T
+        allowed = key_positions(border, 2 * j + b, half) <= limits
+        sums = {}
+        for h in range(3):
+            scores = dot_nt(k2v0 if h == 2 else k01, qh[h])
+            prob = jnp.exp(jnp.where(allowed, scores, NEG) - lse[m, h : h + 1, :])
+            d_prob = dot_nt(k2v0 if h == 0 else v12, doh[h])
+            d_scores = (prob * (d_prob - delta[h])).astype(BF16)
+            dk = dot_nn(d_scores, qh[h])
+            dv = dot_nn(prob.astype(BF16), doh[h])
+            k_at, v_at = (1 if h == 2 else 0), (1 if h == 0 else 2)
+            sums[k_at] = dk if k_at not in sums else sums[k_at] + dk
+            sums[v_at] = dv if v_at not in sums else sums[v_at] + dv
+            k_t = t2[0:64] if h == 2 else t01[h * 64 : (h + 1) * 64]
+            dq_t[h * 64 : (h + 1) * 64, :] += dot_nn(k_t, d_scores)
+        for k in range(3):
+            acc[span, k * 128 : (k + 1) * 128] = sums[k]
 
     def backward(m, side):
         flat = pl.ds(m * rows, rows)
@@ -602,152 +630,169 @@
         d_heads = narrow(wo, upper).astype(BF16)
         doh[0] = d_heads[:, 128:256]
         doh[1], doh[2] = halves(d_heads[:, 0:128])
-        size = wo.shape[2]
-        d_heads_t = dot_nt(wo[0], upper[:, 0:size])
+        share = wo.shape[2]
+        d_heads_t = dot_nt(wo[0], upper[:, 0:share])
         for i in range(1, wo.shape[0]):
-            d_heads_t += dot_nt(wo[i], upper[:, i * size : (i + 1) * size])
+            d_heads_t += dot_nt(wo[i], upper[:, i * share : (i + 1) * share])
         for h in range(3):
             at = 192 if h == 0 else (h - 1) * 64
             delta[h] = jnp.sum(d_heads_t[at : at + 64] * o_t[m, h], axis=0, keepdims=True)
         split_queries(m)
         dq_t[...] = jnp.zeros(dq_t.shape, F32)
 
-        @pl.loop(0, 2 * n - 1)
+        @pl.loop(0, steps)
         def _(t):
-            s = n - 1 - lax.div(t, 2)
-            own = t == 2 * n - 2
+            own = t >= steps - 2
+            s = n - 1 - lax.div(t, 4)
+            b = jnp.where(own, t - (steps - 2), lax.rem(lax.div(t, 2), 2))
             right = jnp.logical_and(lax.rem(t, 2) == 0, jnp.logical_not(own))
-            j = jnp.where(right, c + s, c - s)
+            left = jnp.logical_and(lax.rem(t, 2) == 1, jnp.logical_not(own))
+            j = jnp.where(own, c, jnp.where(right, c + s, c - s))
+            span = block_rows(b)
+
+            for at, jobs in side:
+                at_step(t, at, jobs)
 
             @pl.when(jnp.logical_and(j >= 0, j < n))
             def _():
-                attend_back(m, j, limits)
+                attend_back(m, j, b, limits)
 
                 def pass_on(way):
                     if m > 0:
-                        dkv_copy(m - 1, way, j).wait_send()
+                        dkv_copy(m - 1, way, j, b).wait_send()
 
                     @pl.when(upstream(way))
                     def _():
-                        dkv_landed(m, way, j).wait_recv()
-                        sbuf[j] = (acc[...] + rbuf[m, j + 1 - way].astype(F32)).astype(BF16)
+                        dkv_landed(m, way, j, b).wait_recv()
+                        sbuf[j, span, :] = (
+                            acc[span, :] + rbuf[m, j + 1 - way, span, :].astype(F32)
+                        ).astype(BF16)
 
                     @pl.when(jnp.logical_not(upstream(way)))
                     def _():
-                        sbuf[j] = acc[...].astype(BF16)
-
-                    dkv_copy(m, way, j).start()
+                        sbuf[j, span, :] = acc[span, :].astype(BF16)
+
+                    dkv_copy(m, way, j, b).start()
 
                 pl.when(right)(lambda: pass_on(0))
-                pl.when(jnp.logical_and(jnp.logical_not(right), jnp.logical_not(own)))(
-                    lambda: pass_on(1)
-                )
-
-            for at, jobs in side.items():
-                at_step(t, at, jobs)
-
-        @pl.when(upstream(0))
-        def _():
-            dkv_landed(m, 0, c).wait_recv()
-            acc[...] += rbuf[m, c + 1].astype(F32)
-
-        @pl.when(upstream(1))
-        def _():
-            dkv_landed(m, 1, c).wait_recv()
-            acc[...] += rbuf[m, c].astype(F32)
+                pl.when(left)(lambda: pass_on(1))
+
+        for way in range(2):
+            @pl.when(upstream(way))
+            def _(way=way):
+                for b in range(2):
+                    span = block_rows(b)
+                    dkv_landed(m, way, c, b).wait_recv()
+                    acc[span, :] += rbuf[m, c + 1 - way, span, :].astype(F32)
 
         d_pack[flat, 256:640] = acc[...].astype(BF16)
         d_pack[flat, 0:256] = (dq_t[...].T * HEAD_DIM ** (-0.5)).astype(BF16)
-        n1_sums[m].start(
-            lambda span: dot_nt(d_pack[pl.ds(m * rows + span.start, half), :], wp[...])
+        start_both(
+            n1_sums[m],
+            lambda span: wide(wp, lambda w: dot_nn(d_pack[pl.ds(m * rows + span.start, size), :], w)),
         )
 
-    def finish_rows(m):
-        @pl.loop(0, tiles)
-        def _(i):
+    def finish_rows(m, q):
+        n1_sums[m][q].finish()
+
+        @pl.loop(0, 2)
+        def _(core):
+            i = q + (tiles // 2) * core
             xhat, inv = normalize(hid[m, tile(i), :].astype(F32))
             dn = n2_tot[m, tile(i), :].astype(F32)
             grad_in[m, tile(i), :] += norm_back(dn, xhat, inv, gain0)
             stats[0:1, :] += column_sums(dn * xhat)
             stats[2:3, :] += column_sums(dn)
 
-    def pack_tile(k, i):
-        return dot_tn(h1[:, tile(i, k * own_rows)], d_pack[...])
+    def pack_tile(k, at, count):
+        left = h1[:, pl.ds(pl.multiple_of(k * cols, 128), cols)]
+        return dot_tn(d_pack[:, at : at + count], left)
 
     def do(jobs):
         for job in jobs:
             job()
 
+    def each(group, name):
+        return lambda: do(stage(group, name))
+
+    def middle_ready(m):
+        for q in range(2):
+            middle_gradient(m, q)
+        for piece in n2_sums[m]:
+            piece.drain()
+
+    def mlp_piece(m, q):
+        a_sums[m][q].finish()
+        mlp_tiles(m, q)
+
+    def by_place(at_end, inside):
+        return jnp.where(jnp.logical_or(c == 0, c == n - 1), at_end, inside)
+
     stats[...] = jnp.zeros(stats.shape, F32)
-    a0, a1 = a_sums
-    x0, x1 = n2_sums
-    u0, u1 = mlp_sums
-    y0, y1 = n1_sums
-    forward(0, {})
-    forward(1, {
-        0: [a0.step2],
-        2: [a0.step3, a0.finish, lambda: weight_wait(3, 4), lambda: mlp_tiles(0, 0, tiles // 2)],
-        4: [lambda: mlp_tiles(0, tiles // 2, tiles), lambda: n2_start(0)],
-        6: [x0.step2],
-    })
-    a1.step2()
-    x0.step3()
-    x0.finish()
-    middle_gradient(0)
-    x0.drain()
-    backward(0, {
-        0: [lambda: mlp_start(0)],
-        1: [a1.step3],
-        2: [a1.finish, lambda: mlp_tiles(1, 0, tiles // 2)],
-        3: [u0.step2, lambda: mlp_tiles(1, tiles // 2, tiles), lambda: n2_start(1)],
-        4: [x1.step2, down_gradient] + stage(early[0:1], "s0"),
-        5: [up_gradient] + stage(early[1:3], "s0"),
-        6: [u0.step3, lambda: mlp_start(1), x1.step3],
-    })
-    x1.finish()
-    middle_gradient(1)
-    x1.drain()
+    (a0, a1), (x0, x1), (u0, u1), (y0, y1) = a_sums, n2_sums, mlp_sums, n1_sums
+    forward(0, [])
+    forward(1, [
+        (0, [each(a0, "step2")]),
+        (3, [a0[0].step3]),
+        (5, [lambda: weight_wait(3, 4), lambda: mlp_piece(0, 0), a0[1].step3]),
+        (7, [x0[0].step2, lambda: mlp_piece(0, 1)]),
+        (9, [x0[1].step2]),
+    ])
+    do(stage(x0, "step3"))
+    do(stage(a1, "step2"))
+    middle_ready(0)
+    spot = by_place(5, 0)
+    backward(0, [
+        (spot, [a1[0].step3, a1[1].step3, lambda: mlp_piece(1, 0), lambda: mlp_piece(1, 1)]),
+        (spot + 2, [each(x1, "step2"), lambda: mlp_start(0)]),
+        (spot + 4, [down_gradient, each(early[0:1], "s0")]),
+        (spot + 6, [up_gradient, each(early[1:3], "s0"), each(u0, "step2"), each(x1, "step3")]),
+        (steps - 1, [lambda: mlp_start(1)]),
+    ])
+    middle_ready(1)
     out_gradient()
     do(stage(early[3:], "s0"))
-    backward(1, {
-        0: [y0.step2, u1.step2],
-        2: stage(early[0:1], "s1"),
-        3: [y0.step3] + stage(early[1:2], "s1"),
-        4: stage(early[2:3], "s1") + stage(early[0:1], "s2"),
-        5: [u1.step3] + stage(early[3:], "s1") + stage(early[1:2], "s2"),
-        6: stage(early[2:], "s2") + stage(early[0:2], "s3"),
-    })
+    backward(1, [
+        (0, [each(y0, "step2"), each(u0, "step3")]),
+        (by_place(0, steps - 1), [each(early[0:2], "s1")]),
+        (steps - 3, [each(u1, "step2"), each(y0, "step3")]),
+        (by_place(steps - 1, steps), [each(early[2:], "s1")]),
+    ])
     if exchange:
-        for i in range(len(late)):
-            gb_buf[1 - p.d, i * B_CUT : (i + 1) * B_CUT, :] = pack_tile(1 - p.d, i).astype(BF16)
-            late[i].s0()
-        for i in range(len(late)):
-            gb_buf[p.d, i * B_CUT : (i + 1) * B_CUT, :] = pack_tile(p.d, i).astype(BF16)
+        for piece, (at, count) in zip(late, cuts_of(640, 256)):
+            gb_buf[1 - p.d, at : at + count, :] = pack_tile(1 - p.d, at, count).astype(BF16)
+            piece.s0()
+        do(stage(early[0:2], "s2"))
+        for at, count in cuts_of(640, 256):
+            gb_buf[p.d, at : at + count, :] = pack_tile(p.d, at, count).astype(BF16)
     else:
-        @pl.loop(0, width // 128)
-        def _(i):
-            gb[tile(i), :] = pack_tile(0, i)
-    y1.step2()
-    y0.finish()
-    finish_rows(0)
-    do(stage(late[0:2], "s1"))
+        for at, count in cuts_of(640, 128):
+            gb[at : at + count, :] = pack_tile(0, at, count)
+    do(stage(y1, "step2"))
+    do(stage(u1, "step3"))
+    for q in range(2):
+        finish_rows(0, q)
+    if exchange:
+        @pl.when(by_place(0, 1) == 1)
+        def _():
+            do(stage(early[2:], "s1"))
     write_block(0)
-    do(stage(late[2:], "s1"))
-    y1.step3()
-    do(stage(late[0:2], "s2"))
+    do(stage(late, "s1"))
+    do(stage(early[2:], "s2"))
+    do(stage(y1, "step3"))
     write_block(1)
-    do(stage(late[2:], "s2"))
-    y1.finish()
-    finish_rows(1)
+    for q in range(2):
+        finish_rows(1, q)
     if exchange:
         for k in range(2):
             cut = slice(k * cols, (k + 1) * cols)
             gs_buf[k] = jnp.concatenate([stats[:, cut], jnp.zeros((8, cols), F32)], axis=0).astype(BF16)
         do(stage(last, "s0"))
-        do(stage(early[2:], "s3"))
+        do(stage(late, "s2"))
         do(stage(last, "s1"))
+        do(stage(early, "s3"))
+        do(stage(last, "s2"))
         do(stage(late, "s3"))
-        do(stage(last, "s2"))
         do(stage(last, "s3"))
         for piece in early + late + last:
             piece.drain()
@@ -755,15 +800,18 @@
             weight_copy(i).wait_send()
     else:
         gs[...] = stats[...]
-    for m in range(micro):
-        for way in range(2):
-            for s in range(n - 1):
-                pl.when(sends(way, s))(lambda m=m, way=way, s=s: kv_copy(m, way, s).wait_send())
-        a_sums[m].drain()
-        n1_sums[m].drain()
-    for j in range(n):
-        pl.when(c < j)(lambda j=j: dkv_copy(micro - 1, 0, j).wait_send())
-        pl.when(c > j)(lambda j=j: dkv_copy(micro - 1, 1, j).wait_send())
+    for b in range(2):
+        for m in range(micro):
+            for way in range(2):
+                for s in range(n - 1):
+                    pl.when(sends(way, s))(
+                        lambda m=m, way=way, s=s, b=b: kv_copy(m, way, s, b).wait_send()
+                    )
+        for j in range(n):
+            pl.when(c < j)(lambda j=j, b=b: dkv_copy(micro - 1, 0, j, b).wait_send())
+            pl.when(c > j)(lambda j=j, b=b: dkv_copy(micro - 1, 1, j, b).wait_send())
+    for piece in a0 + a1 + y0 + y1:
+        piece.drain()
 
 
 def run_block(n_ctx, exchange, prefix, border, hid, cot, weights, ff):
@@ -779,20 +827,20 @@
     outs = [sds((micro, rows, width), BF16), sds((micro, rows, width), F32)]
     scratch = []
     if exchange:
-        outs += [sds((grad_rows, cols), BF16), sds((cols, 640), BF16), sds((16, cols), BF16)]
-        pieces = len(cuts_of(grad_rows)) + cols // B_CUT + 1
+        outs += [sds((grad_rows, cols), BF16), sds((640, cols), BF16), sds((16, cols), BF16)]
+        pieces = len(cuts_of(grad_rows, 512)) + len(cuts_of(640, 256)) + 1
         scratch += [
-            vmem((width, 640), BF16), vmem((2, 256, cols), BF16), vmem((width, ff), BF16),
+            vmem((2, 640, cols), BF16), vmem((2, 256, cols), BF16), vmem((width, ff), BF16),
             vmem((2, ff, cols), BF16), vmem((2, 8, cols), F32),
-            vmem((2, grad_rows, cols), BF16), vmem((2, cols, 640), BF16), vmem((2, 16, cols), BF16),
-            vmem((cols, 640), BF16), vmem((cols, 640), BF16),
+            vmem((2, grad_rows, cols), BF16), vmem((2, 640, cols), BF16), vmem((2, 16, cols), BF16),
+            vmem((640, cols), BF16), vmem((640, cols), BF16),
             vmem((grad_rows, cols), BF16), vmem((grad_rows, cols), BF16),
             vmem((16, cols), BF16), vmem((16, cols), BF16),
             sems((5,)), sems((5,)), sems((pieces, 4)), sems((pieces, 4)),
         ]
     else:
         outs += [
-            sds((1, grad_rows, cols), BF16), sds((width, 640), F32), sds((8, width), F32)
+            sds((1, grad_rows, cols), BF16), sds((640, width), F32), sds((8, width), F32)
         ]
     scratch += [
         vmem((micro, rows, width), BF16), vmem((total, 256), BF16), vmem((micro, 8, rows), F32),
@@ -805,10 +853,10 @@
         vmem((rows, 384), F32), vmem((3, rows, 128), BF16), vmem((3, rows, 128), BF16),
         vmem((256, rows), F32), vmem((3, 1, rows), F32), vmem((total, 640), BF16),
         vmem((8, width), F32),
-        sems((micro, 2, n_ctx + 1)), sems((micro, 2, n_ctx + 1)),
-        sems((micro, 2, n_ctx)), sems((micro, 2, n_ctx)),
+        sems((micro, 2, n_ctx + 1, 2)), sems((micro, 2, n_ctx + 1, 2)),
+        sems((micro, 2, n_ctx, 2)), sems((micro, 2, n_ctx, 2)),
     ]
-    scratch += [vmem((8, half, width), BF16)] * 4 + [sems((8, 3))] * 2
+    scratch += [vmem((16, half // 2, width), BF16)] * 4 + [sems((16, 3))] * 2
     smem = pl.BlockSpec(memory_space=pltpu.SMEM)
     return pl.pallas_call(
         functools.partial(block_kernel, n_ctx, exchange),
@@ -824,16 +872,15 @@
 
 
 def unpack_kernel(ff, ga, gb, gs, qkv, out, up, down, gains, shifts):
-    rows, cols = qkv.shape[1], ga.shape[1]
+    rows, cols = qkv.shape[2], ga.shape[1]
     down[...] = ga[0:ff, :].astype(F32)
     for k in range(ff // cols):
         up[:, k * cols : (k + 1) * cols] = ga[ff + k * rows : ff + (k + 1) * rows, :].astype(F32)
     at = ff + rows * (ff // cols)
     out[0:64, :] = ga[at + 192 : at + 256, :].astype(F32)
     out[64:192, :] = ga[at : at + 128, :].astype(F32)
-    qkv[0] = gb[:, 0:192].astype(F32)
-    qkv[1] = gb[:, 256:448].astype(F32)
-    qkv[2] = gb[:, 384:640].astype(F32)[:, 64:256]
+    for i, at in enumerate((0, 256, 448)):
+        qkv[i] = gb[at : at + 192, :].astype(F32)
     gains[...] = gs[...].astype(F32)[0:2]
     shifts[...] = gs[...].astype(F32)[2:4]
 
@@ -847,25 +894,27 @@
     exchange = lax.axis_size("dp") == 2 and n_ctx % 2 == 0
     ff = up_weight.shape[1]
     params = (qkv_weight, out_weight, up_weight, down_weight, ln_gains, ln_shifts)
-    weights = params if exchange else pack_weights(*params)
+    turned = jnp.swapaxes(qkv_weight, 1, 2)
+    weights = (turned,) + params[1:] if exchange else pack_weights(*params)
     hid, cot = hidden_in[:, 0], cotangent[:, 0]
     block, grad_in, ga, gb, gs = run_block(
-        n_ctx, exchange, prefix, block_order, hid, cot, weights, ff
+        n_ctx, exchange, prefix[:, 0], block_order, hid, cot, weights, ff
     )
     if exchange:
         owned = pl.pallas_call(
             functools.partial(unpack_kernel, ff),
-            out_shape=[jax.ShapeDtypeStruct(w.shape, F32) for w in params],
+            out_shape=[jax.ShapeDtypeStruct(w.shape, F32) for w in (turned,) + params[1:]],
             in_specs=vmem_specs(3),
             out_specs=vmem_specs(6),
             name="unpack_gradients",
         )(ga, gb, gs)
+        owned = [jnp.swapaxes(owned[0], 1, 2)] + list(owned[1:])
     else:
         ga = ga[0].astype(F32)
         g_out = ga[ff + width :]
         whole = lax.psum(
             (
-                jnp.stack([gb[:, 0:192], gb[:, 256:448], gb[:, 448:640]]),
+                jnp.swapaxes(jnp.stack([gb[0:192], gb[256:448], gb[448:640]]), 1, 2),
                 jnp.concatenate([g_out[192:], g_out[:128]], axis=0), ga[ff : ff + width], ga[:ff],
                 gs[0:2], gs[2:4],
             ),

time: 270 us -> 220 us (0.81)
  Pallas kernels: 259 us -> 215 us
  local copies, waits for them, and re-layouts: 10 us -> 4.12 us
    pallas_call x1, Pallas kernels: 256 us -> 212 us  [run_block(): pl.pallas_call(functools.partial(block_kernel, n_ctx, exchange), out_shap...]
    unnamed x9 -> x6, local copies, waits for them, and re-layouts: 10 us -> 4.12 us
where the time goes in v4:
time: 220 us
  Pallas kernels  215 us (98%)
  local copies, waits for them, and re-layouts  4.12 us (2%)
    pallas_call x1, Pallas kernels, run_block(): pl.pallas_call(functools.partial(block_kernel, n_ctx, exchange), out_shap...  212 us

profile of v4, /device:TPU:0, one launch (start us, length us, event | category | flops | bytes accessed | tf_op | source)
XLA Modules:
  0.0 220.1 jit_solution(17936790142029434214)
XLA Ops:
  0.6 211.9 %block_both_ways.1 = (bf16[2,512,768]{2,1,0:T(8,128)(2,1)}, f32[2,512,768]{2,1,0:T(8,128)}, bf16[1792,384]{1,0:T(8,128)(2,1)}, bf16[640,384]{1,0:T(8,128)(2,1)}, bf16[16,384]{1,0:T(8,128)(2,1)}) custom-call(s32[2]{0:T(128)} %bitcast.16, s32[8]{0:T(128)} %border.1, bf16[2,512,768]{2,1,0:T(8,128)(2,1)} %bitcast.13, bf16[2,512,768]{2,1,0:T(8,128)(2,1)} %bitcast.14, ...), custom_call_target="tpu_custom_call" | custom-call | tf_op jit(solution)/shard_map/block_both_ways/pallas_call | solution.py:861
  212.5 0.0 copy-start.1
  212.5 3.5 %unpack_gradients.1 = (f32[3,192,384]{2,1,0:T(8,128)}, f32[192,384]{1,0:T(8,128)}, f32[384,768]{1,0:T(8,128)}, f32[768,384]{1,0:T(8,128)}, f32[2,384]{1,0:T(2,128)}, /*index=5*/f32[2,384]{1,0:T(2,128)}) custom-call(bf16[1792,384]{1,0:T(8,128)(2,1)} %get-tuple-element.21.ga, bf16[640,384]{1,0:T(8,128)(2,1)} %get-tuple-element.22.gb, ...), custom_call_target="tpu_custom_call" | custom-call | tf_op jit(solution)/shard_map/unpack_gradients/pallas_call | solution.py:904
  216.0 0.0 copy-done.1
  216.0 0.0 copy-start
  216.0 1.1 copy.22
  217.2 1.3 copy-done
  218.5 1.7 copy.23
Async XLA Ops:
  212.5 3.5 %copy-start.1 = (bf16[2,512,768]{2,1,0:T(8,128)(2,1)S(1)}, bf16[2,512,768]{2,1,0:T(8,128)(2,1)}, u32[]{:S(2)}) copy-start(bf16[2,512,768]{2,1,0:T(8,128)(2,1)} %get-tuple-element.19) | copy-start | bytes 4718596
  216.0 2.5 %copy-start = (f32[2,512,768]{2,1,0:T(8,128)S(1)}, f32[2,512,768]{2,1,0:T(8,128)}, u32[]{:S(2)}) copy-start(f32[2,512,768]{2,1,0:T(8,128)} %get-tuple-element.20) | copy-start | bytes 9437188

commit v5 on v4

--- a/solution.py
+++ b/solution.py
@@ -172,11 +172,12 @@
     return jnp.concatenate([fn(ref_stack[i]) for i in range(ref_stack.shape[0])], axis=1)
 
 
-def narrow(ref_stack, value):
+def narrow(ref_stack, value, at=0, count=None):
     size = ref_stack.shape[2]
-    total = dot_nt(value[:, 0:size], ref_stack[0])
+    span = pl.ds(at, ref_stack.shape[1] if count is None else count)
+    total = dot_nt(value[:, 0:size], ref_stack[0, span, :])
     for i in range(1, ref_stack.shape[0]):
-        total += dot_nt(value[:, i * size : (i + 1) * size], ref_stack[i])
+        total += dot_nt(value[:, i * size : (i + 1) * size], ref_stack[i, span, :])
     return total
 
 
@@ -261,6 +262,8 @@
         pl.when(jnp.logical_not(self.end))(lambda: self.down_copy().wait_send())
 
 
+EARLY_ROWS = 384
+PACK_CUTS = ((0, 256, 0, 192), (256, 256, 192, 256), (512, 128, 448, 128))
 A_SUM, N2_SUM, MLP_SUM, N1_SUM = 0, 2, 4, 6
 
 
@@ -285,7 +288,7 @@
         (block, grad_in, grads, gb, gs) = refs[5:10]
         refs = refs[10:]
     (attn, heads, lse, o_t, qs, kv, h1, m_row, l_row, o_acc, act, d_mlp, d_up, h2, n2_tot, d_attn,
-     sbuf, rbuf, acc, qh, doh, dq_t, delta, d_pack, stats, ks, kr, kvs, kvr,
+     sbuf, rbuf, q_all, do_all, st_all, qos, qor, acc, qh, doh, dq_t, delta, d_pack, stats, ks, kr, kvs, kvr,
      t_mine, t_out, t_in, t_sum, tsend, trecv) = refs
     p = Place(n_ctx)
     c, n = p.c, n_ctx
@@ -326,8 +329,9 @@
 
     if exchange:
         mine = pl.ds(pl.multiple_of(p.d * own_rows, own_rows), own_rows)
-        places = (ln.at[p.d], wp.at[p.d], wo.at[p.d], wu.at[mine], wd.at[p.d])
-        sources = (ln.at[p.d], wp.at[p.d], wo.at[p.d], up_s, down_s)
+        kv_part, q_part = wp.at[p.d, pl.ds(256, 384)], wp.at[p.d, pl.ds(0, 192)]
+        places = (ln.at[p.d], kv_part, q_part, wo.at[p.d], wu.at[mine], wd.at[p.d])
+        sources = (ln.at[p.d], kv_part, q_part, wo.at[p.d], up_s, down_s)
 
         def weight_copy(i):
             return remote(sources[i], places[i], wsend.at[i], wrecv.at[i], dp=1 - p.d)
@@ -336,10 +340,12 @@
             [gain_s[...].astype(F32), shift_s[...].astype(F32), jnp.zeros((4, cols), F32)], axis=0
         )
         weight_copy(0).start()
-        for i, at in enumerate((0, 256, 448)):
-            wp[p.d, at : at + 192, :] = qkv_s[i]
-        wp[p.d, 192:256, :] = jnp.zeros((64, cols), BF16)
+        wp[p.d, 256:448, :] = qkv_s[1]
+        wp[p.d, 448:640, :] = qkv_s[2]
         weight_copy(1).start()
+        wp[p.d, 0:192, :] = qkv_s[0]
+        for k in range(2):
+            wp[k, 192:256, :] = jnp.zeros((64, cols), BF16)
         wo[p.d, 0:128, :] = out_s[64:192, :]
         wo[p.d, 128:192, :] = jnp.zeros((64, cols), BF16)
         wo[p.d, 192:256, :] = out_s[0:64, :]
@@ -386,21 +392,29 @@
 
     weight_wait(1)
     if exchange:
-        for i in range(2, 5):
+        weight_copy(2).start()
+    for m in range(micro):
+        @pl.loop(0, 2)
+        def _(b, m=m):
+            for i in range(tiles // 2):
+                span = pl.ds(pl.multiple_of(b * half + i * 128, 128), 128)
+                flat = pl.ds(pl.multiple_of(m * rows + b * half + i * 128, 128), 128)
+                kv[m, c, span, :] = narrow(wp, h1[flat, :], 256, 384).astype(BF16)
+            if m == 0:
+                for way in range(2):
+                    pl.when(sends(way, 0))(lambda way=way: kv_copy(0, way, 0, b).start())
+
+    pl.when(c == 0)(lambda: send_own(1, 0))
+    pl.when(c == n - 1)(lambda: send_own(1, 1))
+    weight_wait(2)
+    if exchange:
+        for i in range(3, 6):
             weight_copy(i).start()
     for m in range(micro):
         @pl.loop(0, tiles)
         def _(i, m=m):
-            packed = narrow(wp, h1[tile(i, m * rows), :])
-            q = packed[:, 0:256].astype(BF16).astype(F32) * HEAD_DIM ** (-0.5)
-            qs[m, tile(i), :] = q.astype(BF16)
-            kv[m, c, tile(i), :] = packed[:, 256:640].astype(BF16)
-
-        if m == 0:
-            for way in range(2):
-                pl.when(sends(way, 0))(lambda way=way: send_own(0, way))
-    pl.when(c == 0)(lambda: send_own(1, 0))
-    pl.when(c == n - 1)(lambda: send_own(1, 1))
+            q = narrow(wp, h1[tile(i, m * rows), :], 0, 256).astype(BF16).astype(F32)
+            qs[m, tile(i), :] = (q * HEAD_DIM ** (-0.5)).astype(BF16)
 
     lanes = lax.broadcasted_iota(jnp.int32, (rows, 128), 1)
 
@@ -483,7 +497,7 @@
             dq_t[at : at + 64, :] = norm
         heads[flat, :] = dq_t[...].T.astype(BF16)
         if m == 0:
-            weight_wait(2)
+            weight_wait(3)
         start_both(
             a_sums[m],
             lambda span: wide(wo, lambda w: dot_nn(heads[pl.ds(m * rows + span.start, size), :], w)),
@@ -558,20 +572,20 @@
     def out_gradient():
         at = ff + own_rows * (ff // cols)
         for k in range(parts):
-            grads[k, at : at + 256, :] = dot_tn(
-                heads[...], d_attn[:, k * cols : (k + 1) * cols]
-            ).astype(BF16)
+            value = dot_tn(heads[...], d_attn[:, k * cols : (k + 1) * cols]).astype(BF16)
+            grads[k, at : at + 128, :] = value[0:128]
+            grads[k, at + 128 : at + 192, :] = value[192:256]
 
     early, late, last = [], [], []
     if exchange:
-        for i, (at, count) in enumerate(cuts_of(grads.shape[1], 512)):
+        for i, (at, count) in enumerate(cuts_of(grads.shape[1], EARLY_ROWS)):
             cut = pl.ds(at, count)
             early.append(GradSum(
                 p, grads.at[1 - p.d, cut], grads.at[p.d, cut], ga.at[cut], a_fu.at[cut],
                 a_fm.at[cut], gsend.at[i], grecv.at[i],
             ))
-        for i, (at, count) in enumerate(cuts_of(640, 256)):
-            cut, k = pl.ds(at, count), len(early) + i
+        for i, (_, _, to, count) in enumerate(PACK_CUTS):
+            cut, k = pl.ds(to, count), len(early) + i
             late.append(GradSum(
                 p, gb_buf.at[1 - p.d, cut], gb_buf.at[p.d, cut], gb.at[cut], b_fu.at[cut],
                 b_fm.at[cut], gsend.at[k], grecv.at[k],
@@ -584,22 +598,52 @@
     def stage(group, name):
         return [getattr(piece, name) for piece in group]
 
-    def dkv_message(m, way, j, b, to):
+    def dkv_message(way, j, b, to):
         return remote(
-            sbuf.at[j, block_rows(b)], rbuf.at[m, j + 1 - way, block_rows(b)],
-            kvs.at[m, way, j, b], kvr.at[m, way, j, b], ctx=to,
+            sbuf.at[j, block_rows(b)], rbuf.at[j + 1 - way, block_rows(b)],
+            kvs.at[way, j, b], kvr.at[way, j, b], ctx=to,
         )
 
-    def dkv_copy(m, way, j, b):
-        return dkv_message(m, way, j, b, c + 1 if way == 0 else c - 1)
-
-    def dkv_landed(m, way, j, b):
-        return dkv_message(m, way, j, b, c - 1 if way == 0 else c + 1)
+    def dkv_copy(way, j, b):
+        return dkv_message(way, j, b, c + 1 if way == 0 else c - 1)
+
+    def dkv_landed(way, j, b):
+        return dkv_message(way, j, b, c - 1 if way == 0 else c + 1)
+
+    gathered = (q_all, do_all, st_all)
+
+    def qo_copy(kind, way, s):
+        j, to = (c - s, c + 1) if way == 0 else (c + s, c - 1)
+        piece = gathered[kind].at[j]
+        return remote(piece, piece, qos.at[kind, way, s], qor.at[kind, way, s + 1], ctx=to)
+
+    def qo_arrival(kind, way, s):
+        j, to = (c - s, c - 1) if way == 0 else (c + s, c + 1)
+        piece = gathered[kind].at[j]
+        return remote(piece, piece, qos.at[kind, way, s], qor.at[kind, way, s], ctx=to)
+
+    def qo_send(kind):
+        for way in range(2):
+            pl.when(sends(way, 0))(lambda way=way: qo_copy(kind, way, 0).start())
+
+    def qo_step(kind, way, s):
+        @pl.when(has(way, s))
+        def _():
+            qo_arrival(kind, way, s).wait_recv()
+            pl.when(sends(way, s))(lambda: qo_copy(kind, way, s).start())
+
+    def qo_steps(kind, s):
+        for way in range(2):
+            qo_step(kind, way, s)
+
+    def send_queries(m):
+        q_all[c] = qs[m].T[0:192]
+        qo_send(0)
 
     def upstream(way):
         return c > 0 if way == 0 else c < n - 1
 
-    def attend_back(m, j, b, limits):
+    def attend_back(m, j, b, limits, keys_too=True):
         span = block_rows(b)
         k01 = kv[m, j, span, 0:128]
         k2v0 = kv[m, j, span, 128:256]
@@ -613,23 +657,40 @@
             prob = jnp.exp(jnp.where(allowed, scores, NEG) - lse[m, h : h + 1, :])
             d_prob = dot_nt(k2v0 if h == 0 else v12, doh[h])
             d_scores = (prob * (d_prob - delta[h])).astype(BF16)
-            dk = dot_nn(d_scores, qh[h])
-            dv = dot_nn(prob.astype(BF16), doh[h])
-            k_at, v_at = (1 if h == 2 else 0), (1 if h == 0 else 2)
-            sums[k_at] = dk if k_at not in sums else sums[k_at] + dk
-            sums[v_at] = dv if v_at not in sums else sums[v_at] + dv
             k_t = t2[0:64] if h == 2 else t01[h * 64 : (h + 1) * 64]
             dq_t[h * 64 : (h + 1) * 64, :] += dot_nn(k_t, d_scores)
-        for k in range(3):
+            if keys_too:
+                dk = dot_nn(d_scores, qh[h])
+                dv = dot_nn(prob.astype(BF16), doh[h])
+                k_at, v_at = (1 if h == 2 else 0), (1 if h == 0 else 2)
+                sums[k_at] = dk if k_at not in sums else sums[k_at] + dk
+                sums[v_at] = dv if v_at not in sums else sums[v_at] + dv
+        for k in sums:
             acc[span, k * 128 : (k + 1) * 128] = sums[k]
 
-    def backward(m, side):
-        flat = pl.ds(m * rows, rows)
-        limits = query_limits(border, prefix, m, c, rows)
-        upper = d_attn[flat, :]
-        d_heads = narrow(wo, upper).astype(BF16)
-        doh[0] = d_heads[:, 128:256]
-        doh[1], doh[2] = halves(d_heads[:, 0:128])
+    def attend_keys(m, j, b):
+        span = block_rows(b)
+        k01 = kv[m, c, span, 0:128]
+        k2v0 = kv[m, c, span, 128:256]
+        v12 = kv[m, c, span, 256:384]
+        limits = query_limits(border, prefix, m, j, rows)
+        allowed = key_positions(border, 2 * c + b, half) <= limits
+        zero = jnp.zeros((64, rows), BF16)
+        for h in range(3):
+            q_h = q_all[j, h * 64 : (h + 1) * 64, :]
+            q_h = jnp.concatenate([zero, q_h] if h == 1 else [q_h, zero], axis=0)
+            do_h = do_all[j, h * 64 : (h + 1) * 64, :]
+            do_h = jnp.concatenate([do_h, zero] if h == 1 else [zero, do_h], axis=0)
+            scores = dot_nn(k2v0 if h == 2 else k01, q_h)
+            prob = jnp.exp(jnp.where(allowed, scores, NEG) - st_all[j, h : h + 1, :])
+            d_prob = dot_nn(k2v0 if h == 0 else v12, do_h)
+            d_scores = (prob * (d_prob - st_all[j, 3 + h : 4 + h, :])).astype(BF16)
+            k_at, v_at = (128 if h == 2 else 0), (128 if h == 0 else 256)
+            acc[span, k_at : k_at + 128] += dot_nt(d_scores, q_h)
+            acc[span, v_at : v_at + 128] += dot_nt(prob.astype(BF16), do_h)
+
+    def head_gradients(m):
+        upper = d_attn[pl.ds(m * rows, rows), :]
         share = wo.shape[2]
         d_heads_t = dot_nt(wo[0], upper[:, 0:share])
         for i in range(1, wo.shape[0]):
@@ -637,8 +698,32 @@
         for h in range(3):
             at = 192 if h == 0 else (h - 1) * 64
             delta[h] = jnp.sum(d_heads_t[at : at + 64] * o_t[m, h], axis=0, keepdims=True)
+            if m > 0:
+                do_all[c, h * 64 : (h + 1) * 64, :] = d_heads_t[at : at + 64].astype(BF16)
+                st_all[c, h : h + 1, :] = lse[m, h : h + 1, :]
+                st_all[c, 3 + h : 4 + h, :] = delta[h]
+        if m > 0:
+            st_all[c, 6:8, :] = jnp.zeros((2, rows), F32)
+            qo_send(2)
+            qo_send(1)
+        d_heads = narrow(wo, upper).astype(BF16)
+        doh[0] = d_heads[:, 128:256]
+        doh[1], doh[2] = halves(d_heads[:, 0:128])
         split_queries(m)
         dq_t[...] = jnp.zeros(dq_t.shape, F32)
+
+    def backward_end(m):
+        flat = pl.ds(m * rows, rows)
+        d_pack[flat, 256:640] = acc[...].astype(BF16)
+        d_pack[flat, 0:256] = (dq_t[...].T * HEAD_DIM ** (-0.5)).astype(BF16)
+        start_both(
+            n1_sums[m],
+            lambda span: wide(wp, lambda w: dot_nn(d_pack[pl.ds(m * rows + span.start, size), :], w)),
+        )
+
+    def backward(m, side):
+        limits = query_limits(border, prefix, m, c, rows)
+        head_gradients(m)
 
         @pl.loop(0, steps)
         def _(t):
@@ -658,21 +743,18 @@
                 attend_back(m, j, b, limits)
 
                 def pass_on(way):
-                    if m > 0:
-                        dkv_copy(m - 1, way, j, b).wait_send()
-
                     @pl.when(upstream(way))
                     def _():
-                        dkv_landed(m, way, j, b).wait_recv()
+                        dkv_landed(way, j, b).wait_recv()
                         sbuf[j, span, :] = (
-                            acc[span, :] + rbuf[m, j + 1 - way, span, :].astype(F32)
+                            acc[span, :] + rbuf[j + 1 - way, span, :].astype(F32)
                         ).astype(BF16)
 
                     @pl.when(jnp.logical_not(upstream(way)))
                     def _():
                         sbuf[j, span, :] = acc[span, :].astype(BF16)
 
-                    dkv_copy(m, way, j, b).start()
+                    dkv_copy(way, j, b).start()
 
                 pl.when(right)(lambda: pass_on(0))
                 pl.when(left)(lambda: pass_on(1))
@@ -682,15 +764,40 @@
             def _(way=way):
                 for b in range(2):
                     span = block_rows(b)
-                    dkv_landed(m, way, c, b).wait_recv()
-                    acc[span, :] += rbuf[m, c + 1 - way, span, :].astype(F32)
-
-        d_pack[flat, 256:640] = acc[...].astype(BF16)
-        d_pack[flat, 0:256] = (dq_t[...].T * HEAD_DIM ** (-0.5)).astype(BF16)
-        start_both(
-            n1_sums[m],
-            lambda span: wide(wp, lambda w: dot_nn(d_pack[pl.ds(m * rows + span.start, size), :], w)),
-        )
+                    dkv_landed(way, c, b).wait_recv()
+                    acc[span, :] += rbuf[c + 1 - way, span, :].astype(F32)
+
+        backward_end(m)
+
+    def backward_last(m, side, side_keys):
+        limits = query_limits(border, prefix, m, c, rows)
+        head_gradients(m)
+
+        @pl.loop(0, 2)
+        def _(b):
+            attend_back(m, c, b, limits)
+
+        @pl.loop(0, 2 * (n - 1))
+        def _(t):
+            j = lax.rem(c + 1 + lax.div(t, 2), n)
+            attend_back(m, j, lax.rem(t, 2), limits, keys_too=False)
+            for at, jobs in side:
+                at_step(t, at, jobs)
+
+        @pl.loop(0, 2 * (n - 1))
+        def _(t):
+            s = 1 + lax.div(t, 2)
+            for way in range(2):
+                @pl.when(jnp.logical_and(lax.rem(t, 2) == way, has(way, s)))
+                def _(way=way):
+                    pl.when(s > 2)(lambda: qo_step(2, way, s))
+                    pl.when(s > 2)(lambda: qo_step(1, way, s))
+                    for b in range(2):
+                        attend_keys(m, c - s if way == 0 else c + s, b)
+            for at, jobs in side_keys:
+                at_step(t, at, jobs)
+
+        backward_end(m)
 
     def finish_rows(m, q):
         n1_sums[m][q].finish()
@@ -704,9 +811,10 @@
             stats[0:1, :] += column_sums(dn * xhat)
             stats[2:3, :] += column_sums(dn)
 
-    def pack_tile(k, at, count):
+    def pack_part(to, k, at, count, first, kept):
         left = h1[:, pl.ds(pl.multiple_of(k * cols, 128), cols)]
-        return dot_tn(d_pack[:, at : at + count], left)
+        value = dot_tn(d_pack[:, at : at + count], left)
+        to[first : first + kept, :] = value[0:kept].astype(to.dtype)
 
     def do(jobs):
         for job in jobs:
@@ -734,51 +842,65 @@
     forward(1, [
         (0, [each(a0, "step2")]),
         (3, [a0[0].step3]),
-        (5, [lambda: weight_wait(3, 4), lambda: mlp_piece(0, 0), a0[1].step3]),
-        (7, [x0[0].step2, lambda: mlp_piece(0, 1)]),
-        (9, [x0[1].step2]),
+        (4, [
+            lambda: weight_wait(4, 5), lambda: mlp_piece(0, 0), a0[1].step3, x0[0].step2,
+            lambda: mlp_piece(0, 1),
+        ]),
+        (6, [x0[1].step2]),
     ])
     do(stage(x0, "step3"))
     do(stage(a1, "step2"))
     middle_ready(0)
     spot = by_place(5, 0)
+    send_queries(1)
     backward(0, [
+        (2, [lambda: qo_steps(0, 1)]),
         (spot, [a1[0].step3, a1[1].step3, lambda: mlp_piece(1, 0), lambda: mlp_piece(1, 1)]),
+        (6, [lambda: qo_steps(0, 2)]),
         (spot + 2, [each(x1, "step2"), lambda: mlp_start(0)]),
-        (spot + 4, [down_gradient, each(early[0:1], "s0")]),
-        (spot + 6, [up_gradient, each(early[1:3], "s0"), each(u0, "step2"), each(x1, "step3")]),
-        (steps - 1, [lambda: mlp_start(1)]),
+        (spot + 4, [down_gradient, each(early[0:2], "s0")]),
+        (spot + 6, [up_gradient, each(early[2:-1], "s0"), each(u0, "step2"), each(x1, "step3")]),
+        (steps - 1, [lambda: mlp_start(1)] + [lambda s=s: qo_steps(0, s) for s in range(3, n)]),
     ])
     middle_ready(1)
-    out_gradient()
-    do(stage(early[3:], "s0"))
-    backward(1, [
-        (0, [each(y0, "step2"), each(u0, "step3")]),
-        (by_place(0, steps - 1), [each(early[0:2], "s1")]),
-        (steps - 3, [each(u1, "step2"), each(y0, "step3")]),
-        (by_place(steps - 1, steps), [each(early[2:], "s1")]),
+    backward_last(1, [
+        (0, [out_gradient, each(early[-1:], "s0"), each(y0, "step2")]),
+        (by_place(0, 5), [each(early[0:1], "s1")]),
+        (by_place(1, 6), [each(early[1:2], "s1")]),
+        (2, [lambda: qo_steps(2, 1), lambda: qo_steps(1, 1)]),
+        (5, [lambda: qo_steps(2, 2), lambda: qo_steps(1, 2)]),
+    ], [
+        (by_place(0, 2), [each(early[2:3], "s1")]),
+        (by_place(6, 0), [each(early[1:2], "s1")]),
+        (1, [each(y0, "step3"), each(u0, "step3")]),
+        (2, [each(early[0:1], "s2")]),
+        (by_place(2, 5), [each(early[3:4], "s1")]),
+        (3, [each(u1, "step2")]),
+        (4, [each(early[1:2], "s2")]),
+        (by_place(5, 6), [each(early[4:5], "s1")]),
     ])
     if exchange:
-        for piece, (at, count) in zip(late, cuts_of(640, 256)):
-            gb_buf[1 - p.d, at : at + count, :] = pack_tile(1 - p.d, at, count).astype(BF16)
+        for piece, cut in zip(late, PACK_CUTS):
+            pack_part(gb_buf.at[1 - p.d], 1 - p.d, *cut)
             piece.s0()
-        do(stage(early[0:2], "s2"))
-        for at, count in cuts_of(640, 256):
-            gb_buf[p.d, at : at + count, :] = pack_tile(p.d, at, count).astype(BF16)
+        for cut in PACK_CUTS:
+            pack_part(gb_buf.at[p.d], p.d, *cut)
     else:
-        for at, count in cuts_of(640, 128):
-            gb[at : at + count, :] = pack_tile(0, at, count)
+        for cut in PACK_CUTS:
+            pack_part(gb, 0, *cut)
     do(stage(y1, "step2"))
-    do(stage(u1, "step3"))
     for q in range(2):
         finish_rows(0, q)
     if exchange:
         @pl.when(by_place(0, 1) == 1)
         def _():
-            do(stage(early[2:], "s1"))
+            early[4].s1()
+
+        early[2].s2()
+    do(stage(u1, "step3"))
     write_block(0)
-    do(stage(late, "s1"))
-    do(stage(early[2:], "s2"))
+    if exchange:
+        early[3].s2()
     do(stage(y1, "step3"))
     write_block(1)
     for q in range(2):
@@ -788,15 +910,17 @@
             cut = slice(k * cols, (k + 1) * cols)
             gs_buf[k] = jnp.concatenate([stats[:, cut], jnp.zeros((8, cols), F32)], axis=0).astype(BF16)
         do(stage(last, "s0"))
-        do(stage(late, "s2"))
-        do(stage(last, "s1"))
-        do(stage(early, "s3"))
-        do(stage(last, "s2"))
-        do(stage(late, "s3"))
-        do(stage(last, "s3"))
+
+        chain = early + late + last
+        for i in range(5, len(chain) + 1):
+            if i < len(chain):
+                chain[i].s1()
+            chain[i - 1].s2()
+        for piece in early + late + last:
+            piece.s3()
         for piece in early + late + last:
             piece.drain()
-        for i in range(5):
+        for i in range(6):
             weight_copy(i).wait_send()
     else:
         gs[...] = stats[...]
@@ -808,8 +932,14 @@
                         lambda m=m, way=way, s=s, b=b: kv_copy(m, way, s, b).wait_send()
                     )
         for j in range(n):
-            pl.when(c < j)(lambda j=j, b=b: dkv_copy(micro - 1, 0, j, b).wait_send())
-            pl.when(c > j)(lambda j=j, b=b: dkv_copy(micro - 1, 1, j, b).wait_send())
+            pl.when(c < j)(lambda j=j, b=b: dkv_copy(0, j, b).wait_send())
+            pl.when(c > j)(lambda j=j, b=b: dkv_copy(1, j, b).wait_send())
+    for kind in range(3):
+        for way in range(2):
+            for s in range(n - 1):
+                pl.when(sends(way, s))(
+                    lambda kind=kind, way=way, s=s: qo_copy(kind, way, s).wait_send()
+                )
     for piece in a0 + a1 + y0 + y1:
         piece.drain()
 
@@ -823,24 +953,24 @@
     sds = jax.ShapeDtypeStruct
     vmem = pltpu.VMEM
     sems = pltpu.SemaphoreType.DMA
-    grad_rows = ff + cols * (ff // cols) + 256
+    grad_rows = ff + cols * (ff // cols) + 192
     outs = [sds((micro, rows, width), BF16), sds((micro, rows, width), F32)]
     scratch = []
     if exchange:
-        outs += [sds((grad_rows, cols), BF16), sds((640, cols), BF16), sds((16, cols), BF16)]
-        pieces = len(cuts_of(grad_rows, 512)) + len(cuts_of(640, 256)) + 1
+        outs += [sds((grad_rows, cols), BF16), sds((576, cols), BF16), sds((16, cols), BF16)]
+        pieces = len(cuts_of(grad_rows, EARLY_ROWS)) + len(PACK_CUTS) + 1
         scratch += [
             vmem((2, 640, cols), BF16), vmem((2, 256, cols), BF16), vmem((width, ff), BF16),
             vmem((2, ff, cols), BF16), vmem((2, 8, cols), F32),
-            vmem((2, grad_rows, cols), BF16), vmem((2, 640, cols), BF16), vmem((2, 16, cols), BF16),
-            vmem((640, cols), BF16), vmem((640, cols), BF16),
+            vmem((2, grad_rows, cols), BF16), vmem((2, 576, cols), BF16), vmem((2, 16, cols), BF16),
+            vmem((576, cols), BF16), vmem((576, cols), BF16),
             vmem((grad_rows, cols), BF16), vmem((grad_rows, cols), BF16),
             vmem((16, cols), BF16), vmem((16, cols), BF16),
-            sems((5,)), sems((5,)), sems((pieces, 4)), sems((pieces, 4)),
+            sems((6,)), sems((6,)), sems((pieces, 4)), sems((pieces, 4)),
         ]
     else:
         outs += [
-            sds((1, grad_rows, cols), BF16), sds((640, width), F32), sds((8, width), F32)
+            sds((1, grad_rows, cols), BF16), sds((576, width), F32), sds((8, width), F32)
         ]
     scratch += [
         vmem((micro, rows, width), BF16), vmem((total, 256), BF16), vmem((micro, 8, rows), F32),
@@ -849,12 +979,14 @@
         vmem((3, 1, rows), F32), vmem((3, 1, rows), F32), vmem((3, 64, rows), F32),
         vmem((total, ff), BF16), vmem((total, width), BF16), vmem((total, ff), BF16),
         vmem((total, width), BF16), vmem((micro, rows, width), BF16), vmem((total, width), BF16),
-        vmem((n_ctx, rows, 384), BF16), vmem((micro, n_ctx + 1, rows, 384), BF16),
+        vmem((n_ctx, rows, 384), BF16), vmem((n_ctx + 1, rows, 384), BF16),
+        vmem((n_ctx, 192, rows), BF16), vmem((n_ctx, 192, rows), BF16), vmem((n_ctx, 8, rows), F32),
+        sems((3, 2, n_ctx + 1)), sems((3, 2, n_ctx + 1)),
         vmem((rows, 384), F32), vmem((3, rows, 128), BF16), vmem((3, rows, 128), BF16),
         vmem((256, rows), F32), vmem((3, 1, rows), F32), vmem((total, 640), BF16),
         vmem((8, width), F32),
         sems((micro, 2, n_ctx + 1, 2)), sems((micro, 2, n_ctx + 1, 2)),
-        sems((micro, 2, n_ctx, 2)), sems((micro, 2, n_ctx, 2)),
+        sems((2, n_ctx, 2)), sems((2, n_ctx, 2)),
     ]
     scratch += [vmem((16, half // 2, width), BF16)] * 4 + [sems((16, 3))] * 2
     smem = pl.BlockSpec(memory_space=pltpu.SMEM)
@@ -877,9 +1009,9 @@
     for k in range(ff // cols):
         up[:, k * cols : (k + 1) * cols] = ga[ff + k * rows : ff + (k + 1) * rows, :].astype(F32)
     at = ff + rows * (ff // cols)
-    out[0:64, :] = ga[at + 192 : at + 256, :].astype(F32)
+    out[0:64, :] = ga[at + 128 : at + 192, :].astype(F32)
     out[64:192, :] = ga[at : at + 128, :].astype(F32)
-    for i, at in enumerate((0, 256, 448)):
+    for i, at in enumerate((0, 192, 384)):
         qkv[i] = gb[at : at + 192, :].astype(F32)
     gains[...] = gs[...].astype(F32)[0:2]
     shifts[...] = gs[...].astype(F32)[2:4]
@@ -914,8 +1046,8 @@
         g_out = ga[ff + width :]
         whole = lax.psum(
             (
-                jnp.swapaxes(jnp.stack([gb[0:192], gb[256:448], gb[448:640]]), 1, 2),
-                jnp.concatenate([g_out[192:], g_out[:128]], axis=0), ga[ff : ff + width], ga[:ff],
+                jnp.swapaxes(gb.reshape(3, 192, -1), 1, 2),
+                jnp.concatenate([g_out[128:], g_out[:128]], axis=0), ga[ff : ff + width], ga[:ff],
                 gs[0:2], gs[2:4],
             ),
             "ctx",

time: 220 us -> 191 us (0.87)
  Pallas kernels: 215 us -> 186 us
    pallas_call x1, Pallas kernels: 212 us -> 182 us  [run_block(): pl.pallas_call(functools.partial(block_kernel, n_ctx, exchange), out_shap...]
where the time goes in v5:
time: 191 us; the launch traced here: 190 us
  Pallas kernels  186 us (97%)
  local copies, waits for them, and re-layouts  4.12 us (2%)
    pallas_call x1, Pallas kernels, run_block(): pl.pallas_call(functools.partial(block_kernel, n_ctx, exchange), out_shap...  182 us
    unnamed x6, local copies, waits for them, and re-layouts  4.12 us

profile of v5, /device:TPU:0, one launch (start us, length us, event | category | flops | bytes accessed | tf_op | source)
XLA Modules:
  0.0 190.3 jit_solution(4269089200518855687)
XLA Ops:
  0.6 182.1 %block_both_ways.1 = (bf16[2,512,768]{2,1,0:T(8,128)(2,1)}, f32[2,512,768]{2,1,0:T(8,128)}, bf16[1728,384]{1,0:T(8,128)(2,1)}, bf16[576,384]{1,0:T(8,128)(2,1)}, bf16[16,384]{1,0:T(8,128)(2,1)}) custom-call(s32[2]{0:T(128)} %bitcast.16, s32[8]{0:T(128)} %border.1, bf16[2,512,768]{2,1,0:T(8,128)(2,1)} %bitcast.13, bf16[2,512,768]{2,1,0:T(8,128)(2,1)} %bitcast.14, ...), custom_call_target="tpu_custom_call" | custom-call | tf_op jit(solution)/shard_map/block_both_ways/pallas_call | solution.py:993
  182.8 0.0 copy-start.1
  182.8 3.4 %unpack_gradients.1 = (f32[3,192,384]{2,1,0:T(8,128)}, f32[192,384]{1,0:T(8,128)}, f32[384,768]{1,0:T(8,128)}, f32[768,384]{1,0:T(8,128)}, f32[2,384]{1,0:T(2,128)}, /*index=5*/f32[2,384]{1,0:T(2,128)}) custom-call(bf16[1728,384]{1,0:T(8,128)(2,1)} %get-tuple-element.21.ga, bf16[576,384]{1,0:T(8,128)(2,1)} %get-tuple-element.22.gb, ...), custom_call_target="tpu_custom_call" | custom-call | tf_op jit(solution)/shard_map/unpack_gradients/pallas_call | solution.py:1036
  186.2 0.0 copy-done.1
  186.2 0.0 copy-start
  186.2 1.1 copy.22
  187.4 1.3 copy-done
  188.7 1.7 copy.23
Async XLA Ops:
  182.8 3.5 %copy-start.1 = (bf16[2,512,768]{2,1,0:T(8,128)(2,1)S(1)}, bf16[2,512,768]{2,1,0:T(8,128)(2,1)}, u32[]{:S(2)}) copy-start(bf16[2,512,768]{2,1,0:T(8,128)(2,1)} %get-tuple-element.19) | copy-start | bytes 4718596
  186.2 2.5 %copy-start = (f32[2,512,768]{2,1,0:T(8,128)S(1)}, f32[2,512,768]{2,1,0:T(8,128)}, u32[]{:S(2)}) copy-start(f32[2,512,768]{2,1,0:T(8,128)} %get-tuple-element.20) | copy-start | bytes 9437188

commit v6 on v5

--- a/solution.py
+++ b/solution.py
@@ -80,10 +80,9 @@
             hello(tp=self.across)
             count += 2
         if ctx:
-            pl.when(self.c > 0)(lambda: hello(ctx=self.c - 1))
-            pl.when(self.c < self.n - 1)(lambda: hello(ctx=self.c + 1))
-        if ctx:
-            count = count + jnp.minimum(self.c, 1) + jnp.minimum(self.n - 1 - self.c, 1)
+            for j in range(1, self.n):
+                hello(ctx=lax.rem(self.c + j, self.n))
+            count += self.n - 1
         pl.semaphore_wait(sem, count)
 
 
@@ -262,8 +261,49 @@
         pl.when(jnp.logical_not(self.end))(lambda: self.down_copy().wait_send())
 
 
+class StatSum:
+    def __init__(self, place, parts, from_dp, every, out, send, recv):
+        self.p, self.parts, self.from_dp, self.every, self.out = place, parts, from_dp, every, out
+        self.send, self.recv = send, recv
+
+    def dp_copy(self):
+        return remote(
+            self.parts.at[1 - self.p.d], self.from_dp, self.send.at[0], self.recv.at[0],
+            dp=1 - self.p.d,
+        )
+
+    def copy(self, owner, k):
+        piece = self.every.at[owner]
+        return remote(
+            piece, piece, self.send.at[k], self.recv.at[k], ctx=lax.rem(self.p.c + k, self.p.n)
+        )
+
+    def s0(self):
+        self.dp_copy().start()
+
+    def s1(self):
+        self.dp_copy().wait_recv()
+        both = self.parts[self.p.d].astype(F32) + self.from_dp[...].astype(F32)
+        self.every[self.p.c] = both.astype(BF16)
+        for k in range(1, self.p.n):
+            self.copy(self.p.c, k).start()
+
+    def s2(self):
+        for k in range(1, self.p.n):
+            self.copy(lax.rem(self.p.c + self.p.n - k, self.p.n), k).wait_recv()
+        total = self.every[0].astype(F32)
+        for j in range(1, self.p.n):
+            total += self.every[j].astype(F32)
+        self.out[...] = total
+
+    def drain(self):
+        self.dp_copy().wait_send()
+        for k in range(1, self.p.n):
+            self.copy(self.p.c, k).wait_send()
+
+
 EARLY_ROWS = 384
-PACK_CUTS = ((0, 256, 0, 192), (256, 256, 192, 256), (512, 128, 448, 128))
+PACK_CUTS = ((0, 256, 0, 192), (256, 128, 192, 128), (384, 128, 320, 128), (512, 128, 448, 128))
 A_SUM, N2_SUM, MLP_SUM, N1_SUM = 0, 2, 4, 6
 
 
@@ -276,14 +316,16 @@
     return cuts
 
 
-def block_kernel(n_ctx, exchange, prefix, border, hid, cot, *refs):
+def block_kernel(n_ctx, exchange, prefix, border, hid_in, cot_in, *refs):
     if exchange:
         (qkv_s, out_s, up_s, down_s, gain_s, shift_s) = refs[:6]
-        (block, grad_in, ga, gb, gs) = refs[6:11]
-        (wp, wo, wu, wd, ln, grads, gb_buf, gs_buf, b_fu, b_fm, a_fu, a_fm, s_fu, s_fm,
-         wsend, wrecv, gsend, grecv) = refs[11:29]
-        refs = refs[29:]
+        (block_out, grad_out, ga_out, gb_out, gs) = refs[6:11]
+        (wp, wo, wu, wd, ln, grads, gb_buf, gs_buf, b_fu, b_fm, a_fu, a_fm, s_dp, s_all,
+         hid, cot, block, grad_in, ga, gb, load, keep, wsend, wrecv, gsend, grecv, ssend,
+         srecv) = refs[11:39]
+        refs = refs[39:]
     else:
+        hid, cot = hid_in, cot_in
         (wp, wo, wu, wd, ln) = refs[:5]
         (block, grad_in, grads, gb, gs) = refs[5:10]
         refs = refs[10:]
@@ -299,6 +341,12 @@
     cols = width // parts
     own_rows = width // parts
     tiles = rows // 128
+    loads = []
+    if exchange:
+        spot = pl.ds(pl.multiple_of(p.d * cols, cols), cols)
+        pairs = ((hid_in, hid), (cot_in, cot), (up_s, wu.at[spot]), (down_s, wd.at[p.d]))
+        loads = [pltpu.make_async_copy(a, b, load.at[i]) for i, (a, b) in enumerate(pairs)]
+        loads[0].start()
     p.barrier(exchange, True, True)
 
     size = half // 2
@@ -349,8 +397,9 @@
         wo[p.d, 0:128, :] = out_s[64:192, :]
         wo[p.d, 128:192, :] = jnp.zeros((64, cols), BF16)
         wo[p.d, 192:256, :] = out_s[0:64, :]
-        wu[mine, :] = up_s[...]
-        wd[p.d] = down_s[...]
+        for piece in loads[1:]:
+            piece.start()
+        loads[0].wait()
 
     def weight_wait(*which):
         if exchange:
@@ -407,6 +456,8 @@
     pl.when(c == 0)(lambda: send_own(1, 0))
     pl.when(c == n - 1)(lambda: send_own(1, 1))
     weight_wait(2)
+    for piece in loads[1:]:
+        piece.wait()
     if exchange:
         for i in range(3, 6):
             weight_copy(i).start()
@@ -576,7 +627,15 @@
             grads[k, at : at + 128, :] = value[0:128]
             grads[k, at + 128 : at + 192, :] = value[192:256]
 
-    early, late, last = [], [], []
+    early, late, norms = [], [], None
+    stores = []
+
+    def store(source, to, *index):
+        if exchange:
+            piece = pltpu.make_async_copy(source.at[index], to.at[index], keep.at[len(stores)])
+            piece.start()
+            stores.append(piece)
+
     if exchange:
         for i, (at, count) in enumerate(cuts_of(grads.shape[1], EARLY_ROWS)):
             cut = pl.ds(at, count)
@@ -590,10 +649,7 @@
                 p, gb_buf.at[1 - p.d, cut], gb_buf.at[p.d, cut], gb.at[cut], b_fu.at[cut],
                 b_fm.at[cut], gsend.at[k], grecv.at[k],
             ))
-        k = len(early) + len(late)
-        last = [GradSum(
-            p, gs_buf.at[1 - p.d], gs_buf.at[p.d], gs, s_fu, s_fm, gsend.at[k], grecv.at[k]
-        )]
+        norms = StatSum(p, gs_buf, s_dp, s_all, gs, ssend, srecv)
 
     def stage(group, name):
         return [getattr(piece, name) for piece in group]
@@ -712,10 +768,12 @@
         split_queries(m)
         dq_t[...] = jnp.zeros(dq_t.shape, F32)
 
+    def query_gradient(m):
+        flat = pl.ds(m * rows, rows)
+        d_pack[flat, 0:256] = (dq_t[...].T * HEAD_DIM ** (-0.5)).astype(BF16)
+
     def backward_end(m):
-        flat = pl.ds(m * rows, rows)
-        d_pack[flat, 256:640] = acc[...].astype(BF16)
-        d_pack[flat, 0:256] = (dq_t[...].T * HEAD_DIM ** (-0.5)).astype(BF16)
+        d_pack[pl.ds(m * rows, rows), 256:640] = acc[...].astype(BF16)
         start_both(
             n1_sums[m],
             lambda span: wide(wp, lambda w: dot_nn(d_pack[pl.ds(m * rows + span.start, size), :], w)),
@@ -767,9 +825,10 @@
                     dkv_landed(way, c, b).wait_recv()
                     acc[span, :] += rbuf[c + 1 - way, span, :].astype(F32)
 
+        query_gradient(m)
         backward_end(m)
 
-    def backward_last(m, side, side_keys):
+    def backward_last(m, side, between, side_keys):
         limits = query_limits(border, prefix, m, c, rows)
         head_gradients(m)
 
@@ -783,6 +842,9 @@
             attend_back(m, j, lax.rem(t, 2), limits, keys_too=False)
             for at, jobs in side:
                 at_step(t, at, jobs)
+
+        query_gradient(m)
+        do(between)
 
         @pl.loop(0, 2 * (n - 1))
         def _(t):
@@ -846,7 +908,7 @@
             lambda: weight_wait(4, 5), lambda: mlp_piece(0, 0), a0[1].step3, x0[0].step2,
             lambda: mlp_piece(0, 1),
         ]),
-        (6, [x0[1].step2]),
+        (5, [x0[1].step2]),
     ])
     do(stage(x0, "step3"))
     do(stage(a1, "step2"))
@@ -862,64 +924,90 @@
         (spot + 6, [up_gradient, each(early[2:-1], "s0"), each(u0, "step2"), each(x1, "step3")]),
         (steps - 1, [lambda: mlp_start(1)] + [lambda s=s: qo_steps(0, s) for s in range(3, n)]),
     ])
+    def at_place(ends, jobs):
+        @pl.when(by_place(1, 0) == ends)
+        def _():
+            do(jobs)
+
+    at_place(1, stage(early[0:1], "s1"))
     middle_ready(1)
+    query_pieces = []
+    if exchange:
+        def query_piece():
+            pack_part(gb_buf.at[1 - p.d], 1 - p.d, *PACK_CUTS[0])
+            late[0].s0()
+            pack_part(gb_buf.at[p.d], p.d, *PACK_CUTS[0])
+
+        query_pieces = [query_piece]
     backward_last(1, [
         (0, [out_gradient, each(early[-1:], "s0"), each(y0, "step2")]),
-        (by_place(0, 5), [each(early[0:1], "s1")]),
-        (by_place(1, 6), [each(early[1:2], "s1")]),
+        (by_place(0, 5), [each(early[1:2], "s1")]),
         (2, [lambda: qo_steps(2, 1), lambda: qo_steps(1, 1)]),
+        (by_place(9, 3), [each(early[0:1], "s1")]),
         (5, [lambda: qo_steps(2, 2), lambda: qo_steps(1, 2)]),
-    ], [
-        (by_place(0, 2), [each(early[2:3], "s1")]),
-        (by_place(6, 0), [each(early[1:2], "s1")]),
+        (by_place(4, 9), [each(early[2:3], "s1")]),
+    ], query_pieces, [
+        (by_place(0, 9), [each(early[3:4], "s1")]),
+        (0, [each(early[0:1], "s2")]),
         (1, [each(y0, "step3"), each(u0, "step3")]),
-        (2, [each(early[0:1], "s2")]),
-        (by_place(2, 5), [each(early[3:4], "s1")]),
-        (3, [each(u1, "step2")]),
-        (4, [each(early[1:2], "s2")]),
-        (by_place(5, 6), [each(early[4:5], "s1")]),
+        (by_place(9, 2), [each(early[2:3], "s1")]),
+        (by_place(2, 9), [each(early[4:5], "s1")]),
+        (3, [each(u1, "step2"), each(early[1:2], "s2")]),
+        (by_place(9, 5), [each(early[3:4], "s1")]),
     ])
     if exchange:
-        for piece, cut in zip(late, PACK_CUTS):
+        for piece, cut in zip(late[1:], PACK_CUTS[1:]):
             pack_part(gb_buf.at[1 - p.d], 1 - p.d, *cut)
             piece.s0()
-        for cut in PACK_CUTS:
+        for cut in PACK_CUTS[1:]:
             pack_part(gb_buf.at[p.d], p.d, *cut)
     else:
         for cut in PACK_CUTS:
             pack_part(gb, 0, *cut)
     do(stage(y1, "step2"))
+    if exchange:
+        at_place(1, stage(late[0:1], "s1"))
+        at_place(0, stage(early[2:3], "s2"))
     for q in range(2):
         finish_rows(0, q)
-    if exchange:
-        @pl.when(by_place(0, 1) == 1)
-        def _():
-            early[4].s1()
-
-        early[2].s2()
+    store(grad_in, grad_out if exchange else None, 0)
+    if exchange:
+        at_place(1, stage(late[1:3], "s1"))
+        at_place(0, stage(early[4:5] + late[0:1], "s1"))
     do(stage(u1, "step3"))
     write_block(0)
-    if exchange:
-        early[3].s2()
-    do(stage(y1, "step3"))
-    write_block(1)
+    store(block, block_out if exchange else None, 0)
+    if exchange:
+        at_place(1, stage(late[3:], "s1"))
+        at_place(0, stage(late[1:2], "s1") + stage(early[3:4], "s2"))
+    for q in range(2):
+        y1[q].step3()
     for q in range(2):
         finish_rows(1, q)
+    store(grad_in, grad_out if exchange else None, 1)
     if exchange:
         for k in range(2):
             cut = slice(k * cols, (k + 1) * cols)
             gs_buf[k] = jnp.concatenate([stats[:, cut], jnp.zeros((8, cols), F32)], axis=0).astype(BF16)
-        do(stage(last, "s0"))
-
-        chain = early + late + last
-        for i in range(5, len(chain) + 1):
-            if i < len(chain):
-                chain[i].s1()
-            chain[i - 1].s2()
-        for piece in early + late + last:
-            piece.s3()
-        for piece in early + late + last:
+        norms.s0()
+        at_place(0, stage(early[4:5], "s2") + stage(late[2:], "s1") + stage(late[0:1], "s2"))
+    write_block(1)
+    store(block, block_out if exchange else None, 1)
+    if exchange:
+        norms.s1()
+        at_place(0, stage(late[1:], "s2"))
+        for group, held, to, cuts in (
+            (early, ga, ga_out, cuts_of(ga.shape[0], EARLY_ROWS)),
+            (late, gb, gb_out, [cut[2:] for cut in PACK_CUTS]),
+        ):
+            for piece, (at, count) in zip(group, cuts):
+                piece.s3()
+                store(held, to, pl.ds(at, count))
+        norms.s2()
+        for piece in early + late + [norms]:
             piece.drain()
+        for piece in stores:
+            piece.wait()
         for i in range(6):
             weight_copy(i).wait_send()
     else:
@@ -957,16 +1045,20 @@
     outs = [sds((micro, rows, width), BF16), sds((micro, rows, width), F32)]
     scratch = []
     if exchange:
-        outs += [sds((grad_rows, cols), BF16), sds((576, cols), BF16), sds((16, cols), BF16)]
-        pieces = len(cuts_of(grad_rows, EARLY_ROWS)) + len(PACK_CUTS) + 1
+        outs += [sds((grad_rows, cols), BF16), sds((576, cols), BF16), sds((16, cols), F32)]
+        pieces = len(cuts_of(grad_rows, EARLY_ROWS)) + len(PACK_CUTS)
         scratch += [
             vmem((2, 640, cols), BF16), vmem((2, 256, cols), BF16), vmem((width, ff), BF16),
             vmem((2, ff, cols), BF16), vmem((2, 8, cols), F32),
             vmem((2, grad_rows, cols), BF16), vmem((2, 576, cols), BF16), vmem((2, 16, cols), BF16),
             vmem((576, cols), BF16), vmem((576, cols), BF16),
             vmem((grad_rows, cols), BF16), vmem((grad_rows, cols), BF16),
-            vmem((16, cols), BF16), vmem((16, cols), BF16),
+            vmem((16, cols), BF16), vmem((n_ctx, 16, cols), BF16),
+            vmem(hid.shape, BF16), vmem(hid.shape, BF16), vmem(hid.shape, BF16), vmem(hid.shape, F32),
+            vmem((grad_rows, cols), BF16), vmem((576, cols), BF16), sems((4,)),
+            sems((2 * micro + pieces,)),
             sems((6,)), sems((6,)), sems((pieces, 4)), sems((pieces, 4)),
+            sems((n_ctx,)), sems((n_ctx,)),
         ]
     else:
         outs += [
@@ -990,11 +1082,15 @@
     ]
     scratch += [vmem((16, half // 2, width), BF16)] * 4 + [sems((16, 3))] * 2
     smem = pl.BlockSpec(memory_space=pltpu.SMEM)
+    stay = pl.BlockSpec(memory_space=pl.ANY)
+    specs = vmem_specs(2 + len(weights))
+    if exchange:
+        specs = [stay, stay] + vmem_specs(2) + [stay, stay] + vmem_specs(2)
     return pl.pallas_call(
         functools.partial(block_kernel, n_ctx, exchange),
         out_shape=outs,
-        in_specs=[smem, smem] + vmem_specs(2 + len(weights)),
-        out_specs=vmem_specs(len(outs)),
+        in_specs=[smem, smem] + specs,
+        out_specs=([stay] * 4 + vmem_specs(1)) if exchange else vmem_specs(len(outs)),
         scratch_shapes=scratch,
         compiler_params=pltpu.CompilerParams(
             collective_id=0, has_side_effects=True, vmem_limit_bytes=67043328
@@ -1003,18 +1099,61 @@
     )(prefix, border, hid, cot, *weights)
 
 
-def unpack_kernel(ff, ga, gb, gs, qkv, out, up, down, gains, shifts):
-    rows, cols = qkv.shape[2], ga.shape[1]
-    down[...] = ga[0:ff, :].astype(F32)
-    for k in range(ff // cols):
-        up[:, k * cols : (k + 1) * cols] = ga[ff + k * rows : ff + (k + 1) * rows, :].astype(F32)
-    at = ff + rows * (ff // cols)
-    out[0:64, :] = ga[at + 128 : at + 192, :].astype(F32)
-    out[64:192, :] = ga[at : at + 128, :].astype(F32)
-    for i, at in enumerate((0, 192, 384)):
-        qkv[i] = gb[at : at + 192, :].astype(F32)
-    gains[...] = gs[...].astype(F32)[0:2]
-    shifts[...] = gs[...].astype(F32)[2:4]
+def unpack_kernel(
+    block_in, grad_in, down_in, left_in, right_in, out_in, qkv_in, gs,
+    block, grad, down, up, qkv, out, gains, shifts,
+):
+    cols = down_in.shape[1]
+    block[...] = block_in[...]
+    grad[...] = grad_in[...]
+    down[...] = down_in[...].astype(F32)
+    up[:, 0:cols] = left_in[...].astype(F32)
+    up[:, cols : 2 * cols] = right_in[...].astype(F32)
+    qkv[...] = qkv_in[...].astype(F32)
+
+    @pl.when(pl.program_id(0) == 0)
+    def _():
+        out[0:64, :] = out_in[128:192, :].astype(F32)
+        out[64:192, :] = out_in[0:128, :].astype(F32)
+        gains[...] = gs[0:2]
+        shifts[...] = gs[2:4]
+
+
+UNPACK_STEPS = 4
+
+
+def unpack(block, grad_in, ga, gb, gs, ff):
+    cols = ga.shape[1]
+    d, u, q = ff // UNPACK_STEPS, cols // UNPACK_STEPS, gb.shape[0] // UNPACK_STEPS
+    total, width = block.shape
+    r = total // UNPACK_STEPS
+    sds = jax.ShapeDtypeStruct
+
+    def rows(count, wide_by, first=0):
+        return pl.BlockSpec((count, wide_by), lambda i: (first + i, 0))
+
+    def whole(*shape, at=0):
+        return pl.BlockSpec(shape, lambda i: (at, 0))
+
+    return pl.pallas_call(
+        unpack_kernel,
+        grid=(UNPACK_STEPS,),
+        out_shape=[
+            sds((total, width), BF16), sds((total, width), F32), sds((ff, cols), F32),
+            sds((cols, 2 * cols), F32), sds(gb.shape, F32), sds((192, cols), F32),
+            sds((2, cols), F32), sds((2, cols), F32),
+        ],
+        in_specs=[
+            rows(r, width), rows(r, width), rows(d, cols), rows(u, cols, ff // u),
+            rows(u, cols, (ff + cols) // u), whole(192, cols, at=(ff + 2 * cols) // 192), rows(q, cols),
+            whole(*gs.shape),
+        ],
+        out_specs=[
+            rows(r, width), rows(r, width), rows(d, cols), rows(u, 2 * cols), rows(q, cols),
+            whole(192, cols), whole(2, cols), whole(2, cols),
+        ],
+        name="unpack_outputs",
+    )(block, grad_in, ga, ga, ga, ga, gb, gs)
 
 
 def body(
@@ -1033,29 +1172,30 @@
         n_ctx, exchange, prefix[:, 0], block_order, hid, cot, weights, ff
     )
     if exchange:
-        owned = pl.pallas_call(
-            functools.partial(unpack_kernel, ff),
-            out_shape=[jax.ShapeDtypeStruct(w.shape, F32) for w in (turned,) + params[1:]],
-            in_specs=vmem_specs(3),
-            out_specs=vmem_specs(6),
-            name="unpack_gradients",
-        )(ga, gb, gs)
-        owned = [jnp.swapaxes(owned[0], 1, 2)] + list(owned[1:])
-    else:
-        ga = ga[0].astype(F32)
-        g_out = ga[ff + width :]
-        whole = lax.psum(
-            (
-                jnp.swapaxes(gb.reshape(3, 192, -1), 1, 2),
-                jnp.concatenate([g_out[128:], g_out[:128]], axis=0), ga[ff : ff + width], ga[:ff],
-                gs[0:2], gs[2:4],
-            ),
-            "ctx",
+        total = micro * tokens
+        block, grad_in, g_down, g_up, g_qkv, g_out, g_gains, g_shifts = unpack(
+            block.reshape(total, width), grad_in.reshape(total, width), ga, gb, gs, ff
         )
-        owned = [
-            lax.psum_scatter(v, "dp", scatter_dimension=d, tiled=True)
-            for v, d in zip(whole, (1, 1, 0, 1, 1, 1))
-        ]
+        shape = (micro, 1, tokens, width)
+        g_qkv = jnp.swapaxes(g_qkv.reshape(turned.shape), 1, 2)
+        return (
+            block.reshape(shape), grad_in.reshape(shape), g_qkv, g_out, g_up, g_down, g_gains,
+            g_shifts,
+        )
+    ga = ga[0].astype(F32)
+    g_out = ga[ff + width :]
+    whole = lax.psum(
+        (
+            jnp.swapaxes(gb.reshape(3, 192, -1), 1, 2),
+            jnp.concatenate([g_out[128:], g_out[:128]], axis=0), ga[ff : ff + width], ga[:ff],
+            gs[0:2], gs[2:4],
+        ),
+        "ctx",
+    )
+    owned = [
+        lax.psum_scatter(v, "dp", scatter_dimension=d, tiled=True)
+        for v, d in zip(whole, (1, 1, 0, 1, 1, 1))
+    ]
     return (block[:, None], grad_in[:, None], *owned)
 
 

time: 191 us -> 185 us (0.969)
  local copies, waits for them, and re-layouts: 4.12 us -> 0 us
  Pallas kernels: 186 us -> 184 us
    pallas_call x1, Pallas kernels: 182 us -> 177 us  [run_block(): pl.pallas_call(functools.partial(block_kernel, n_ctx, exchange), out_shap...]
    unnamed x6 -> x0, local copies, waits for them, and re-layouts: 4.12 us -> none
    pallas_call x1, Pallas kernels: 3.45 us -> 6.7 us  [unpack(): pl.pallas_call(unpack_kernel, grid=(UNPACK_STEPS,), out_shape=[sds((total...]
where the time goes in v6:
time: 185 us; the launch traced here: 184 us
  Pallas kernels  184 us (99%)
    pallas_call x1, Pallas kernels, run_block(): pl.pallas_call(functools.partial(block_kernel, n_ctx, exchange), out_shap...  177 us
    pallas_call x1, Pallas kernels, unpack(): pl.pallas_call(unpack_kernel, grid=(UNPACK_STEPS,), out_shape=[sds((total...  6.7 us

profile of v6, /device:TPU:0, one launch (start us, length us, event | category | flops | bytes accessed | tf_op | source)
XLA Modules:
  0.0 184.4 jit_solution(1618285290529117659)
XLA Ops:
  0.6 176.8 %block_both_ways.1 = (bf16[2,512,768]{2,1,0:T(8,128)(2,1)}, f32[2,512,768]{2,1,0:T(8,128)}, bf16[1728,384]{1,0:T(8,128)(2,1)}, bf16[576,384]{1,0:T(8,128)(2,1)}, f32[16,384]{1,0:T(8,128)}) custom-call(s32[2]{0:T(128)} %bitcast.20, s32[8]{0:T(128)} %border.1, bf16[2,512,768]{2,1,0:T(8,128)(2,1)} %bitcast.16, bf16[2,512,768]{2,1,0:T(8,128)(2,1)} %bitcast.17, ...), custom_call_target="tpu_custom_call" | custom-call | tf_op jit(solution)/shard_map/block_both_ways/pallas_call | solution.py:1089
  177.5 6.7 %unpack_outputs.1 = (bf16[1024,768]{1,0:T(8,128)(2,1)}, f32[1024,768]{1,0:T(8,128)}, f32[768,384]{1,0:T(8,128)}, f32[384,768]{1,0:T(8,128)}, f32[576,384]{1,0:T(...) custom-call(bf16[1024,768]{1,0:T(8,128)(2,1)} %bitcast.18, f32[1024,768]{1,0:T(8,128)} %bitcast.15, ...), custom_call_target="tpu_custom_call" | custom-call | tf_op jit(solution)/shard_map/unpack_outputs/pallas_call | solution.py:1138

commit v7 on v6

--- a/solution.py
+++ b/solution.py
@@ -351,15 +351,15 @@
 
     size = half // 2
 
+    def tp_piece(kind, m, q, total):
+        i = 2 * (kind + m) + q
+        return TpSum(
+            p, half, q * size, size, t_mine.at[i], t_out.at[i], t_in.at[i], t_sum.at[i], total,
+            tsend.at[i], trecv.at[i],
+        )
+
     def tp_sums(kind, m, total):
-        pieces = []
-        for q in range(2):
-            i = 2 * (kind + m) + q
-            pieces.append(TpSum(
-                p, half, q * size, size, t_mine.at[i], t_out.at[i], t_in.at[i], t_sum.at[i], total,
-                tsend.at[i], trecv.at[i],
-            ))
-        return pieces
+        return [tp_piece(kind, m, q, total) for q in range(2)]
 
     a_sums = [tp_sums(A_SUM, m, attn.at[m]) for m in range(micro)]
     n2_sums = [tp_sums(N2_SUM, m, n2_tot.at[m]) for m in range(micro)]
@@ -445,10 +445,8 @@
     for m in range(micro):
         @pl.loop(0, 2)
         def _(b, m=m):
-            for i in range(tiles // 2):
-                span = pl.ds(pl.multiple_of(b * half + i * 128, 128), 128)
-                flat = pl.ds(pl.multiple_of(m * rows + b * half + i * 128, 128), 128)
-                kv[m, c, span, :] = narrow(wp, h1[flat, :], 256, 384).astype(BF16)
+            flat = pl.ds(pl.multiple_of(m * rows + b * half, half), half)
+            kv[m, c, block_rows(b), :] = narrow(wp, h1[flat, :], 256, 384).astype(BF16)
             if m == 0:
                 for way in range(2):
                     pl.when(sends(way, 0))(lambda way=way: kv_copy(0, way, 0, b).start())
@@ -462,10 +460,11 @@
         for i in range(3, 6):
             weight_copy(i).start()
     for m in range(micro):
-        @pl.loop(0, tiles)
-        def _(i, m=m):
-            q = narrow(wp, h1[tile(i, m * rows), :], 0, 256).astype(BF16).astype(F32)
-            qs[m, tile(i), :] = (q * HEAD_DIM ** (-0.5)).astype(BF16)
+        @pl.loop(0, 2)
+        def _(b, m=m):
+            flat = pl.ds(pl.multiple_of(m * rows + b * half, half), half)
+            q = narrow(wp, h1[flat, :], 0, 256).astype(BF16).astype(F32)
+            qs[m, block_rows(b), :] = (q * HEAD_DIM ** (-0.5)).astype(BF16)
 
     lanes = lax.broadcasted_iota(jnp.int32, (rows, 128), 1)
 
@@ -558,22 +557,26 @@
         return hid[m, tile(i), :].astype(F32) + BRANCH * attn[m, tile(i), :].astype(F32)
 
     def mlp_tiles(m, q):
-        @pl.loop(0, 2)
-        def _(core):
-            i = q + (tiles // 2) * core
-            flat = tile(i, m * rows)
-            xhat, _ = normalize(middle(m, i))
-            normed = (xhat * gain1 + shift1).astype(BF16)
-            h2[flat, :] = normed
-            up = dot_nn(normed, wu[...])
-            active = gelu_value(up).astype(BF16)
-            act[flat, :] = active
-            down_grad = (BRANCH * cot[m, tile(i), :].astype(F32)).astype(BF16)
-            d_mlp[flat, :] = down_grad
-            d_up[flat, :] = (narrow(wd, down_grad) * gelu_slope(up)).astype(BF16)
-            block[m, tile(i), :] = wide(wd, lambda w: dot_nn(active, w)).astype(BF16)
-
-        n2_sums[m][q].start(
+        order = (q, q + tiles // 2)
+
+        def rows_of(read):
+            return jnp.concatenate([read(i) for i in order], axis=0)
+
+        def keep_rows(ref, value, base=0):
+            for k, i in enumerate(order):
+                ref[tile(i, base), :] = value[k * 128 : (k + 1) * 128]
+
+        xhat, _ = normalize(rows_of(lambda i: middle(m, i)))
+        normed = (xhat * gain1 + shift1).astype(BF16)
+        keep_rows(h2, normed, m * rows)
+        up = dot_nn(normed, wu[...])
+        active = gelu_value(up).astype(BF16)
+        keep_rows(act, active, m * rows)
+        down_grad = (BRANCH * rows_of(lambda i: cot[m, tile(i), :].astype(F32))).astype(BF16)
+        keep_rows(d_mlp, down_grad, m * rows)
+        keep_rows(d_up, (narrow(wd, down_grad) * gelu_slope(up)).astype(BF16), m * rows)
+        keep_rows(block.at[m], wide(wd, lambda w: dot_nn(active, w)).astype(BF16))
+        tp_piece(N2_SUM, m, q, n2_tot.at[m]).start(
             lambda span: dot_nt(d_up[pl.ds(m * rows + span.start, size), :], wu[...])
         )
 
@@ -892,8 +895,13 @@
             piece.drain()
 
     def mlp_piece(m, q):
-        a_sums[m][q].finish()
+        tp_piece(A_SUM, m, q, attn.at[m]).finish()
         mlp_tiles(m, q)
+
+    def mlp_pieces(m):
+        @pl.loop(0, 2)
+        def _(q):
+            mlp_piece(m, q)
 
     def by_place(at_end, inside):
         return jnp.where(jnp.logical_or(c == 0, c == n - 1), at_end, inside)
@@ -917,7 +925,7 @@
     send_queries(1)
     backward(0, [
         (2, [lambda: qo_steps(0, 1)]),
-        (spot, [a1[0].step3, a1[1].step3, lambda: mlp_piece(1, 0), lambda: mlp_piece(1, 1)]),
+        (spot, [a1[0].step3, a1[1].step3, lambda: mlp_pieces(1)]),
         (6, [lambda: qo_steps(0, 2)]),
         (spot + 2, [each(x1, "step2"), lambda: mlp_start(0)]),
         (spot + 4, [down_gradient, each(early[0:2], "s0")]),
@@ -932,13 +940,17 @@
     at_place(1, stage(early[0:1], "s1"))
     middle_ready(1)
     query_pieces = []
-    if exchange:
-        def query_piece():
-            pack_part(gb_buf.at[1 - p.d], 1 - p.d, *PACK_CUTS[0])
-            late[0].s0()
-            pack_part(gb_buf.at[p.d], p.d, *PACK_CUTS[0])
-
-        query_pieces = [query_piece]
+
+    def pack_pieces(first, end):
+        @pl.loop(0, 2)
+        def _(i):
+            k = lax.rem(p.d + 1 + i, 2)
+            for piece, cut in list(zip(late, PACK_CUTS))[first:end]:
+                pack_part(gb_buf.at[k], k, *cut)
+                pl.when(i == 0)(piece.s0)
+
+    if exchange:
+        query_pieces = [lambda: pack_pieces(0, 1)]
     backward_last(1, [
         (0, [out_gradient, each(early[-1:], "s0"), each(y0, "step2")]),
         (by_place(0, 5), [each(early[1:2], "s1")]),
@@ -956,11 +968,7 @@
         (by_place(9, 5), [each(early[3:4], "s1")]),
     ])
     if exchange:
-        for piece, cut in zip(late[1:], PACK_CUTS[1:]):
-            pack_part(gb_buf.at[1 - p.d], 1 - p.d, *cut)
-            piece.s0()
-        for cut in PACK_CUTS[1:]:
-            pack_part(gb_buf.at[p.d], p.d, *cut)
+        pack_pieces(1, len(late))
     else:
         for cut in PACK_CUTS:
             pack_part(gb, 0, *cut)
@@ -1119,7 +1127,7 @@
         shifts[...] = gs[2:4]
 
 
-UNPACK_STEPS = 4
+UNPACK_STEPS = 2
 
 
 def unpack(block, grad_in, ga, gb, gs, ff):

time: 185 us -> 180 us (0.973)
  Pallas kernels: 184 us -> 179 us
    pallas_call x1, Pallas kernels: 177 us -> 174 us  [run_block(): pl.pallas_call(functools.partial(block_kernel, n_ctx, exchange), out_shap...]
where the time goes in v7:
time: 180 us
  Pallas kernels  179 us (99%)
    pallas_call x1, Pallas kernels, run_block(): pl.pallas_call(functools.partial(block_kernel, n_ctx, exchange), out_shap...  174 us
    pallas_call x1, Pallas kernels, unpack(): pl.pallas_call(unpack_kernel, grid=(UNPACK_STEPS,), out_shape=[sds((total...  5.49 us

profile of v7, /device:TPU:0, one launch (start us, length us, event | category | flops | bytes accessed | tf_op | source)
XLA Modules:
  0.0 180.2 jit_solution(9195871246343990572)
XLA Ops:
  0.6 173.9 %block_both_ways.1 = (bf16[2,512,768]{2,1,0:T(8,128)(2,1)}, f32[2,512,768]{2,1,0:T(8,128)}, bf16[1728,384]{1,0:T(8,128)(2,1)}, bf16[576,384]{1,0:T(8,128)(2,1)}, f32[16,384]{1,0:T(8,128)}) custom-call(s32[2]{0:T(128)} %bitcast.20, s32[8]{0:T(128)} %border.1, bf16[2,512,768]{2,1,0:T(8,128)(2,1)} %bitcast.16, bf16[2,512,768]{2,1,0:T(8,128)(2,1)} %bitcast.17, ...), custom_call_target="tpu_custom_call" | custom-call | tf_op jit(solution)/shard_map/block_both_ways/pallas_call | solution.py:1097
  174.5 5.5 %unpack_outputs.1 = (bf16[1024,768]{1,0:T(8,128)(2,1)}, f32[1024,768]{1,0:T(8,128)}, f32[768,384]{1,0:T(8,128)}, f32[384,768]{1,0:T(8,128)}, f32[576,384]{1,0:T(...) custom-call(bf16[1024,768]{1,0:T(8,128)(2,1)} %bitcast.18, f32[1024,768]{1,0:T(8,128)} %bitcast.15, ...), custom_call_target="tpu_custom_call" | custom-call | tf_op jit(solution)/shard_map/unpack_outputs/pallas_call | solution.py:1146
